TPU v7x, 32 devices: a whole 2x2x4 slice. The times are simulated.
32 devices in a mesh: wide: 8 (over z, x), narrow: 4 (over y, core).
Axes of the slice: x: 2, y: 2, z: 4, core: 2. Of those that a mesh axis runs over, the one named last changes fastest.
Arguments:
- tokens: bfloat16 [4, 1024, 1536], P(None, 'wide', 'narrow'), may hold values from -6 to 6
- cotangent: bfloat16 [4, 1024, 1536], P(None, 'wide', 'narrow'), may hold values from -6 to 6
- first_prenorm: float32 [1536], P('narrow'), may hold values from 0.1 to 1.9
- first_query: bfloat16 [1536, 1536], P('wide', 'narrow'), may hold values from -0.15625 to 0.15625
- first_keys: bfloat16 [1536, 768], P('wide', 'narrow'), may hold values from -0.15625 to 0.15625
- first_values: bfloat16 [1536, 768], P('wide', 'narrow'), may hold values from -0.15625 to 0.15625
- first_output: bfloat16 [1536, 1536], P('narrow', 'wide'), may hold values from -2.5 to 2.5
- first_midnorm: float32 [1536], P('narrow'), may hold values from 0.1 to 1.9
- first_gate: bfloat16 [1536, 4096], P('wide', 'narrow'), may hold values from -0.15625 to 0.15625
- first_upward: bfloat16 [1536, 4096], P('wide', 'narrow'), may hold values from -0.15625 to 0.15625
- first_down: bfloat16 [4096, 1536], P('narrow', 'wide'), may hold values from -0.09375 to 0.09375
- second_prenorm: float32 [1536], P('narrow'), may hold values from 0.1 to 1.9
- second_query: bfloat16 [1536, 1536], P('wide', 'narrow'), may hold values from -0.15625 to 0.15625
- second_keys: bfloat16 [1536, 768], P('wide', 'narrow'), may hold values from -0.15625 to 0.15625
- second_values: bfloat16 [1536, 768], P('wide', 'narrow'), may hold values from -0.15625 to 0.15625
- second_output: bfloat16 [1536, 1536], P('narrow', 'wide'), may hold values from -2.5 to 2.5
- second_midnorm: float32 [1536], P('narrow'), may hold values from 0.1 to 1.9
- second_gate: bfloat16 [1536, 4096], P('wide', 'narrow'), may hold values from -0.15625 to 0.15625
- second_upward: bfloat16 [1536, 4096], P('wide', 'narrow'), may hold values from -0.15625 to 0.15625
- second_down: bfloat16 [4096, 1536], P('narrow', 'wide'), may hold values from -0.09375 to 0.09375
Outputs:
- block_output: float32 [4, 1024, 1536], P(None, 'wide', 'narrow')
- tokens_gradient: float32 [4, 1024, 1536], P(None, 'wide', 'narrow')
- first_prenorm_gradient: float32 [1536], P('narrow')
- first_query_gradient: float32 [1536, 1536], P('wide', 'narrow')
- first_keys_gradient: float32 [1536, 768], P('wide', 'narrow')
- first_values_gradient: float32 [1536, 768], P('wide', 'narrow')
- first_output_gradient: float32 [1536, 1536], P('narrow', 'wide')
- first_midnorm_gradient: float32 [1536], P('narrow')
- first_gate_gradient: float32 [1536, 4096], P('wide', 'narrow')
- first_upward_gradient: float32 [1536, 4096], P('wide', 'narrow')
- first_down_gradient: float32 [4096, 1536], P('narrow', 'wide')
- second_prenorm_gradient: float32 [1536], P('narrow')
- second_query_gradient: float32 [1536, 1536], P('wide', 'narrow')
- second_keys_gradient: float32 [1536, 768], P('wide', 'narrow')
- second_values_gradient: float32 [1536, 768], P('wide', 'narrow')
- second_output_gradient: float32 [1536, 1536], P('narrow', 'wide')
- second_midnorm_gradient: float32 [1536], P('narrow')
- second_gate_gradient: float32 [1536, 4096], P('wide', 'narrow')
- second_upward_gradient: float32 [1536, 4096], P('wide', 'narrow')
- second_down_gradient: float32 [4096, 1536], P('narrow', 'wide')
All inputs are finite; a program needn't handle non-finite values.
Results may differ from a plain program's by a relative error of at most 0.035.
Values may be sent and summed in bfloat16 or wider, within the bound.
A program may use at most 256 MiB of HBM per device.

v0:
```python
import jax
import jax.numpy as jnp
from jax import lax
from jax.sharding import PartitionSpec as P

HEAD_DIM = 96


EPSILON = 1e-05
THETA = 100000.0
NEGATIVE = -1e30
BFLOAT = jnp.bfloat16
SINGLE = jnp.float32


def rotate(values, cosine_table, sine_table):
    halfway = values.shape[-1] // 2
    leading = values[..., :halfway]
    trailing = values[..., halfway:]
    return jnp.concatenate(
        [
            leading * cosine_table - trailing * sine_table,
            trailing * cosine_table + leading * sine_table,
        ],
        axis=-1,
    )


def unrotate(upstream, cosine_table, sine_table):
    halfway = upstream.shape[-1] // 2
    leading = upstream[..., :halfway]
    trailing = upstream[..., halfway:]
    return jnp.concatenate(
        [
            leading * cosine_table + trailing * sine_table,
            trailing * cosine_table - leading * sine_table,
        ],
        axis=-1,
    )


def contract_rows(left, right):
    return lax.dot_general(left, right, (((0,), (0,)), ((), ())), preferred_element_type=SINGLE)


def contract_last(left, right):
    return lax.dot_general(left, right, (((1,), (1,)), ((), ())), preferred_element_type=SINGLE)


def normalize(residual, gain):
    whole, gain_full = (
        lax.all_gather(residual, "narrow", axis=2, tiled=True),
        lax.all_gather(gain, "narrow", axis=0, tiled=True),
    )
    inverse = lax.rsqrt(jnp.mean(whole * whole, axis=-1, keepdims=True) + EPSILON)
    scaled = whole * inverse
    normed = (scaled * gain_full).astype(BFLOAT)
    return (normed.reshape(-1, whole.shape[2]), scaled, inverse, gain_full)


def fold_rows(normed, portions):
    return tuple((jnp.dot(normed, portion, preferred_element_type=SINGLE) for portion in portions))


def project_out(inputs_low, weight, batches, seq_dev):
    partial_value = jnp.dot(
        inputs_low,
        lax.all_gather(weight, "wide", axis=1, tiled=True),
        preferred_element_type=SINGLE,
    )
    return lax.psum_scatter(
        partial_value.reshape(batches, seq_dev, partial_value.shape[1]).astype(jnp.bfloat16),
        "narrow",
        scatter_dimension=2,
        tiled=True,
    ).astype(jnp.float32)


def gather_branch(residual_back):
    lowered = residual_back.astype(BFLOAT)
    whole = lax.all_gather(lowered, "narrow", axis=2, tiled=True)
    return whole.reshape(-1, whole.shape[2])


def back_out(gathered, weight):
    return contract_last(gathered, lax.all_gather(weight, "wide", axis=1, tiled=True))


def norm_back(partial_value, scaled, inverse, gain_full, residual_back):
    partial_value = partial_value.reshape(scaled.shape)
    gain_term = jnp.sum(partial_value * scaled, axis=(0, 1))
    weighted = partial_value * gain_full
    inner_mean = jnp.mean(weighted * scaled, axis=-1, keepdims=True)
    input_term = inverse * (weighted - scaled * inner_mean)
    rows_back, gain_back = (
        lax.psum_scatter(
            input_term.astype(jnp.bfloat16), "narrow", scatter_dimension=2, tiled=True
        ).astype(jnp.float32),
        lax.psum_scatter(
            gain_term.astype(jnp.bfloat16), "narrow", scatter_dimension=0, tiled=True
        ).astype(jnp.float32),
    )
    return (residual_back + rows_back, gain_back)


def gather_keys(keys_rot, values_low):
    return (
        lax.all_gather(keys_rot, "wide", axis=1, tiled=True),
        lax.all_gather(values_low, "wide", axis=1, tiled=True),
    )


def score_block(grouped, keys_heads, causal):
    scores = jnp.einsum(
        "sgrd,lgd->grsl", grouped, keys_heads, preferred_element_type=SINGLE
    ) * HEAD_DIM ** (-0.5)
    return jnp.where(causal, scores, NEGATIVE)


def attend(queries, keys_every, values_every, causal, kv_local):

    def per_batch(operands):
        query_one, keys_one, values_one = operands
        seq_dev = query_one.shape[0]
        length = keys_one.shape[0]
        grouped = query_one.reshape(seq_dev, kv_local, -1, HEAD_DIM)
        keys_heads = keys_one.reshape(length, kv_local, HEAD_DIM)
        values_heads = values_one.reshape(length, kv_local, HEAD_DIM)
        scores = score_block(grouped, keys_heads, causal)
        highest = jnp.max(scores, axis=-1, keepdims=True)
        logsum = highest + jnp.log(jnp.sum(jnp.exp(scores - highest), axis=-1, keepdims=True))
        weights_low = jnp.exp(scores - logsum).astype(BFLOAT)
        mixed = jnp.einsum(
            "grsl,lgd->sgrd", weights_low, values_heads, preferred_element_type=SINGLE
        )
        return (mixed.reshape(seq_dev, -1), logsum[..., 0])

    return lax.map(per_batch, (queries, keys_every, values_every))


def attend_back(queries, keys_every, values_every, logsums, mixed_back, causal, kv_local):

    def per_batch(operands):
        query_one, keys_one, values_one, logsum_one, back_one = operands
        seq_dev = query_one.shape[0]
        length = keys_one.shape[0]
        grouped = query_one.reshape(seq_dev, kv_local, -1, HEAD_DIM)
        keys_heads = keys_one.reshape(length, kv_local, HEAD_DIM)
        values_heads = values_one.reshape(length, kv_local, HEAD_DIM)
        scores = score_block(grouped, keys_heads, causal)
        probs = jnp.exp(scores - logsum_one[..., None])
        back_heads = back_one.reshape(seq_dev, kv_local, -1, HEAD_DIM)
        prob_back = jnp.einsum(
            "sgrd,lgd->grsl", back_heads, values_heads, preferred_element_type=SINGLE
        )
        inner_sum = jnp.sum(probs * prob_back, axis=-1, keepdims=True)
        score_back = (probs * (prob_back - inner_sum)).astype(BFLOAT)
        query_part = jnp.einsum(
            "grsl,lgd->sgrd", score_back, keys_heads, preferred_element_type=SINGLE
        ) * HEAD_DIM ** (-0.5)
        keys_part = jnp.einsum(
            "grsl,sgrd->lgd", score_back, grouped, preferred_element_type=SINGLE
        ) * HEAD_DIM ** (-0.5)
        values_part = jnp.einsum(
            "grsl,sgrd->lgd", probs.astype(BFLOAT), back_heads, preferred_element_type=SINGLE
        )
        return (
            query_part.reshape(seq_dev, -1),
            keys_part.reshape(length, -1),
            values_part.reshape(length, -1),
        )

    return lax.map(per_batch, (queries, keys_every, values_every, logsums, mixed_back))


def layer_forward(residual, weights, cosine_table, sine_table, causal):
    (
        prenorm,
        query_weight,
        keys_weight,
        values_weight,
        output_weight,
        midnorm,
        gate_weight,
        upward_weight,
        down_weight,
    ) = weights
    batches, seq_dev, narrow_width = residual.shape
    head_local = query_weight.shape[1] // HEAD_DIM
    kv_local = keys_weight.shape[1] // HEAD_DIM
    normed_mix, scaled_mix, inverse_mix, gain_mix = normalize(residual, prenorm)
    row_count = normed_mix.shape[0]
    query_raw, keys_raw, values_raw = fold_rows(
        normed_mix,
        (
            lax.all_gather(query_weight, "wide", axis=0, tiled=True),
            lax.all_gather(keys_weight, "wide", axis=0, tiled=True),
            lax.all_gather(values_weight, "wide", axis=0, tiled=True),
        ),
    )
    queries = (
        rotate(query_raw.reshape(batches, seq_dev, head_local, HEAD_DIM), cosine_table, sine_table)
        .astype(BFLOAT)
        .reshape(batches, seq_dev, -1)
    )
    keys_rot = (
        rotate(keys_raw.reshape(batches, seq_dev, kv_local, HEAD_DIM), cosine_table, sine_table)
        .astype(BFLOAT)
        .reshape(batches, seq_dev, -1)
    )
    values_low = values_raw.astype(BFLOAT).reshape(batches, seq_dev, -1)
    keys_every, values_every = gather_keys(keys_rot, values_low)
    mixed, logsums = attend(queries, keys_every, values_every, causal, kv_local)
    mixed_low = mixed.astype(BFLOAT).reshape(row_count, -1)
    middle = residual + project_out(mixed_low, output_weight, batches, seq_dev)
    normed_feed, scaled_feed, inverse_feed, gain_feed = normalize(middle, midnorm)
    gate_raw, upward_raw = fold_rows(
        normed_feed,
        (
            lax.all_gather(gate_weight, "wide", axis=0, tiled=True),
            lax.all_gather(upward_weight, "wide", axis=0, tiled=True),
        ),
    )
    activated = (jax.nn.silu(gate_raw) * upward_raw).astype(BFLOAT)
    result = middle + project_out(activated, down_weight, batches, seq_dev)
    saved = (
        normed_mix,
        scaled_mix,
        inverse_mix,
        gain_mix,
        queries,
        keys_rot,
        values_low,
        keys_every,
        values_every,
        logsums,
        mixed_low,
        normed_feed,
        scaled_feed,
        inverse_feed,
        gain_feed,
        gate_raw,
        upward_raw,
        activated,
    )
    return (result, saved)


def layer_backward(residual_back, weights, saved, cosine_table, sine_table, causal):
    (
        prenorm,
        query_weight,
        keys_weight,
        values_weight,
        output_weight,
        midnorm,
        gate_weight,
        upward_weight,
        down_weight,
    ) = weights
    (
        normed_mix,
        scaled_mix,
        inverse_mix,
        gain_mix,
        queries,
        keys_rot,
        values_low,
        saved_keys,
        saved_values,
        logsums,
        mixed_low,
        normed_feed,
        scaled_feed,
        inverse_feed,
        gain_feed,
        gate_raw,
        upward_raw,
        activated,
    ) = saved
    batches, seq_dev, narrow_width = residual_back.shape
    head_local = query_weight.shape[1] // HEAD_DIM
    kv_local = keys_weight.shape[1] // HEAD_DIM
    row_count = normed_mix.shape[0]
    feed_back = gather_branch(residual_back)
    activated_back = back_out(feed_back, down_weight)
    down_gradient = contract_rows(activated, feed_back)
    sigmoid = jax.nn.sigmoid(gate_raw)
    gate_back = (activated_back * upward_raw * sigmoid * (1.0 + gate_raw * (1.0 - sigmoid))).astype(
        BFLOAT
    )
    upward_back = (activated_back * gate_raw * sigmoid).astype(BFLOAT)
    gate_gradient = contract_rows(normed_feed, gate_back)
    upward_gradient = contract_rows(normed_feed, upward_back)
    portions = lax.all_gather((gate_weight, upward_weight), "wide", axis=0, tiled=True)
    feed_partial = contract_last(gate_back, portions[0]) + contract_last(upward_back, portions[1])
    middle_back, midnorm_gradient = norm_back(
        feed_partial, scaled_feed, inverse_feed, gain_feed, residual_back
    )
    mix_back = gather_branch(middle_back)
    mixed_back = back_out(mix_back, output_weight).astype(BFLOAT).reshape(batches, seq_dev, -1)
    output_gradient = contract_rows(mixed_low, mix_back)
    keys_every, values_every = gather_keys(keys_rot, values_low)
    query_part, keys_part, values_part = attend_back(
        queries, keys_every, values_every, logsums, mixed_back, causal, kv_local
    )
    keys_summed, values_summed = (
        lax.psum_scatter(
            keys_part.astype(jnp.bfloat16), "wide", scatter_dimension=1, tiled=True
        ).astype(jnp.float32),
        lax.psum_scatter(
            values_part.astype(jnp.bfloat16), "wide", scatter_dimension=1, tiled=True
        ).astype(jnp.float32),
    )
    query_back = (
        unrotate(
            query_part.reshape(batches, seq_dev, head_local, HEAD_DIM), cosine_table, sine_table
        )
        .astype(BFLOAT)
        .reshape(row_count, -1)
    )
    keys_back = (
        unrotate(
            keys_summed.reshape(batches, seq_dev, kv_local, HEAD_DIM), cosine_table, sine_table
        )
        .astype(BFLOAT)
        .reshape(row_count, -1)
    )
    values_back = values_summed.astype(BFLOAT).reshape(row_count, -1)
    query_gradient = contract_rows(normed_mix, query_back)
    keys_gradient = contract_rows(normed_mix, keys_back)
    values_gradient = contract_rows(normed_mix, values_back)
    portions = lax.all_gather(
        (query_weight, keys_weight, values_weight), "wide", axis=0, tiled=True
    )
    mix_partial = (
        contract_last(query_back, portions[0])
        + contract_last(keys_back, portions[1])
        + contract_last(values_back, portions[2])
    )
    input_back, prenorm_gradient = norm_back(
        mix_partial, scaled_mix, inverse_mix, gain_mix, middle_back
    )
    return (
        input_back,
        (
            prenorm_gradient,
            query_gradient,
            keys_gradient,
            values_gradient,
            output_gradient,
            midnorm_gradient,
            gate_gradient,
            upward_gradient,
            down_gradient,
        ),
    )


def per_device(
    tokens,
    cotangent,
    first_prenorm,
    first_query,
    first_keys,
    first_values,
    first_output,
    first_midnorm,
    first_gate,
    first_upward,
    first_down,
    second_prenorm,
    second_query,
    second_keys,
    second_values,
    second_output,
    second_midnorm,
    second_gate,
    second_upward,
    second_down,
):
    seq_dev = tokens.shape[1]
    wide_count = lax.axis_size("wide")
    halfway = HEAD_DIM // 2
    exponent = jnp.arange(halfway, dtype=SINGLE) * 2.0 / HEAD_DIM
    inverse = jnp.power(jnp.float32(THETA), -exponent)
    query_pos = lax.axis_index("wide") * seq_dev + jnp.arange(seq_dev, dtype=jnp.int32)
    angle = query_pos.astype(SINGLE)[:, None] * inverse[None, :]
    cosine_table = jnp.cos(angle)[:, None, :]
    sine_table = jnp.sin(angle)[:, None, :]
    key_pos = jnp.arange(seq_dev * wide_count, dtype=jnp.int32)
    causal = key_pos[None, :] <= query_pos[:, None]
    first_weights = (
        first_prenorm,
        first_query,
        first_keys,
        first_values,
        first_output,
        first_midnorm,
        first_gate,
        first_upward,
        first_down,
    )
    second_weights = (
        second_prenorm,
        second_query,
        second_keys,
        second_values,
        second_output,
        second_midnorm,
        second_gate,
        second_upward,
        second_down,
    )
    middle_output, first_saved = layer_forward(
        tokens.astype(SINGLE), first_weights, cosine_table, sine_table, causal
    )
    block_output, second_saved = layer_forward(
        middle_output, second_weights, cosine_table, sine_table, causal
    )
    upper_back, second_grads = layer_backward(
        cotangent.astype(SINGLE), second_weights, second_saved, cosine_table, sine_table, causal
    )
    lower_back, first_grads = layer_backward(
        upper_back, first_weights, first_saved, cosine_table, sine_table, causal
    )
    summed = (
        lax.psum_scatter(
            first_grads[1].astype(jnp.bfloat16), "wide", scatter_dimension=0, tiled=True
        ).astype(jnp.float32),
        lax.psum_scatter(
            first_grads[2].astype(jnp.bfloat16), "wide", scatter_dimension=0, tiled=True
        ).astype(jnp.float32),
        lax.psum_scatter(
            first_grads[3].astype(jnp.bfloat16), "wide", scatter_dimension=0, tiled=True
        ).astype(jnp.float32),
        lax.psum_scatter(
            first_grads[4].astype(jnp.bfloat16), "wide", scatter_dimension=1, tiled=True
        ).astype(jnp.float32),
        lax.psum_scatter(
            first_grads[6].astype(jnp.bfloat16), "wide", scatter_dimension=0, tiled=True
        ).astype(jnp.float32),
        lax.psum_scatter(
            first_grads[7].astype(jnp.bfloat16), "wide", scatter_dimension=0, tiled=True
        ).astype(jnp.float32),
        lax.psum_scatter(
            first_grads[8].astype(jnp.bfloat16), "wide", scatter_dimension=1, tiled=True
        ).astype(jnp.float32),
        lax.psum_scatter(
            second_grads[1].astype(jnp.bfloat16), "wide", scatter_dimension=0, tiled=True
        ).astype(jnp.float32),
        lax.psum_scatter(
            second_grads[2].astype(jnp.bfloat16), "wide", scatter_dimension=0, tiled=True
        ).astype(jnp.float32),
        lax.psum_scatter(
            second_grads[3].astype(jnp.bfloat16), "wide", scatter_dimension=0, tiled=True
        ).astype(jnp.float32),
        lax.psum_scatter(
            second_grads[4].astype(jnp.bfloat16), "wide", scatter_dimension=1, tiled=True
        ).astype(jnp.float32),
        lax.psum_scatter(
            second_grads[6].astype(jnp.bfloat16), "wide", scatter_dimension=0, tiled=True
        ).astype(jnp.float32),
        lax.psum_scatter(
            second_grads[7].astype(jnp.bfloat16), "wide", scatter_dimension=0, tiled=True
        ).astype(jnp.float32),
        lax.psum_scatter(
            second_grads[8].astype(jnp.bfloat16), "wide", scatter_dimension=1, tiled=True
        ).astype(jnp.float32),
    )
    gains = lax.psum((first_grads[0], first_grads[5], second_grads[0], second_grads[5]), "wide")
    return (
        block_output,
        lower_back,
        gains[0],
        summed[0],
        summed[1],
        summed[2],
        summed[3],
        gains[1],
        summed[4],
        summed[5],
        summed[6],
        gains[2],
        summed[7],
        summed[8],
        summed[9],
        summed[10],
        gains[3],
        summed[11],
        summed[12],
        summed[13],
    )


def solution(mesh):
    placed = (
        P(None, "wide", "narrow"),
        P(None, "wide", "narrow"),
        P("narrow"),
        P("wide", "narrow"),
        P("wide", "narrow"),
        P("wide", "narrow"),
        P("narrow", "wide"),
        P("narrow"),
        P("wide", "narrow"),
        P("wide", "narrow"),
        P("narrow", "wide"),
        P("narrow"),
        P("wide", "narrow"),
        P("wide", "narrow"),
        P("wide", "narrow"),
        P("narrow", "wide"),
        P("narrow"),
        P("wide", "narrow"),
        P("wide", "narrow"),
        P("narrow", "wide"),
    )
    return jax.shard_map(
        per_device,
        mesh=mesh,
        in_specs=placed,
        out_specs=(
            P(None, "wide", "narrow"),
            P(None, "wide", "narrow"),
            P("narrow"),
            P("wide", "narrow"),
            P("wide", "narrow"),
            P("wide", "narrow"),
            P("narrow", "wide"),
            P("narrow"),
            P("wide", "narrow"),
            P("wide", "narrow"),
            P("narrow", "wide"),
            P("narrow"),
            P("wide", "narrow"),
            P("wide", "narrow"),
            P("wide", "narrow"),
            P("narrow", "wide"),
            P("narrow"),
            P("wide", "narrow"),
            P("wide", "narrow"),
            P("narrow", "wide"),
        ),
        check_vma=False,
    )
```

profile of v0, /device:TPU:0, one launch (start us, length us, event | category | flops | bytes accessed | tf_op | source)
XLA Modules:
  0.0 2649.1 jit_solution(961640043338548249)
XLA Ops:
  138.1 46.0 %all-gather.29.cloned.1.call-done = bf16[4,1024,192]{1,2,0:T(8,128)(2,1)} async-done(((bf16[4,128,192]{1,2,0:T(8,128)(2,1)}), bf16[4,1024,192]{1,2,0:T(8,128)(2,1)}) %all-gather.29.cloned.1.call-update) | async-done | bytes 1572880 | tf_op jit(solution)/shard_map/all_gather | solution.py:109
  292.7 58.6 %all-gather.39.cloned.1.call-done = bf16[1536,1024]{1,0:T(8,128)(2,1)} async-done(((bf16[192,1024]{1,0:T(8,128)(2,1)}), bf16[1536,1024]{1,0:T(8,128)(2,1)}) %all-gather.39.cloned.1.call-update) | async-done | bytes 3145744 | tf_op jit(solution)/shard_map/all_gather | solution.py:220
  356.7 56.1 %all-gather.41.cloned.1.call-done = bf16[1536,1024]{1,0:T(8,128)(2,1)} async-done(((bf16[192,1024]{1,0:T(8,128)(2,1)}), bf16[1536,1024]{1,0:T(8,128)(2,1)}) %all-gather.41.cloned.1.call-update) | async-done | bytes 3145744 | tf_op jit(solution)/shard_map/all_gather | solution.py:221
  419.3 54.9 %all-gather.43.cloned.1.call-done = bf16[1024,1536]{0,1:T(8,128)(2,1)} async-done(((bf16[1024,192]{0,1:T(8,128)(2,1)}), bf16[1024,1536]{0,1:T(8,128)(2,1)}) %all-gather.43.cloned.1.call-update) | async-done | bytes 3145744 | tf_op jit(solution)/shard_map/all_gather | solution.py:68
  644.0 46.0 %all-gather.47.cloned.1.call-done = bf16[4,1024,192]{1,2,0:T(8,128)(2,1)} async-done(((bf16[4,128,192]{1,2,0:T(8,128)(2,1)}), bf16[4,1024,192]{1,2,0:T(8,128)(2,1)}) %all-gather.47.cloned.1.call-update) | async-done | bytes 1572880 | tf_op jit(solution)/shard_map/all_gather | solution.py:109
  806.0 58.6 %all-gather.57.cloned.1.call-done = bf16[1536,1024]{1,0:T(8,128)(2,1)} async-done(((bf16[192,1024]{1,0:T(8,128)(2,1)}), bf16[1536,1024]{1,0:T(8,128)(2,1)}) %all-gather.57.cloned.1.call-update) | async-done | bytes 3145744 | tf_op jit(solution)/shard_map/all_gather | solution.py:220
  870.1 55.9 %all-gather.59.cloned.1.call-done = bf16[1536,1024]{1,0:T(8,128)(2,1)} async-done(((bf16[192,1024]{1,0:T(8,128)(2,1)}), bf16[1536,1024]{1,0:T(8,128)(2,1)}) %all-gather.59.cloned.1.call-update) | async-done | bytes 3145744 | tf_op jit(solution)/shard_map/all_gather | solution.py:221
  945.9 62.9 %all-gather.61.cloned.1.call-done = bf16[1024,1536]{0,1:T(8,128)(2,1)} async-done(((bf16[1024,192]{0,1:T(8,128)(2,1)}), bf16[1024,1536]{0,1:T(8,128)(2,1)}) %all-gather.61.cloned.1.call-update) | async-done | bytes 3145744 | tf_op jit(solution)/shard_map/all_gather | solution.py:68
  1150.6 50.8 %reduce-scatter.89.cloned.1.call-done = bf16[128,768]{1,0:T(8,128)(2,1)} async-done(((bf16[1024,768]{1,0:T(8,128)(2,1)}), bf16[128,768]{1,0:T(8,128)(2,1)}) %reduce-scatter.89.cloned.1.call-update) | async-done | bytes 196624
  1205.2 63.5 %reduce-scatter.91.cloned.1.call-done = bf16[128,768]{1,0:T(8,128)(2,1)} async-done(((bf16[1024,768]{1,0:T(8,128)(2,1)}), bf16[128,768]{1,0:T(8,128)(2,1)}) %reduce-scatter.91.cloned.1.call-update) | async-done | bytes 196624
  1530.2 56.9 %reduce-scatter.99.cloned.1.call-done = bf16[128,768]{1,0:T(8,128)(2,1)} async-done(((bf16[1024,768]{1,0:T(8,128)(2,1)}), bf16[128,768]{1,0:T(8,128)(2,1)}) %reduce-scatter.99.cloned.1.call-update) | async-done | bytes 196624
  1618.9 76.1 %reduce-scatter.73.cloned.1.call-done = bf16[192,1024]{1,0:T(8,128)(2,1)} async-done(((bf16[1536,1024]{1,0:T(8,128)(2,1)}), bf16[192,1024]{1,0:T(8,128)(2,1)}) %reduce-scatter.73.cloned.1.call-update) | async-done | bytes 393232 | tf_op jit(solution)/shard_map/reduce_scatter | solution.py:461
  1697.0 75.5 %reduce-scatter.75.cloned.1.call-done = bf16[192,1024]{1,0:T(8,128)(2,1)} async-done(((bf16[1536,1024]{1,0:T(8,128)(2,1)}), bf16[192,1024]{1,0:T(8,128)(2,1)}) %reduce-scatter.75.cloned.1.call-update) | async-done | bytes 393232 | tf_op jit(solution)/shard_map/reduce_scatter | solution.py:464
  1774.4 75.4 %reduce-scatter.77.cloned.1.call-done = bf16[1024,192]{0,1:T(8,128)(2,1)} async-done(((bf16[1024,1536]{0,1:T(8,128)(2,1)}), bf16[1024,192]{0,1:T(8,128)(2,1)}) %reduce-scatter.77.cloned.1.call-update) | async-done | bytes 393232 | tf_op jit(solution)/shard_map/reduce_scatter | solution.py:467
  1851.8 64.9 %reduce-scatter.65.cloned.1.call-done = bf16[192,384]{1,0:T(8,128)(2,1)} async-done(((bf16[1536,384]{1,0:T(8,128)(2,1)}), bf16[192,384]{1,0:T(8,128)(2,1)}) %reduce-scatter.65.cloned.1.call-update) | async-done | bytes 147472 | tf_op jit(solution)/shard_map/reduce_scatter | solution.py:449
  1918.3 65.2 %reduce-scatter.71.cloned.1.call-done = bf16[384,192]{0,1:T(8,128)(2,1)} async-done(((bf16[384,1536]{0,1:T(8,128)(2,1)}), bf16[384,192]{0,1:T(8,128)(2,1)}) %reduce-scatter.71.cloned.1.call-update) | async-done | bytes 147472 | tf_op jit(solution)/shard_map/reduce_scatter | solution.py:458
  1985.2 63.9 %reduce-scatter.67.cloned.1.call-done = bf16[192,192]{1,0:T(8,128)(2,1)} async-done(((bf16[1536,192]{1,0:T(8,128)(2,1)}), bf16[192,192]{1,0:T(8,128)(2,1)}) %reduce-scatter.67.cloned.1.call-update) | async-done | bytes 73744 | tf_op jit(solution)/shard_map/reduce_scatter | solution.py:452
  2050.7 63.3 %reduce-scatter.69.cloned.1.call-done = bf16[192,192]{1,0:T(8,128)(2,1)} async-done(((bf16[1536,192]{1,0:T(8,128)(2,1)}), bf16[192,192]{1,0:T(8,128)(2,1)}) %reduce-scatter.69.cloned.1.call-update) | async-done | bytes 73744 | tf_op jit(solution)/shard_map/reduce_scatter | solution.py:455
  2115.5 75.6 %reduce-scatter.63.cloned.1.call-done = bf16[1024,192]{0,1:T(8,128)(2,1)} async-done(((bf16[1024,1536]{0,1:T(8,128)(2,1)}), bf16[1024,192]{0,1:T(8,128)(2,1)}) %reduce-scatter.63.cloned.1.call-update) | async-done | bytes 393232 | tf_op jit(solution)/shard_map/reduce_scatter | solution.py:446
  2193.1 75.6 %reduce-scatter.59.cloned.1.call-done = bf16[192,1024]{1,0:T(8,128)(2,1)} async-done(((bf16[1536,1024]{1,0:T(8,128)(2,1)}), bf16[192,1024]{1,0:T(8,128)(2,1)}) %reduce-scatter.59.cloned.1.call-update) | async-done | bytes 393232 | tf_op jit(solution)/shard_map/reduce_scatter | solution.py:440
  2270.7 75.4 %reduce-scatter.61.cloned.1.call-done = bf16[192,1024]{1,0:T(8,128)(2,1)} async-done(((bf16[1536,1024]{1,0:T(8,128)(2,1)}), bf16[192,1024]{1,0:T(8,128)(2,1)}) %reduce-scatter.61.cloned.1.call-update) | async-done | bytes 393232 | tf_op jit(solution)/shard_map/reduce_scatter | solution.py:443
  2348.0 65.1 %reduce-scatter.51.cloned.1.call-done = bf16[192,384]{1,0:T(8,128)(2,1)} async-done(((bf16[1536,384]{1,0:T(8,128)(2,1)}), bf16[192,384]{1,0:T(8,128)(2,1)}) %reduce-scatter.51.cloned.1.call-update) | async-done | bytes 147472 | tf_op jit(solution)/shard_map/reduce_scatter | solution.py:428
  2414.7 65.1 %reduce-scatter.57.cloned.1.call-done = bf16[384,192]{0,1:T(8,128)(2,1)} async-done(((bf16[384,1536]{0,1:T(8,128)(2,1)}), bf16[384,192]{0,1:T(8,128)(2,1)}) %reduce-scatter.57.cloned.1.call-update) | async-done | bytes 147472 | tf_op jit(solution)/shard_map/reduce_scatter | solution.py:437
  2546.9 63.1 %reduce-scatter.55.cloned.1.call-done = bf16[192,192]{1,0:T(8,128)(2,1)} async-done(((bf16[1536,192]{1,0:T(8,128)(2,1)}), bf16[192,192]{1,0:T(8,128)(2,1)}) %reduce-scatter.55.cloned.1.call-update) | async-done | bytes 73744 | tf_op jit(solution)/shard_map/reduce_scatter | solution.py:434
  (681 shorter events, 1213.4 us)
Async XLA Ops:
  90.9 166.4 %reduce-scatter.79.cloned.1.call-start = ((), (), s32[]{:S(2)}) async-start(), calls=%async_computation.62 | async-start | bytes 1966080
  261.2 213.0 %all-gather.43.cloned.1.call-start = ((), (), s32[]{:S(2)}) async-start(), calls=%async_computation.34 | async-start | bytes 3538944 | tf_op jit(solution)/shard_map/all_gather | solution.py:68
  261.8 251.3 %reduce-scatter.81.cloned.1.call-start = ((), (), s32[]{:S(2)}) async-start(), calls=%async_computation.63 | async-start | bytes 1966080
  605.7 163.0 %reduce-scatter.83.cloned.1.call-start = ((), (), s32[]{:S(2)}) async-start(), calls=%async_computation.64 | async-start | bytes 1966080
  774.4 171.6 %all-gather.63.cloned.1.call-start = ((), (), s32[]{:S(2)}) async-start(), calls=%async_computation.44 | async-start | bytes 1966080 | tf_op jit(solution)/shard_map/all_gather | solution.py:81
  775.1 233.7 %all-gather.61.cloned.1.call-start = ((), (), s32[]{:S(2)}) async-start(), calls=%async_computation.43 | async-start | bytes 3538944 | tf_op jit(solution)/shard_map/all_gather | solution.py:68
  775.9 281.6 %reduce-scatter.87.cloned.1.call-start = ((), (), s32[]{:S(2)}) async-start(), calls=%async_computation.66 | async-start | bytes 1966080
  1145.3 167.5 %reduce-scatter.93.cloned.1.call-start = ((), (), s32[]{:S(2)}) async-start(), calls=%async_computation.69 | async-start | bytes 1966080
  1460.3 156.2 %reduce-scatter.85.cloned.1.call-start = ((), (), s32[]{:S(2)}) async-start(), calls=%async_computation.65 | async-start | bytes 1966080
  1470.0 225.1 %reduce-scatter.73.cloned.1.call-start = ((), (), s32[]{:S(2)}) async-start(), calls=%async_computation.59 | async-start | bytes 3538944 | tf_op jit(solution)/shard_map/reduce_scatter | solution.py:461
  1475.2 297.2 %reduce-scatter.75.cloned.1.call-start = ((), (), s32[]{:S(2)}) async-start(), calls=%async_computation.60 | async-start | bytes 3538944 | tf_op jit(solution)/shard_map/reduce_scatter | solution.py:464
  1481.5 368.3 %reduce-scatter.77.cloned.1.call-start = ((), (), s32[]{:S(2)}) async-start(), calls=%async_computation.61 | async-start | bytes 3538944 | tf_op jit(solution)/shard_map/reduce_scatter | solution.py:467
  1487.7 429.0 %reduce-scatter.65.cloned.1.call-start = ((), (), s32[]{:S(2)}) async-start(), calls=%async_computation.55 | async-start | bytes 1327104 | tf_op jit(solution)/shard_map/reduce_scatter | solution.py:449
  1492.2 491.4 %reduce-scatter.71.cloned.1.call-start = ((), (), s32[]{:S(2)}) async-start(), calls=%async_computation.58 | async-start | bytes 1327104 | tf_op jit(solution)/shard_map/reduce_scatter | solution.py:458
  1495.7 553.4 %reduce-scatter.67.cloned.1.call-start = ((), (), s32[]{:S(2)}) async-start(), calls=%async_computation.56 | async-start | bytes 884736 | tf_op jit(solution)/shard_map/reduce_scatter | solution.py:452
  1498.2 615.7 %reduce-scatter.69.cloned.1.call-start = ((), (), s32[]{:S(2)}) async-start(), calls=%async_computation.57 | async-start | bytes 884736 | tf_op jit(solution)/shard_map/reduce_scatter | solution.py:455
  1499.8 691.3 %reduce-scatter.63.cloned.1.call-start = ((), (), s32[]{:S(2)}) async-start(), calls=%async_computation.54 | async-start | bytes 3538944 | tf_op jit(solution)/shard_map/reduce_scatter | solution.py:446
  1505.1 763.6 %reduce-scatter.59.cloned.1.call-start = ((), (), s32[]{:S(2)}) async-start(), calls=%async_computation.52 | async-start | bytes 3538944 | tf_op jit(solution)/shard_map/reduce_scatter | solution.py:440
  1511.3 834.7 %reduce-scatter.61.cloned.1.call-start = ((), (), s32[]{:S(2)}) async-start(), calls=%async_computation.53 | async-start | bytes 3538944 | tf_op jit(solution)/shard_map/reduce_scatter | solution.py:443
  1516.1 896.9 %reduce-scatter.51.cloned.1.call-start = ((), (), s32[]{:S(2)}) async-start(), calls=%async_computation.48 | async-start | bytes 1327104 | tf_op jit(solution)/shard_map/reduce_scatter | solution.py:428
  1519.6 960.1 %reduce-scatter.57.cloned.1.call-start = ((), (), s32[]{:S(2)}) async-start(), calls=%async_computation.51 | async-start | bytes 1327104 | tf_op jit(solution)/shard_map/reduce_scatter | solution.py:437
  1523.4 1021.9 %reduce-scatter.53.cloned.1.call-start = ((), (), s32[]{:S(2)}) async-start(), calls=%async_computation.49 | async-start | bytes 884736 | tf_op jit(solution)/shard_map/reduce_scatter | solution.py:431
  1527.4 1082.6 %reduce-scatter.55.cloned.1.call-start = ((), (), s32[]{:S(2)}) async-start(), calls=%async_computation.50 | async-start | bytes 884736 | tf_op jit(solution)/shard_map/reduce_scatter | solution.py:434
  1594.0 1045.7 %reduce-scatter.101.cloned.1.call-start = ((), (), s32[]{:S(2)}) async-start(), calls=%async_computation.73 | async-start | bytes 1966080
  (108 other events, 5763.8 us)
Sparse Core Ops, SparseCore 0:
  290.8 60.4 all-gather.38
  353.7 59.0 all-gather.40
  415.1 59.0 all-gather.42
  804.1 60.4 all-gather.56
  866.9 59.0 all-gather.58
  948.4 60.4 all-gather.60
  1136.4 64.8 reduce-scatter.88
  1205.0 63.7 reduce-scatter.90
  1454.6 64.8 reduce-scatter.96
  1523.3 63.7 reduce-scatter.98
  1620.6 74.4 reduce-scatter.72
  1699.0 73.3 reduce-scatter.74
  1776.3 73.4 reduce-scatter.76
  1853.4 63.2 reduce-scatter.64
  1920.5 63.0 reduce-scatter.70
  1987.6 61.4 reduce-scatter.66
  2052.4 61.5 reduce-scatter.68
  2117.9 73.1 reduce-scatter.62
  2195.2 73.5 reduce-scatter.58
  2272.6 73.4 reduce-scatter.60
  2349.8 63.2 reduce-scatter.50
  2416.7 63.0 reduce-scatter.56
  2483.8 61.4 reduce-scatter.52
  2548.5 61.4 reduce-scatter.54
  (24 shorter events, 758.5 us)
where the time goes:
time: 2660 us; the launch traced here: 2650 us
  waiting for transfers between devices  2000 us (75%)
  local copies, waits for them, and re-layouts  196 us (7%)
  blocking collectives  187 us (7%)
  matrix products  164 us (6%)
  other arithmetic  78.1 us (3%)
    unnamed x60, waiting for transfers between devices  381 us
    all_gather x4, waiting for transfers between devices, project_out(): lax.all_gather(weight, 'wide', axis=1, tiled=True)  174 us
    all_gather x2, waiting for transfers between devices, layer_forward(): lax.all_gather(gate_weight, 'wide', axis=0, tiled=True)  117 us
    all_gather x2, waiting for transfers between devices, layer_forward(): lax.all_gather(upward_weight, 'wide', axis=0, tiled=True)  112 us
    unnamed x222, local copies, waits for them, and re-layouts  112 us
    all_gather x2, waiting for transfers between devices, gather_keys(): lax.all_gather(values_low, 'wide', axis=1, tiled=True)  92 us
    reduce_scatter x1, waiting for transfers between devices, per_device(): lax.psum_scatter(second_grads[6].astype(jnp.bfloat16), 'wide', scatter_di...  76.1 us
    reduce_scatter x1, waiting for transfers between devices, per_device(): lax.psum_scatter(first_grads[8].astype(jnp.bfloat16), 'wide', scatter_dim...  75.6 us
  transfers between devices with their start and end apart: 48, of which 43 were waited for; matrix products, arithmetic and copies ran while one was open for 8% of the time, Pallas kernels for 0%

commit v1 on v0

v1 whole, which is shorter than its diff:
```python
import jax
import jax.numpy as jnp
from jax import lax
from jax.sharding import PartitionSpec as P

HEAD_DIM = 96
EPSILON = 1e-05
THETA = 100000.0
NEGATIVE = -1e30
BF = jnp.bfloat16
F32 = jnp.float32
OUTER = 4
SCALE = HEAD_DIM**-0.5


def dot(left, right):
    return jnp.dot(left, right, preferred_element_type=F32)


def dot_last(left, right):
    return lax.dot_general(left, right, (((1,), (1,)), ((), ())), preferred_element_type=F32)


def dot_first(left, right):
    return lax.dot_general(left, right, (((0,), (0,)), ((), ())), preferred_element_type=F32)


def exchange(x, distance):
    count = lax.axis_size("wide")
    return lax.ppermute(x, "wide", [(w, w ^ distance) for w in range(count)])


def bits_below(count):
    found, bit = [], 1
    while bit < count:
        found.append(bit)
        bit *= 2
    return found


def gather_blocks(block):
    count = lax.axis_size("wide")
    inner = count // OUTER
    blocks = {0: block}
    for outer in range(1, OUTER):
        blocks[outer * inner] = exchange(block, outer * inner)
    for bit in bits_below(inner):
        for j in sorted(blocks):
            blocks[j + bit] = exchange(blocks[j], bit)
    return [blocks[j] for j in range(count)]


def natural(blocks):
    stacked = jnp.stack(blocks)
    count = stacked.shape[0]
    me = lax.axis_index("wide")
    picked = [lax.dynamic_index_in_dim(stacked, k ^ me, 0, keepdims=False) for k in range(count)]
    return jnp.concatenate(picked, axis=0)


def reduce_blocks(gradient):
    count = lax.axis_size("wide")
    inner = count // OUTER
    me = lax.axis_index("wide")
    split = gradient.reshape(count, gradient.shape[0] // count, gradient.shape[1])
    blocks = {j: lax.dynamic_index_in_dim(split, me ^ j, 0, keepdims=False) for j in range(count)}
    for bit in reversed(bits_below(inner)):
        moved = {}
        for j in sorted(blocks):
            if j % (2 * bit) < bit:
                got = exchange(blocks[j + bit], bit)
                moved[j] = (blocks[j].astype(F32) + got.astype(F32)).astype(BF)
        blocks = moved
    total = blocks[0].astype(F32)
    for outer in range(1, OUTER):
        total = total + exchange(blocks[outer * inner], outer * inner).astype(F32)
    return total


def spread_tokens(x):
    batches = x.shape[0]
    count = lax.axis_size("wide")
    group = count // batches
    me = lax.axis_index("wide")
    rank = me % batches
    own = me // group
    parts = []
    for j in range(batches):
        piece = lax.dynamic_index_in_dim(x, (rank + j) % batches, 0, keepdims=False)
        pairs = [
            (w, ((w % batches + j) % batches) * group + w // batches) for w in range(count)
        ]
        parts.append(lax.ppermute(piece, "wide", pairs))
    stacked = jnp.stack(parts)
    picked = [
        lax.dynamic_index_in_dim(stacked, (own - r) % batches, 0, keepdims=False)
        for r in range(batches)
    ]
    return jnp.stack(picked)


def collect_tokens(x):
    batches = x.shape[0]
    count = lax.axis_size("wide")
    group = count // batches
    me = lax.axis_index("wide")
    rank = me % batches
    own = me // group
    parts = []
    for j in range(batches):
        piece = lax.dynamic_index_in_dim(x, (own - j) % batches, 0, keepdims=False)
        pairs = [
            (((w % batches + j) % batches) * group + w // batches, w) for w in range(count)
        ]
        parts.append(lax.ppermute(piece, "wide", pairs))
    stacked = jnp.stack(parts)
    picked = [
        lax.dynamic_index_in_dim(stacked, (b - rank) % batches, 0, keepdims=False)
        for b in range(batches)
    ]
    return jnp.stack(picked)


def rotate(values, cosine, sine, heads):
    rows = values.shape[0]
    split = values.reshape(rows, heads, 2, HEAD_DIM // 2)
    u, w = split[:, :, 0], split[:, :, 1]
    c, s = cosine[:, None, :], sine[:, None, :]
    return jnp.stack([u * c - w * s, w * c + u * s], axis=2).reshape(rows, -1)


def normed(x, gain, gain_full):
    gathered = lax.all_gather((x * gain).astype(BF), "narrow", axis=1, tiled=True)
    plain = gathered.astype(F32) / gain_full
    inverse = lax.rsqrt(jnp.mean(plain * plain, axis=1, keepdims=True) + EPSILON)
    return gathered, inverse


def scatter_narrow(partial_sum):
    return lax.psum_scatter(
        partial_sum.astype(BF), "narrow", scatter_dimension=1, tiled=True
    ).astype(F32)


def group_gather(x, group):
    blocks = [x] + [exchange(x, d) for d in range(1, group)]
    stacked = jnp.stack(blocks)
    me = lax.axis_index("wide") % group
    return jnp.concatenate(
        [lax.dynamic_index_in_dim(stacked, k ^ me, 0, keepdims=False) for k in range(group)], axis=0
    )


def group_reduce(x, group):
    me = lax.axis_index("wide") % group
    split = x.reshape(group, x.shape[0] // group, x.shape[1])
    total = lax.dynamic_index_in_dim(split, me, 0, keepdims=False)
    for d in range(1, group):
        piece = lax.dynamic_index_in_dim(split, me ^ d, 0, keepdims=False)
        total = total + exchange(piece.astype(BF), d).astype(F32)
    return total


def attention_forward(x, gain, gain_full, w_qkv, w_out, setup):
    cosine, sine, causal, group = setup
    rows = x.shape[0]
    heads = w_out.shape[1] // HEAD_DIM
    kv = (w_qkv.shape[1] - w_out.shape[1]) // 2 // HEAD_DIM
    gathered, inverse = normed(x, gain, gain_full)
    raw = dot(gathered, w_qkv) * inverse
    cut = heads * HEAD_DIM
    q = rotate(raw[:, :cut], cosine, sine, heads).astype(BF)
    k = rotate(raw[:, cut : cut + kv * HEAD_DIM], cosine, sine, kv).astype(BF)
    v = raw[:, cut + kv * HEAD_DIM :].astype(BF)
    kv_all = group_gather(jnp.concatenate([k, v], axis=1), group)
    length = kv_all.shape[0]
    kh = kv_all[:, : kv * HEAD_DIM].reshape(length, kv, HEAD_DIM)
    vh = kv_all[:, kv * HEAD_DIM :].reshape(length, kv, HEAD_DIM)
    qh = q.reshape(rows, kv, heads // kv, HEAD_DIM)
    s = jnp.einsum("sgrd,lgd->grsl", qh, kh, preferred_element_type=F32) * SCALE
    s = jnp.where(causal, s, NEGATIVE)
    top = jnp.max(s, axis=-1, keepdims=True)
    lse = top + jnp.log(jnp.sum(jnp.exp(s - top), axis=-1, keepdims=True))
    p = jnp.exp(s - lse).astype(BF)
    o = jnp.einsum("grsl,lgd->sgrd", p, vh, preferred_element_type=F32).reshape(rows, -1).astype(BF)
    h = x + scatter_narrow(dot_last(o, w_out))
    return h, (x, gathered, inverse, q, k, v, kv_all, lse, o)


def feed_forward(h, gain, gain_full, w_gu, w_down):
    gathered, inverse = normed(h, gain, gain_full)
    raw = dot(gathered, w_gu) * inverse
    half = raw.shape[1] // 2
    g, u = raw[:, :half], raw[:, half:]
    c = (g * jax.nn.sigmoid(g) * u).astype(BF)
    y = h + scatter_narrow(dot_last(c, w_down))
    return y, (h, gathered, inverse, g, u, c)


def back_norm(back, total, x, inverse, gain, dots):
    width = x.shape[1] * lax.axis_size("narrow")
    dots = lax.psum(dots, "narrow")
    result = back + total * gain - x * (inverse * inverse * dots / width)
    return result, jnp.sum(total * x, axis=0)


def feed_backward(dy, saved, gain, w_gu, w_down):
    h, gathered, inverse, g, u, c = saved
    low = lax.all_gather(dy.astype(BF), "narrow", axis=1, tiled=True)
    dc = dot(low, w_down)
    s = jax.nn.sigmoid(g)
    dg = dc * u * s * (1.0 + g * (1.0 - s))
    du = dc * g * s
    dots = jnp.sum(dg * g + du * u, axis=1, keepdims=True)
    scaled = jnp.concatenate([dg * inverse, du * inverse], axis=1).astype(BF)
    total = scatter_narrow(dot_last(scaled, w_gu))
    dh, dgain = back_norm(dy, total, h, inverse, gain, dots)
    return dh, dgain, dot_first(gathered, scaled).astype(BF), dot_first(low, c).astype(BF)


def attention_backward(dh, saved, gain, w_qkv, w_out, setup):
    cosine, sine, causal, group = setup
    x, gathered, inverse, q, k, v, kv_all, lse, o = saved
    rows = x.shape[0]
    heads = w_out.shape[1] // HEAD_DIM
    kv = k.shape[1] // HEAD_DIM
    low = lax.all_gather(dh.astype(BF), "narrow", axis=1, tiled=True)
    do = dot(low, w_out).astype(BF)
    length = kv_all.shape[0]
    kh = kv_all[:, : kv * HEAD_DIM].reshape(length, kv, HEAD_DIM)
    vh = kv_all[:, kv * HEAD_DIM :].reshape(length, kv, HEAD_DIM)
    qh = q.reshape(rows, kv, heads // kv, HEAD_DIM)
    doh = do.reshape(rows, kv, heads // kv, HEAD_DIM)
    s = jnp.einsum("sgrd,lgd->grsl", qh, kh, preferred_element_type=F32) * SCALE
    s = jnp.where(causal, s, NEGATIVE)
    p = jnp.exp(s - lse)
    dp = jnp.einsum("sgrd,lgd->grsl", doh, vh, preferred_element_type=F32)
    ds = (p * (dp - jnp.sum(p * dp, axis=-1, keepdims=True))).astype(BF)
    dq = jnp.einsum("grsl,lgd->sgrd", ds, kh, preferred_element_type=F32).reshape(rows, -1) * SCALE
    dk = jnp.einsum("grsl,sgrd->lgd", ds, qh, preferred_element_type=F32).reshape(length, -1) * SCALE
    dv = jnp.einsum("grsl,sgrd->lgd", p.astype(BF), doh, preferred_element_type=F32)
    dkv = group_reduce(jnp.concatenate([dk, dv.reshape(length, -1)], axis=1), group)
    dk, dv = dkv[:, : kv * HEAD_DIM], dkv[:, kv * HEAD_DIM :]
    dots = (
        jnp.sum(dq * q.astype(F32), axis=1, keepdims=True)
        + jnp.sum(dk * k.astype(F32), axis=1, keepdims=True)
        + jnp.sum(dv * v.astype(F32), axis=1, keepdims=True)
    )
    raw = jnp.concatenate(
        [rotate(dq, cosine, -sine, heads), rotate(dk, cosine, -sine, kv), dv], axis=1
    )
    scaled = (raw * inverse).astype(BF)
    total = scatter_narrow(dot_last(scaled, w_qkv))
    dx, dgain = back_norm(dh, total, x, inverse, gain, dots)
    return dx, dgain, dot_first(gathered, scaled).astype(BF), dot_first(low, o).astype(BF)


def per_device(tokens, cotangent, *weights):
    layers = [weights[:9], weights[9:]]
    batches, s_dev, width = tokens.shape
    count = lax.axis_size("wide")
    group = count // batches
    me = lax.axis_index("wide")
    rows = batches * s_dev
    halfway = HEAD_DIM // 2
    frequency = jnp.power(F32(THETA), -(jnp.arange(halfway, dtype=F32) * 2.0 / HEAD_DIM))
    pos = (me % group) * rows + jnp.arange(rows, dtype=jnp.int32)
    angle = pos.astype(F32)[:, None] * frequency[None, :]
    causal = jnp.arange(rows * group, dtype=jnp.int32)[None, :] <= pos[:, None]
    setup = (jnp.cos(angle), jnp.sin(angle), causal, group)

    gains = jnp.stack([layers[0][0], layers[0][5], layers[1][0], layers[1][5]])
    gains_full = lax.all_gather(gains, "narrow", axis=1, tiled=True)
    gathered = []
    for q, k, v, o, g, u, d in [(w[1], w[2], w[3], w[4], w[6], w[7], w[8]) for w in layers]:
        packs = [jnp.concatenate([q, k, v], axis=1), o.T, jnp.concatenate([g, u], axis=1), d.T]
        gathered.append([natural(gather_blocks(pack)) for pack in packs])

    y = spread_tokens(tokens).reshape(rows, width).astype(F32)
    saved = []
    for i in range(2):
        w_qkv, w_out, w_gu, w_down = gathered[i]
        h, s1 = attention_forward(y, gains[2 * i], gains_full[2 * i], w_qkv, w_out, setup)
        y, s2 = feed_forward(h, gains[2 * i + 1], gains_full[2 * i + 1], w_gu, w_down)
        saved.append((s1, s2))
    output = collect_tokens(y.reshape(batches, s_dev, width))
    dy = spread_tokens(cotangent).reshape(rows, width).astype(F32)
    grads, dgains = [None, None], [None] * 4
    for i in (1, 0):
        w_qkv, w_out, w_gu, w_down = gathered[i]
        s1, s2 = saved[i]
        dh, dgains[2 * i + 1], d_gu, d_down = feed_backward(dy, s2, gains[2 * i + 1], w_gu, w_down)
        r_down = reduce_blocks(d_down)
        r_gu = reduce_blocks(d_gu)
        dy, dgains[2 * i], d_qkv, d_out = attention_backward(dh, s1, gains[2 * i], w_qkv, w_out, setup)
        r_out = reduce_blocks(d_out)
        r_qkv = reduce_blocks(d_qkv)
        cut_q = layers[i][1].shape[1]
        cut_k = cut_q + layers[i][2].shape[1]
        half = r_gu.shape[1] // 2
        grads[i] = (
            r_qkv[:, :cut_q],
            r_qkv[:, cut_q:cut_k],
            r_qkv[:, cut_k:],
            r_out.T,
            r_gu[:, :half],
            r_gu[:, half:],
            r_down.T,
        )
    input_back = collect_tokens(dy.reshape(batches, s_dev, width))
    dg = lax.psum(jnp.stack(dgains), "wide")
    results = [output, input_back]
    for i in range(2):
        a = grads[i]
        results += [dg[2 * i], a[0], a[1], a[2], a[3], dg[2 * i + 1], a[4], a[5], a[6]]
    return tuple(results)


def solution(mesh):
    tokens = P(None, "wide", "narrow")
    gain, rows, columns = P("narrow"), P("wide", "narrow"), P("narrow", "wide")
    layer = (gain, rows, rows, rows, columns, gain, rows, rows, columns)
    placed = (tokens, tokens) + layer + layer
    return jax.shard_map(
        per_device, mesh=mesh, in_specs=placed, out_specs=placed, check_vma=False
    )
```

time: 2660 us -> 1460 us (0.55)
  waiting for transfers between devices: 2000 us -> 624 us
  starting transfers between devices: 3.21 us -> 261 us
  blocking collectives: 187 us -> 51.3 us
  local copies, waits for them, and re-layouts: 196 us -> 242 us
    reduce_scatter x14 -> x0, waiting for transfers between devices: 937 us -> none  [the longest x1 76.1 us: per_device(): lax.psum_scatter(second_grads[6].astype(jnp.bfloat16), 'wide', scatter_di...]
    all_gather x22 -> x8, waiting for transfers between devices: 685 us -> 24 us  [the longest x2 19.5 us: attention_backward(): low = lax.all_gather(dh.astype(BF), 'narrow', axis=1, tiled=True)]
    ppermute x0 -> x132, waiting for transfers between devices: none -> 503 us  [the longest x116 486 us: exchange(): return lax.ppermute(x, 'wide', [(w, w ^ distance) for w in range(count)])]
    unnamed x60 -> x24, waiting for transfers between devices: 381 us -> 97.4 us
    ppermute x0 -> x132, starting transfers between devices: none -> 259 us  [the longest x116 217 us: exchange(): return lax.ppermute(x, 'wide', [(w, w ^ distance) for w in range(count)])]
    all_gather x8 -> x1, blocking collectives: 156 us -> 5.19 us  [per_device(): gains_full = lax.all_gather(gains, 'narrow', axis=1, tiled=True)]
    unnamed x222 -> x368, local copies, waits for them, and re-layouts: 112 us -> 166 us
    dynamic_slice x56 -> x3, local copies, waits for them, and re-layouts: 41.4 us -> 0.94 us  [the longest x1 0.81 us: spread_tokens(): lax.dynamic_index_in_dim(stacked, (own - r) % batches, 0, keepdims=False)]
  transfers between devices with their start and end apart: 48 -> 148, of which waited for: 43 -> 62; matrix products, arithmetic and copies ran while one was open for 8% -> 22% of each run, Pallas kernels for 0% -> 0%
where the time goes in v1:
time: 1460 us; the launch traced here: 1440 us
  waiting for transfers between devices  624 us (43%)
  starting transfers between devices  261 us (18%)
  local copies, waits for them, and re-layouts  242 us (17%)
  matrix products  144 us (10%)
  other arithmetic  104 us (7%)
  blocking collectives  51.3 us (4%)
  between operations  16.5 us (1%)
    ppermute x116, waiting for transfers between devices, exchange(): return lax.ppermute(x, 'wide', [(w, w ^ distance) for w in range(count)])  486 us
    ppermute x116, starting transfers between devices, exchange(): return lax.ppermute(x, 'wide', [(w, w ^ distance) for w in range(count)])  217 us
    unnamed x368, local copies, waits for them, and re-layouts  166 us
    unnamed x24, waiting for transfers between devices  97.4 us
    dot_general x8, matrix products, dot(): return jnp.dot(left, right, preferred_element_type=F32)  41.4 us
    dot_general x8, matrix products, dot_last(): lax.dot_general(left, right, (((1,), (1,)), ((), ())), preferred_element_...  36.4 us
  transfers between devices with their start and end apart: 148, of which 62 were waited for; matrix products, arithmetic and copies ran while one was open for 22% of the time, Pallas kernels for 0%

profile of v1, /device:TPU:0, one launch (start us, length us, event | category | flops | bytes accessed | tf_op | source)
XLA Modules:
  0.0 1443.5 jit_solution(14306737307807564170)
XLA Ops:
  182.2 22.8 %collective-permute-done.36 = bf16[192,768]{1,0:T(8,128)(2,1)S(1)} collective-permute-done((bf16[192,768]{1,0:T(8,128)(2,1)S(1)}, bf16[192,768]{1,0:T(8,128)(2,1)S(1)}, u32[]{:S(2)}, u32[]{:S(2)}) %collective-permute-start.36) | collective-permute-done | bytes 294944 | tf_op jit(solution)/shard_map/ppermute | solution.py:30
  262.2 20.6 %collective-permute-start.51 = (bf16[192,2048]{1,0:T(8,128)(2,1)}, bf16[192,2048]{1,0:T(8,128)(2,1)}, u32[]{:S(2)}, u32[]{:S(2)}) collective-permute-start(bf16[192,2048]{1,0:T(8,128)(2,1)} %constant_dynamic-update-slice_fusion.34), channel_id=1, source_target_pairs={{0,16},{4,20},{8,24},{12,28},{16,0},{20,4},{24,8},{28,12},{1,17},{... | collective-permute-start | bytes 2359304 | tf_op jit(solution)/shard_map/ppermute | solution.py:30
  286.4 8.5 collective-permute-done.59
  296.3 15.5 %collective-permute-done.32 = bf16[192,1024]{1,0:T(8,128)(2,1)S(1)} collective-permute-done((bf16[192,1024]{1,0:T(8,128)(2,1)S(1)}, bf16[192,1024]{1,0:T(8,128)(2,1)S(1)}, u32[]{:S(2)}, u32[]{:S(2)}) %collective-permute-start.32) | collective-permute-done | bytes 393248 | tf_op jit(solution)/shard_map/ppermute | solution.py:30
  332.7 11.1 collective-permute-done.19
  413.9 8.7 collective-permute-done.23
  429.1 10.0 reduce-scatter.25.cloned.1.call-done
  479.2 28.1 %reduce-scatter.27.cloned.1.call-done = bf16[384,512]{1,0:T(8,128)(2,1)} async-done(((bf16[1536,512]{1,0:T(8,128)(2,1)}), bf16[384,512]{1,0:T(8,128)(2,1)}) %reduce-scatter.27.cloned.1.call-update) | async-done | bytes 393232
  568.0 28.3 %reduce-scatter.29.cloned.1.call-done = bf16[384,512]{1,0:T(8,128)(2,1)} async-done(((bf16[1536,512]{1,0:T(8,128)(2,1)}), bf16[384,512]{1,0:T(8,128)(2,1)}) %reduce-scatter.29.cloned.1.call-update) | async-done | bytes 393232
  628.9 8.8 convolution_multiply_fusion
  671.2 16.6 %reduce-scatter.33.cloned.1.call-done = bf16[384,512]{1,0:T(8,128)(2,1)} async-done(((bf16[1536,512]{1,0:T(8,128)(2,1)}), bf16[384,512]{1,0:T(8,128)(2,1)}) %reduce-scatter.33.cloned.1.call-update) | async-done | bytes 393232
  690.3 19.5 %all-gather.19.cloned.1.call-done = bf16[512,1536]{1,0:T(8,128)(2,1)} async-done(((bf16[512,384]{1,0:T(8,128)(2,1)}), bf16[512,1536]{1,0:T(8,128)(2,1)}) %all-gather.19.cloned.1.call-update) | async-done | bytes 1572880 | tf_op jit(solution)/shard_map/all_gather | solution.py:227
  790.7 14.0 reduce-scatter.35.cloned.1.call-done
  821.1 57.0 %collective-permute-done.128 = bf16[192,1024]{1,0:T(8,128)(2,1)S(1)} collective-permute-done((bf16[192,1024]{1,0:T(8,128)(2,1)S(1)}, bf16[192,1024]{1,0:T(8,128)(2,1)S(1)}, u32[]{:S(2)}, u32[]{:S(2)}) %collective-permute-start.128) | collective-permute-done | bytes 393248 | tf_op jit(solution)/shard_map/ppermute | solution.py:30
  898.4 9.6 collective-permute-done.127
  923.3 70.8 %collective-permute-done.129 = bf16[192,1024]{1,0:T(8,128)(2,1)} collective-permute-done((bf16[192,1024]{1,0:T(8,128)(2,1)}, bf16[192,1024]{1,0:T(8,128)(2,1)}, u32[]{:S(2)}, u32[]{:S(2)}) %collective-permute-start.129) | collective-permute-done | bytes 393248 | tf_op jit(solution)/shard_map/ppermute | solution.py:30
  1095.3 44.8 %collective-permute-done.104 = bf16[192,768]{1,0:T(8,128)(2,1)} collective-permute-done((bf16[192,768]{1,0:T(8,128)(2,1)}, bf16[192,768]{1,0:T(8,128)(2,1)}, u32[]{:S(2)}, u32[]{:S(2)}) %collective-permute-start.104) | collective-permute-done | bytes 294944 | tf_op jit(solution)/shard_map/ppermute | solution.py:30
  1152.0 24.0 %collective-permute-done.108 = bf16[192,768]{1,0:T(8,128)(2,1)S(1)} collective-permute-done((bf16[192,768]{1,0:T(8,128)(2,1)S(1)}, bf16[192,768]{1,0:T(8,128)(2,1)S(1)}, u32[]{:S(2)}, u32[]{:S(2)}) %collective-permute-start.108) | collective-permute-done | bytes 294944 | tf_op jit(solution)/shard_map/ppermute | solution.py:30
  1180.4 25.2 %collective-permute-start.94 = (bf16[192,2048]{1,0:T(8,128)(2,1)S(1)}, bf16[192,2048]{1,0:T(8,128)(2,1)S(1)}, u32[]{:S(2)}, u32[]{:S(2)}) collective-permute-start(bf16[192,2048]{1,0:T(8,128)(2,1)S(1)} %get-tuple-element.62), channel_id=1, source_target_pairs={{0,16},{4,20},{8,24},{12,28},{16,0},{20,4},{24,8},{28,12},{1,17},{... | collective-permute-start | bytes 2359304 | tf_op jit(solution)/shard_map/ppermute | solution.py:30
  1208.4 22.3 %collective-permute-done.101 = bf16[192,1024]{1,0:T(8,128)(2,1)S(1)} collective-permute-done((bf16[192,1024]{1,0:T(8,128)(2,1)S(1)}, bf16[192,1024]{1,0:T(8,128)(2,1)S(1)}, u32[]{:S(2)}, u32[]{:S(2)}) %collective-permute-start.101) | collective-permute-done | bytes 393248 | tf_op jit(solution)/shard_map/ppermute | solution.py:30
  1233.0 27.4 %collective-permute-done.94 = bf16[192,2048]{1,0:T(8,128)(2,1)S(1)} collective-permute-done((bf16[192,2048]{1,0:T(8,128)(2,1)S(1)}, bf16[192,2048]{1,0:T(8,128)(2,1)S(1)}, u32[]{:S(2)}, u32[]{:S(2)}) %collective-permute-start.94) | collective-permute-done | bytes 786464 | tf_op jit(solution)/shard_map/ppermute | solution.py:30
  1330.5 13.3 collective-permute-done.64
  1388.6 10.6 collective-permute-done.80
  1412.6 22.4 %psum.39 = f32[4,384]{1,0:T(4,128)S(1)} all-reduce(f32[4,384]{1,0:T(4,128)S(1)} %pad_maximum_fusion.29), channel_id=1, replica_groups=mesh['wide'=8,'narrow'=4] {'wide'}, use_global_device_ids=true, to_apply=%region_34.35 | all-reduce | flops 1536 | bytes 12288 | tf_op jit(solution)/shard_map/psum | solution.py:311
  (872 shorter events, 886.8 us)
Async XLA Ops:
  7.2 358.8 %all-gather.9.cloned.1.call-start = ((), (), s32[]{:S(2)}) async-start(), calls=%async_computation.8 | async-start | bytes 1966080 | tf_op jit(solution)/shard_map/all_gather | solution.py:133
  7.3 76.7 %collective-permute-start.15 = (bf16[192,384]{1,0:T(8,128)(2,1)}, bf16[192,384]{1,0:T(8,128)(2,1)}, u32[]{:S(2)}, u32[]{:S(2)}) collective-permute-start(bf16[192,384]{1,0:T(8,128)(2,1)} %bitcast.43), channel_id=1, source_target_pairs={{0,16},{4,20},{8,24},{12,28},{16,0},{20,4},{24,8},{28,12},{1,17},{... | collective-permute-start | bytes 442376 | tf_op jit(solution)/shard_map/ppermute | solution.py:30
  69.9 369.2 %reduce-scatter.25.cloned.1.call-start = ((), (), s32[]{:S(2)}) async-start(), calls=%async_computation.16 | async-start | bytes 1966080
  84.0 161.5 %collective-permute-start.29 = (bf16[192,1024]{1,0:T(8,128)(2,1)S(1)}, bf16[192,1024]{1,0:T(8,128)(2,1)S(1)}, u32[]{:S(2)}, u32[]{:S(2)}) collective-permute-start(bf16[192,1024]{1,0:T(8,128)(2,1)S(1)} %bitcast.829), channel_id=1, source_target_pairs={{0,16},{4,20},{8,24},{12,28},{16,0},{20,4},{24,8},{28,12},{1,17},{... | collective-permute-start | bytes 1179656 | tf_op jit(solution)/shard_map/ppermute | solution.py:30
  143.4 140.8 %collective-permute-start.31 = (bf16[192,1024]{1,0:T(8,128)(2,1)S(1)}, bf16[192,1024]{1,0:T(8,128)(2,1)S(1)}, u32[]{:S(2)}, u32[]{:S(2)}) collective-permute-start(bf16[192,1024]{1,0:T(8,128)(2,1)S(1)} %bitcast.832), channel_id=1, source_target_pairs={{0,24},{4,28},{8,16},{12,20},{16,8},{20,12},{24,0},{28,4},{1,25},{... | collective-permute-start | bytes 1179656 | tf_op jit(solution)/shard_map/ppermute | solution.py:30
  245.5 133.1 %collective-permute-start.53 = (bf16[192,2048]{1,0:T(8,128)(2,1)}, bf16[192,2048]{1,0:T(8,128)(2,1)}, u32[]{:S(2)}, u32[]{:S(2)}) collective-permute-start(bf16[192,2048]{1,0:T(8,128)(2,1)} %constant_dynamic-update-slice_fusion.34), channel_id=1, source_target_pairs={{0,24},{4,28},{8,16},{12,20},{16,8},{20,12},{24,0},{28,4},{1,25},{... | collective-permute-start | bytes 2359304 | tf_op jit(solution)/shard_map/ppermute | solution.py:30
  262.2 82.7 %collective-permute-start.51 = (bf16[192,2048]{1,0:T(8,128)(2,1)}, bf16[192,2048]{1,0:T(8,128)(2,1)}, u32[]{:S(2)}, u32[]{:S(2)}) collective-permute-start(bf16[192,2048]{1,0:T(8,128)(2,1)} %constant_dynamic-update-slice_fusion.34), channel_id=1, source_target_pairs={{0,16},{4,20},{8,24},{12,28},{16,0},{20,4},{24,8},{28,12},{1,17},{... | collective-permute-start | bytes 2359304 | tf_op jit(solution)/shard_map/ppermute | solution.py:30
  509.5 86.8 %reduce-scatter.29.cloned.1.call-start = ((), (), s32[]{:S(2)}) async-start(), calls=%async_computation.18 | async-start | bytes 1966080
  599.4 88.4 %reduce-scatter.33.cloned.1.call-start = ((), (), s32[]{:S(2)}) async-start(), calls=%async_computation.20 | async-start | bytes 1966080
  690.0 114.6 %reduce-scatter.35.cloned.1.call-start = ((), (), s32[]{:S(2)}) async-start(), calls=%async_computation.21 | async-start | bytes 1966080
  776.3 231.4 %all-gather.21.cloned.1.call-start = ((), (), s32[]{:S(2)}) async-start(), calls=%async_computation.14 | async-start | bytes 1966080 | tf_op jit(solution)/shard_map/all_gather | solution.py:209
  808.8 232.6 %reduce-scatter.31.cloned.1.call-start = ((), (), s32[]{:S(2)}) async-start(), calls=%async_computation.19 | async-start | bytes 1966080
  817.0 75.1 %collective-permute-start.121 = (bf16[192,2048]{1,0:T(8,128)(2,1)S(1)}, bf16[192,2048]{1,0:T(8,128)(2,1)S(1)}, u32[]{:S(2)}, u32[]{:S(2)}) collective-permute-start(bf16[192,2048]{1,0:T(8,128)(2,1)S(1)} %get-tuple-element.51), channel_id=1, source_target_pairs={{0,4},{4,0},{8,12},{12,8},{16,20},{20,16},{24,28},{28,24},{1,5},{5... | collective-permute-start | bytes 2359304 | tf_op jit(solution)/shard_map/ppermute | solution.py:30
  817.6 77.0 %collective-permute-start.119 = (bf16[192,2048]{1,0:T(8,128)(2,1)S(1)}, bf16[192,2048]{1,0:T(8,128)(2,1)S(1)}, u32[]{:S(2)}, u32[]{:S(2)}) collective-permute-start(bf16[192,2048]{1,0:T(8,128)(2,1)S(1)} %get-tuple-element.52), channel_id=1, source_target_pairs={{0,4},{4,0},{8,12},{12,8},{16,20},{20,16},{24,28},{28,24},{1,5},{5... | collective-permute-start | bytes 2359304 | tf_op jit(solution)/shard_map/ppermute | solution.py:30
  886.5 110.2 %collective-permute-start.118 = (bf16[192,2048]{1,0:T(8,128)(2,1)}, bf16[192,2048]{1,0:T(8,128)(2,1)}, u32[]{:S(2)}, u32[]{:S(2)}) collective-permute-start(bf16[192,2048]{1,0:T(8,128)(2,1)} %get-tuple-element.49), channel_id=1, source_target_pairs={{0,4},{4,0},{8,12},{12,8},{16,20},{20,16},{24,28},{28,24},{1,5},{5... | collective-permute-start | bytes 2359304 | tf_op jit(solution)/shard_map/ppermute | solution.py:30
  896.6 100.2 %collective-permute-start.120 = (bf16[192,2048]{1,0:T(8,128)(2,1)}, bf16[192,2048]{1,0:T(8,128)(2,1)}, u32[]{:S(2)}, u32[]{:S(2)}) collective-permute-start(bf16[192,2048]{1,0:T(8,128)(2,1)} %get-tuple-element.53), channel_id=1, source_target_pairs={{0,8},{4,12},{8,0},{12,4},{16,24},{20,28},{24,16},{28,20},{1,9},{5... | collective-permute-start | bytes 2359304 | tf_op jit(solution)/shard_map/ppermute | solution.py:30
  897.2 99.6 %collective-permute-start.124 = (bf16[192,2048]{1,0:T(8,128)(2,1)}, bf16[192,2048]{1,0:T(8,128)(2,1)}, u32[]{:S(2)}, u32[]{:S(2)}) collective-permute-start(bf16[192,2048]{1,0:T(8,128)(2,1)} %get-tuple-element.54), channel_id=1, source_target_pairs={{0,24},{4,28},{8,16},{12,20},{16,8},{20,12},{24,0},{28,4},{1,25},{... | collective-permute-start | bytes 2359304 | tf_op jit(solution)/shard_map/ppermute | solution.py:30
  908.0 88.8 %collective-permute-start.122 = (bf16[192,2048]{1,0:T(8,128)(2,1)}, bf16[192,2048]{1,0:T(8,128)(2,1)}, u32[]{:S(2)}, u32[]{:S(2)}) collective-permute-start(bf16[192,2048]{1,0:T(8,128)(2,1)} %get-tuple-element.55), channel_id=1, source_target_pairs={{0,16},{4,20},{8,24},{12,28},{16,0},{20,4},{24,8},{28,12},{1,17},{... | collective-permute-start | bytes 2359304 | tf_op jit(solution)/shard_map/ppermute | solution.py:30
  913.2 81.0 %collective-permute-start.129 = (bf16[192,1024]{1,0:T(8,128)(2,1)}, bf16[192,1024]{1,0:T(8,128)(2,1)}, u32[]{:S(2)}, u32[]{:S(2)}) collective-permute-start(bf16[192,1024]{1,0:T(8,128)(2,1)} %get-tuple-element.72), channel_id=1, source_target_pairs={{0,16},{4,20},{8,24},{12,28},{16,0},{20,4},{24,8},{28,12},{1,17},{... | collective-permute-start | bytes 1179656 | tf_op jit(solution)/shard_map/ppermute | solution.py:30
  923.1 155.7 %reduce-scatter.37.cloned.1.call-start = ((), (), s32[]{:S(2)}) async-start(), calls=%async_computation.22 | async-start | bytes 1966080
  1025.4 239.1 %all-gather.23.cloned.1.call-start = ((), (), s32[]{:S(2)}) async-start(), calls=%async_computation.15 | async-start | bytes 1966080 | tf_op jit(solution)/shard_map/all_gather | solution.py:227
  1092.9 309.0 %reduce-scatter.39.cloned.1.call-start = ((), (), s32[]{:S(2)}) async-start(), calls=%async_computation.23 | async-start | bytes 1966080
  1152.0 80.9 %collective-permute-start.90 = (bf16[192,2048]{1,0:T(8,128)(2,1)S(1)}, bf16[192,2048]{1,0:T(8,128)(2,1)S(1)}, u32[]{:S(2)}, u32[]{:S(2)}) collective-permute-start(bf16[192,2048]{1,0:T(8,128)(2,1)S(1)} %copy-done.60), channel_id=1, source_target_pairs={{0,4},{4,0},{8,12},{12,8},{16,20},{20,16},{24,28},{28,24},{1,5},{5... | collective-permute-start | bytes 2359304 | tf_op jit(solution)/shard_map/ppermute | solution.py:30
  1180.4 80.0 %collective-permute-start.94 = (bf16[192,2048]{1,0:T(8,128)(2,1)S(1)}, bf16[192,2048]{1,0:T(8,128)(2,1)S(1)}, u32[]{:S(2)}, u32[]{:S(2)}) collective-permute-start(bf16[192,2048]{1,0:T(8,128)(2,1)S(1)} %get-tuple-element.62), channel_id=1, source_target_pairs={{0,16},{4,20},{8,24},{12,28},{16,0},{20,4},{24,8},{28,12},{1,17},{... | collective-permute-start | bytes 2359304 | tf_op jit(solution)/shard_map/ppermute | solution.py:30
  (247 other events, 6463.7 us)
Sparse Core Ops, SparseCore 0:
  70.0 19.8 all-gather.8
  405.5 33.5 reduce-scatter.24
  441.4 19.6 all-gather.10
  479.2 28.0 reduce-scatter.26
  509.6 19.6 all-gather.12
  568.1 28.1 reduce-scatter.28
  598.6 19.6 all-gather.14
  620.4 19.6 all-gather.16
  659.6 28.1 reduce-scatter.32
  690.2 19.6 all-gather.18
  776.5 28.1 reduce-scatter.34
  808.9 19.6 all-gather.20
  923.2 26.1 reduce-scatter.30
  1025.5 26.5 reduce-scatter.36
  1093.1 17.8 all-gather.22
  1314.1 26.5 reduce-scatter.38

commit v2 on v1

--- a/solution.py
+++ b/solution.py
@@ -1,6 +1,10 @@
+import functools
+
 import jax
 import jax.numpy as jnp
 from jax import lax
+from jax.experimental import pallas as pl
+from jax.experimental.pallas import tpu as pltpu
 from jax.sharding import PartitionSpec as P
 
 HEAD_DIM = 96
@@ -255,6 +259,512 @@
     return dx, dgain, dot_first(gathered, scaled).astype(BF), dot_first(low, o).astype(BF)
 
 
+MESH = pl.DeviceIdType.MESH
+QKV, OUT, GATE, UP, DOWN = range(5)
+PIECES = 5
+TILE = 256
+
+
+def flip(index, distance):
+    for bit in bits_below(2 * distance):
+        if distance & bit:
+            index = index + bit * (1 - 2 * ((index // bit) % 2))
+    return index
+
+
+def top_bit(value):
+    return bits_below(value + 1)[-1]
+
+
+class Wide:
+    def __init__(self, count):
+        self.count = count
+        self.inner = count // OUTER
+        self.bits = bits_below(self.inner)
+        direct = [j for j in range(1, count) if j % self.inner == 0]
+        rest = [j for j in range(1, count) if j % self.inner]
+        rest.sort(key=lambda j: (top_bit(j % self.inner), j))
+        self.direct, self.rest = direct, rest
+
+    def via(self, j):
+        low = j % self.inner
+        return top_bit(low) if low else j
+
+    def sends(self, i):
+        low = i % self.inner
+        bits = [b for b in self.bits if low == 0 or b > top_bit(low)]
+        return (self.direct + bits) if i == 0 else bits
+
+
+def rows_of(index, size):
+    return pl.ds(pl.multiple_of(index * size, size), size)
+
+
+def each_tile(rows, tile, body):
+    def step(i, carry):
+        body(pl.ds(pl.multiple_of(i * tile, tile), tile))
+        return carry
+
+    lax.fori_loop(0, rows // tile, step, 0)
+
+
+def rotated(raw, cosine, sine):
+    width = raw.shape[1]
+    lane = lax.broadcasted_iota(jnp.int32, raw.shape, 1)
+    first = lane % HEAD_DIM < HEAD_DIM // 2
+    half = HEAD_DIM // 2
+    partner = jnp.where(first, pltpu.roll(raw, width - half, 1), pltpu.roll(raw, half, 1))
+    return raw * cosine + partner * sine
+
+
+def enter(count, me, n):
+    barrier = pltpu.get_barrier_semaphore()
+    for d in range(1, count):
+        pl.semaphore_signal(barrier, inc=1, device_id=(flip(me, d), n), device_id_type=MESH)
+    for d in range(1, 4):
+        pl.semaphore_signal(barrier, inc=1, device_id=(me, flip(n, d)), device_id_type=MESH)
+    pl.semaphore_wait(barrier, count + 2)
+
+
+def remote(src, dst, send, recv, target):
+    return pltpu.make_async_remote_copy(
+        src_ref=src, dst_ref=dst, send_sem=send, recv_sem=recv, device_id=target, device_id_type=MESH
+    )
+
+
+def forward_kernel(
+    count,
+    tokens, cotangent, gains, cosine, sine, select,
+    p_qkv, p_out, p_gate, p_up, p_down,
+    a_qkv, a_out, a_gate, a_up, a_down,
+    o_xall, o_resid, o_rinv, o_q, o_kv, o_mix, o_lse, o_g, o_u, o_c, o_dy,
+    w_qkv, w_out, w_gate, w_up, w_down,
+    tok, gall, xall, resid, rinv, qpad, kvall, kvpad, mixpad, mix, lse, gst, ust, cst,
+    own, stage, crecv, yrecv,
+    bsend, brecv, bown, load, tsend, trecv, dsend, drecv, gsend, grecv,
+    agsend, agrecv, ksend, krecv, rsend, rrecv, save,
+):
+    me, n = lax.axis_index("wide"), lax.axis_index("narrow")
+    wide = Wide(count)
+    batches, s_dev, width = tokens.shape
+    rows = batches * s_dev
+    group = count // batches
+    packs = (p_qkv, p_out, p_gate, p_up, p_down)
+    alls = (a_qkv, a_out, a_gate, a_up, a_down)
+    bufs = (w_qkv, w_out, w_gate, w_up, w_down)
+    kr = p_qkv.shape[1]
+    heads = qpad.shape[2] // 128
+    kv = kvpad.shape[2] // 256
+    length = kvpad.shape[1]
+    core, other, cross = flip(n, 1), flip(n, 2), flip(n, 3)
+    enter(count, me, n)
+
+    rank, place = me % batches, me // batches
+
+    def spread(source, target, send, recv, start):
+        for b in range(batches):
+            to = b * group + place
+
+            @pl.when(to != me)
+            def _():
+                c = remote(source.at[b], target.at[rank], send.at[b], recv.at[rank], (to, n))
+                c.start() if start else c.wait_send()
+
+            if start:
+
+                @pl.when(to == me)
+                def _():
+                    pltpu.make_async_copy(source.at[b], target.at[rank], recv.at[rank]).start()
+
+    def spread_wait(source, target, send, recv):
+        for r in range(batches):
+            origin = (me % group) * batches + r
+
+            @pl.when(origin != me)
+            def _():
+                remote(source.at[0], target.at[r], send.at[0], recv.at[r], (origin, n)).wait_recv()
+
+            @pl.when(origin == me)
+            def _():
+                pltpu.make_async_copy(source.at[0], target.at[r], recv.at[r]).wait()
+
+    def gain_copy(d):
+        return remote(gall.at[n], gall.at[n], gsend.at[d], grecv.at[d], (me, flip(n, d)))
+
+    def gain_in(d):
+        return remote(gall.at[n], gall.at[flip(n, d)], gsend.at[d], grecv.at[d], (me, flip(n, d)))
+
+    spread(tokens, tok, tsend, trecv, True)
+    gall[n] = gains[...]
+    for d in (1, 2, 3):
+        gain_copy(d).start()
+
+    def piece_copy(l, c, i, dist):
+        block = rows_of(flip(me, i), kr)
+        src = packs[c].at[l] if i == 0 else alls[c].at[l, block]
+        t, j = l * PIECES + c, i ^ dist
+        return remote(src, alls[c].at[l, block], bsend.at[t, j], brecv.at[t, j], (flip(me, dist), n))
+
+    def piece_in(l, c, j):
+        block = rows_of(flip(me, j), kr)
+        dst = alls[c].at[l, block]
+        t = l * PIECES + c
+        return remote(dst, dst, bsend.at[t, j], brecv.at[t, j], (flip(me, wide.via(j)), n))
+
+    def piece_own(l, c):
+        return pltpu.make_async_copy(
+            packs[c].at[l], alls[c].at[l, rows_of(me, kr)], bown.at[l * PIECES + c]
+        )
+
+    def send_own(l, c):
+        for dist in wide.sends(0):
+            piece_copy(l, c, 0, dist).start()
+        piece_own(l, c).start()
+
+    def relay(l, c):
+        for j in wide.direct:
+            piece_in(l, c, j).wait_recv()
+            for dist in wide.sends(j):
+                piece_copy(l, c, j, dist).start()
+        ahead = c + 2
+        if ahead < PIECES:
+            send_own(l, ahead)
+        else:
+
+            @pl.when(l == 0)
+            def _():
+                send_own(1, ahead - PIECES)
+
+    def arrive(l, c):
+        for j in wide.rest:
+            piece_in(l, c, j).wait_recv()
+            for dist in wide.sends(j):
+                piece_copy(l, c, j, dist).start()
+        piece_own(l, c).wait()
+        fetch = pltpu.make_async_copy(alls[c].at[l], bufs[c], load.at[c])
+        fetch.start()
+        fetch.wait()
+
+    send_own(0, QKV)
+    send_own(0, OUT)
+    spread(cotangent, o_dy, dsend, drecv, True)
+    spread_wait(tokens, tok, tsend, trecv)
+    for b in range(batches):
+        resid[0, b * s_dev : (b + 1) * s_dev] = tok[b].astype(F32)
+    for d in (1, 2, 3):
+        gain_in(d).wait_recv()
+
+    def ag_own(a, dist):
+        return remote(
+            xall.at[a, n], xall.at[a, n], agsend.at[a, dist], agrecv.at[a, dist], (me, flip(n, dist))
+        )
+
+    def ag_in(a, dist):
+        ref = xall.at[a, flip(n, dist)]
+        return remote(ref, ref, agsend.at[a, dist], agrecv.at[a, dist], (me, flip(n, dist)))
+
+    def ag_forward(a):
+        ref = xall.at[a, other]
+        return remote(ref, ref, agsend.at[a, 3], agrecv.at[a, 3], (me, core))
+
+    def ag_start(a):
+        gain = gall[n, pl.ds(a, 1), :]
+
+        def body(r):
+            xall[a, n, r] = (resid[a, r] * gain).astype(BF)
+
+        each_tile(rows, 128, body)
+        ag_own(a, 2).start()
+        ag_own(a, 1).start()
+
+    def ag_finish(a):
+        ag_in(a, 2).wait_recv()
+        ag_forward(a).start()
+        ag_in(a, 1).wait_recv()
+        ref = xall.at[a, cross]
+        remote(ref, ref, agsend.at[a, 3], agrecv.at[a, 3], (me, core)).wait_recv()
+        inverse = [1.0 / gall[s, pl.ds(a, 1), :] for s in range(4)]
+
+        def body(r):
+            total = 0.0
+            for s in range(4):
+                plain = xall[a, s, r].astype(F32) * inverse[s]
+                total = total + jnp.sum(plain * plain, axis=1, keepdims=True)
+            rinv[a, r] = lax.rsqrt(total * (1.0 / (4 * width)) + EPSILON)
+
+        each_tile(rows, 128, body)
+
+    def rs_core(a, k):
+        return remote(stage.at[k], crecv.at[a, k], rsend.at[a, k], rrecv.at[a, k], (me, core))
+
+    def rs_other(a):
+        return remote(stage.at[2], yrecv.at[a], rsend.at[a, 2], rrecv.at[a, 2], (me, other))
+
+    def reduce_narrow(a, product):
+        for k, b in ((1, cross), (0, core)):
+
+            def body(r, k=k, b=b):
+                stage[k, r] = product(b, r).astype(BF)
+
+            each_tile(rows, TILE, body)
+            rs_core(a, k).start()
+
+        def body_other(r):
+            own[r] = product(other, r)
+
+        each_tile(rows, TILE, body_other)
+        rs_core(a, 1).wait_recv()
+
+        def add_other(r):
+            stage[2, r] = (own[r] + crecv[a, 1, r].astype(F32)).astype(BF)
+
+        each_tile(rows, 128, add_other)
+        rs_other(a).start()
+
+        def body_own(r):
+            own[r] = product(n, r)
+
+        each_tile(rows, TILE, body_own)
+        rs_core(a, 0).wait_recv()
+        rs_other(a).wait_recv()
+
+        def add_own(r):
+            resid[a + 1, r] = (
+                resid[a, r] + own[r] + crecv[a, 0, r].astype(F32) + yrecv[a, r].astype(F32)
+            )
+
+        each_tile(rows, 128, add_own)
+        rs_core(a, 1).wait_send()
+        rs_core(a, 0).wait_send()
+        rs_other(a).wait_send()
+
+    mine = me % group
+
+    def kv_copy(l, d):
+        part = kvall.at[l, rows_of(mine, rows)]
+        return remote(part, part, ksend.at[l, d], krecv.at[l, d], (flip(me, d), n))
+
+    def kv_in(l, d):
+        part = kvall.at[l, rows_of(flip(mine, d), rows)]
+        return remote(part, part, ksend.at[l, d], krecv.at[l, d], (flip(me, d), n))
+
+    tile_q = TILE if length <= 2048 else 128
+
+    def attention(l):
+        each_tile(length, TILE, lambda r: kvpad.__setitem__(
+            (l, r), dot(kvall[l, r], select[...]).astype(BF)))
+
+        def step(i, carry):
+            h, part = i // (rows // tile_q), i % (rows // tile_q)
+            r = rows_of(part, tile_q)
+            g = h // (heads // kv)
+            lanes = rows_of(h, 128)
+            s = dot_last(qpad[l, r, lanes], kvpad[l, :, rows_of(g, 128)]) * SCALE
+            pos = mine * rows + part * tile_q + lax.broadcasted_iota(jnp.int32, s.shape, 0)
+            s = jnp.where(lax.broadcasted_iota(jnp.int32, s.shape, 1) <= pos, s, NEGATIVE)
+            top = jnp.max(s, axis=1, keepdims=True)
+            total = jnp.sum(jnp.exp(s - top), axis=1, keepdims=True)
+            norm = top + jnp.log(total)
+            p = jnp.exp(s - norm).astype(BF)
+            lse[l, h, r] = norm
+            mixpad[r, lanes] = dot(p, kvpad[l, :, rows_of(kv + g, 128)]).astype(BF)
+            return carry
+
+        lax.fori_loop(0, heads * (rows // tile_q), step, 0)
+        each_tile(rows, TILE, lambda r: mix.__setitem__(
+            (l, r), dot_last(mixpad[r], select[...]).astype(BF)))
+
+    def narrow_sum(a, ref, r, columns):
+        total = 0.0
+        for s in range(4):
+            total = total + dot(xall[a, s, r], ref[s * width : (s + 1) * width, columns])
+        return total
+
+    def saved(src, dst, index):
+        return pltpu.make_async_copy(src, dst, save.at[index])
+
+    def layer_saves(l):
+        pairs = [
+            (xall.at[2 * l], o_xall.at[2 * l]), (xall.at[2 * l + 1], o_xall.at[2 * l + 1]),
+            (rinv.at[2 * l], o_rinv.at[2 * l]), (rinv.at[2 * l + 1], o_rinv.at[2 * l + 1]),
+            (resid.at[2 * l], o_resid.at[2 * l]), (resid.at[2 * l + 1], o_resid.at[2 * l + 1]),
+            (qpad.at[l], o_q.at[l]), (kvpad.at[l], o_kv.at[l]), (mix.at[l], o_mix.at[l]),
+            (lse.at[l], o_lse.at[l]), (gst, o_g.at[l]), (ust, o_u.at[l]), (cst, o_c.at[l]),
+        ]
+        return [functools.partial(saved, s, d, i) for i, (s, d) in enumerate(pairs)]
+
+    def layer(l, carry):
+        first, second = 2 * l, 2 * l + 1
+        ag_start(first)
+        ag_finish(first)
+        relay(l, QKV)
+        arrive(l, QKV)
+
+        def project(r):
+            cut = heads * HEAD_DIM
+            for half in (1, 0):
+                columns = slice(half * cut, (half + 1) * cut)
+                raw = narrow_sum(first, w_qkv, r, columns) * rinv[first, r]
+                low = rotated(raw, cosine[r, columns], sine[r, columns]).astype(BF)
+                if half:
+                    base = pl.multiple_of(mine * rows, rows) + r.start
+                    kvall[l, pl.ds(pl.multiple_of(base, TILE), TILE)] = low
+                else:
+                    qpad[l, r] = dot(low, select[...]).astype(BF)
+
+        each_tile(rows, TILE, project)
+        for d in range(1, group):
+            kv_copy(l, d).start()
+        relay(l, OUT)
+        for d in range(1, group):
+            kv_in(l, d).wait_recv()
+        attention(l)
+        relay(l, GATE)
+        arrive(l, OUT)
+        reduce_narrow(
+            first, lambda b, r: dot_last(mix[l, r], w_out[rows_of(b, width)])
+        )
+        ag_start(second)
+        ag_finish(second)
+        relay(l, UP)
+        arrive(l, GATE)
+        arrive(l, UP)
+
+        @pl.when(l == 1)
+        def _():
+            for c in layer_saves(0)[10:]:
+                c().wait()
+
+        columns_of = lambda j: rows_of(j, TILE)
+
+        def hidden(j, carry):
+            columns = columns_of(j)
+
+            def body(r):
+                g = narrow_sum(second, w_gate, r, columns) * rinv[second, r]
+                u = narrow_sum(second, w_up, r, columns) * rinv[second, r]
+                gst[r, columns] = g
+                ust[r, columns] = u
+                cst[r, columns] = (g / (1.0 + jnp.exp(-g)) * u).astype(BF)
+
+            each_tile(rows, TILE, body)
+            return carry
+
+        lax.fori_loop(0, w_gate.shape[1] // TILE, hidden, 0)
+        for c in layer_saves(l):
+            c().start()
+        relay(l, DOWN)
+        arrive(l, DOWN)
+        reduce_narrow(
+            second, lambda b, r: dot_last(cst[r], w_down[rows_of(b, width)])
+        )
+        return carry
+
+    lax.fori_loop(0, 2, layer, 0)
+    last = saved(resid.at[4], o_resid.at[4], 13)
+    last.start()
+    for c in layer_saves(0)[:10]:
+        c().wait()
+    for c in layer_saves(1):
+        c().wait()
+    last.wait()
+    spread_wait(cotangent, o_dy, dsend, drecv)
+    spread(tokens, tok, tsend, trecv, False)
+    spread(cotangent, o_dy, dsend, drecv, False)
+    for d in (1, 2, 3):
+        gain_copy(d).wait_send()
+
+    def drain(l, carry):
+        for c in range(PIECES):
+            for i in range(count):
+                for dist in wide.sends(i):
+                    piece_copy(l, c, i, dist).wait_send()
+        for d in range(1, group):
+            kv_copy(l, d).wait_send()
+        for a in (2 * l, 2 * l + 1):
+            ag_own(a, 1).wait_send()
+            ag_own(a, 2).wait_send()
+            ag_forward(a).wait_send()
+        return carry
+
+    lax.fori_loop(0, 2, drain, 0)
+
+
+def forward_pass(tokens, cotangent, gains, cosine, sine, select, packs, heads, kv):
+    count = lax.axis_size("wide")
+    batches, s_dev, width = tokens.shape
+    rows, group = batches * s_dev, count // batches
+    length = rows * group
+    kr = packs[0].shape[1]
+    ff = packs[GATE].shape[2]
+    sd = jax.ShapeDtypeStruct
+    whole = [sd((2, kr * count, p.shape[2]), BF) for p in packs]
+    outs = whole + [
+        sd((4, 4, rows, width), BF),
+        sd((5, rows, width), F32),
+        sd((4, rows, 1), F32),
+        sd((2, rows, heads * 128), BF),
+        sd((2, length, kv * 256), BF),
+        sd((2, rows, heads * HEAD_DIM), BF),
+        sd((2, heads, rows, 1), F32),
+        sd((2, rows, ff), F32),
+        sd((2, rows, ff), F32),
+        sd((2, rows, ff), BF),
+        sd((batches, s_dev, width), BF),
+    ]
+    dma = pltpu.SemaphoreType.DMA
+    scratch = [pltpu.VMEM((kr * count, p.shape[2]), BF) for p in packs] + [
+        pltpu.VMEM((batches, s_dev, width), BF),
+        pltpu.VMEM((4, 8, width), F32),
+        pltpu.VMEM((4, 4, rows, width), BF),
+        pltpu.VMEM((5, rows, width), F32),
+        pltpu.VMEM((4, rows, 1), F32),
+        pltpu.VMEM((2, rows, heads * 128), BF),
+        pltpu.VMEM((2, length, kv * 2 * HEAD_DIM), BF),
+        pltpu.VMEM((2, length, kv * 256), BF),
+        pltpu.VMEM((rows, heads * 128), BF),
+        pltpu.VMEM((2, rows, heads * HEAD_DIM), BF),
+        pltpu.VMEM((2, heads, rows, 1), F32),
+        pltpu.VMEM((rows, ff), F32),
+        pltpu.VMEM((rows, ff), F32),
+        pltpu.VMEM((rows, ff), BF),
+        pltpu.VMEM((rows, width), F32),
+        pltpu.VMEM((3, rows, width), BF),
+        pltpu.VMEM((4, 2, rows, width), BF),
+        pltpu.VMEM((4, rows, width), BF),
+        dma((2 * PIECES, count)),
+        dma((2 * PIECES, count)),
+        dma((2 * PIECES,)),
+        dma((PIECES,)),
+        dma((batches,)),
+        dma((batches,)),
+        dma((batches,)),
+        dma((batches,)),
+        dma((4,)),
+        dma((4,)),
+        dma((4, 4)),
+        dma((4, 4)),
+        dma((2, group)),
+        dma((2, group)),
+        dma((4, 3)),
+        dma((4, 3)),
+        dma((14,)),
+    ]
+    hbm = pl.BlockSpec(memory_space=pl.ANY)
+    vmem = pl.BlockSpec(memory_space=pltpu.VMEM)
+    return pl.pallas_call(
+        functools.partial(forward_kernel, count),
+        out_shape=outs,
+        in_specs=[hbm, hbm] + [vmem] * 4 + [hbm] * PIECES,
+        out_specs=[hbm] * len(outs),
+        scratch_shapes=scratch,
+        compiler_params=pltpu.CompilerParams(
+            collective_id=0, has_side_effects=True, vmem_limit_bytes=60 * 1024 * 1024
+        ),
+        name="forward",
+    )(tokens, cotangent, gains, cosine, sine, select, *packs)
+
+
 def per_device(tokens, cotangent, *weights):
     layers = [weights[:9], weights[9:]]
     batches, s_dev, width = tokens.shape
@@ -263,28 +773,54 @@
     me = lax.axis_index("wide")
     rows = batches * s_dev
     halfway = HEAD_DIM // 2
+    heads = layers[0][1].shape[1] // HEAD_DIM
+    kv = layers[0][2].shape[1] // HEAD_DIM
     frequency = jnp.power(F32(THETA), -(jnp.arange(halfway, dtype=F32) * 2.0 / HEAD_DIM))
     pos = (me % group) * rows + jnp.arange(rows, dtype=jnp.int32)
     angle = pos.astype(F32)[:, None] * frequency[None, :]
     causal = jnp.arange(rows * group, dtype=jnp.int32)[None, :] <= pos[:, None]
-    setup = (jnp.cos(angle), jnp.sin(angle), causal, group)
+    cos, sin = jnp.cos(angle), jnp.sin(angle)
+    setup = (cos, sin, causal, group)
+    cut = kv * HEAD_DIM
+    cosine = jnp.concatenate([cos] * (2 * (heads + kv)) + [jnp.ones((rows, cut), F32)], axis=1)
+    sine = jnp.concatenate([-sin, sin] * (heads + kv) + [jnp.zeros((rows, cut), F32)], axis=1)
+    place = jnp.arange(heads * HEAD_DIM)
+    select = (
+        (place // HEAD_DIM * 128 + place % HEAD_DIM)[:, None] == jnp.arange(heads * 128)[None, :]
+    ).astype(BF)
 
     gains = jnp.stack([layers[0][0], layers[0][5], layers[1][0], layers[1][5]])
-    gains_full = lax.all_gather(gains, "narrow", axis=1, tiled=True)
-    gathered = []
-    for q, k, v, o, g, u, d in [(w[1], w[2], w[3], w[4], w[6], w[7], w[8]) for w in layers]:
-        packs = [jnp.concatenate([q, k, v], axis=1), o.T, jnp.concatenate([g, u], axis=1), d.T]
-        gathered.append([natural(gather_blocks(pack)) for pack in packs])
-
-    y = spread_tokens(tokens).reshape(rows, width).astype(F32)
+    gains_in = jnp.concatenate([gains, jnp.ones_like(gains)], axis=0)
+    packs = [
+        jnp.stack([jnp.concatenate([w[1], w[2], w[3]], axis=1) for w in layers]),
+        jnp.stack([w[4].T for w in layers]),
+        jnp.stack([w[6] for w in layers]),
+        jnp.stack([w[7] for w in layers]),
+        jnp.stack([w[8].T for w in layers]),
+    ]
+    outs = forward_pass(tokens, cotangent, gains_in, cosine, sine, select, packs, heads, kv)
+    a_qkv, a_out, a_gate, a_up, a_down = outs[:PIECES]
+    o_xall, o_resid, o_rinv, o_q, o_kv, o_mix, o_lse, o_g, o_u, o_c, o_dy = outs[PIECES:]
     saved = []
+    unpad = lambda x, m: x.reshape(x.shape[0], m, 128)[:, :, :HEAD_DIM].reshape(x.shape[0], -1)
     for i in range(2):
-        w_qkv, w_out, w_gu, w_down = gathered[i]
-        h, s1 = attention_forward(y, gains[2 * i], gains_full[2 * i], w_qkv, w_out, setup)
-        y, s2 = feed_forward(h, gains[2 * i + 1], gains_full[2 * i + 1], w_gu, w_down)
+        full = lambda a: jnp.concatenate([o_xall[a, s] for s in range(4)], axis=1)
+        kv_all = unpad(o_kv[i], 2 * kv)
+        own = lax.dynamic_slice_in_dim(kv_all, (me % group) * rows, rows, 0)
+        lse = o_lse[i].reshape(kv, heads // kv, rows, 1)
+        s1 = (
+            o_resid[2 * i], full(2 * i), o_rinv[2 * i], unpad(o_q[i], heads),
+            own[:, :cut], own[:, cut:], kv_all, lse, o_mix[i],
+        )
+        s2 = (o_resid[2 * i + 1], full(2 * i + 1), o_rinv[2 * i + 1], o_g[i], o_u[i], o_c[i])
         saved.append((s1, s2))
+    gathered = [
+        (a_qkv[i], a_out[i], jnp.concatenate([a_gate[i], a_up[i]], axis=1), a_down[i])
+        for i in range(2)
+    ]
+    y = o_resid[4]
     output = collect_tokens(y.reshape(batches, s_dev, width))
-    dy = spread_tokens(cotangent).reshape(rows, width).astype(F32)
+    dy = o_dy.reshape(rows, width).astype(F32)
     grads, dgains = [None, None], [None] * 4
     for i in (1, 0):
         w_qkv, w_out, w_gu, w_down = gathered[i]

time: 1460 us -> 1110 us (0.76)
  Pallas kernels: 0 us -> 392 us
  waiting for transfers between devices: 624 us -> 270 us
  local copies, waits for them, and re-layouts: 242 us -> 91.2 us
  starting transfers between devices: 261 us -> 124 us
  matrix products: 144 us -> 92.2 us
  other arithmetic: 104 us -> 63 us
    pallas_call x0 -> x1, Pallas kernels: none -> 392 us  [forward_pass(): pl.pallas_call(functools.partial(forward_kernel, count), out_shape=outs,...]
    ppermute x116 -> x58, waiting for transfers between devices: 486 us -> 230 us  [exchange(): return lax.ppermute(x, 'wide', [(w, w ^ distance) for w in range(count)])]
    unnamed x368 -> x216, local copies, waits for them, and re-layouts: 166 us -> 23.1 us
    ppermute x116 -> x58, starting transfers between devices: 217 us -> 96.4 us  [exchange(): return lax.ppermute(x, 'wide', [(w, w ^ distance) for w in range(count)])]
    unnamed x24 -> x12, waiting for transfers between devices: 97.4 us -> 18.9 us
    ppermute x8 -> x0, starting transfers between devices: 23.2 us -> none  [spread_tokens(): parts.append(lax.ppermute(piece, 'wide', pairs))]
    dot_general x8 -> x4, matrix products: 36.4 us -> 15.6 us  [dot_last(): lax.dot_general(left, right, (((1,), (1,)), ((), ())), preferred_element_...]
    dot_general x8 -> x4, matrix products: 41.4 us -> 21.1 us  [dot(): return jnp.dot(left, right, preferred_element_type=F32)]
  transfers between devices with their start and end apart: 148 -> 74, of which waited for: 62 -> 28; matrix products, arithmetic and copies ran while one was open for 22% -> 15% of each run, Pallas kernels for 0% -> 0%
where the time goes in v2:
time: 1110 us; the launch traced here: 1090 us
  Pallas kernels  392 us (35%)
  waiting for transfers between devices  270 us (24%)
  starting transfers between devices  124 us (11%)
  matrix products  92.2 us (8%)
  local copies, waits for them, and re-layouts  91.2 us (8%)
  other arithmetic  63 us (6%)
  blocking collectives  44.7 us (4%)
  between operations  16.6 us (1%)
    pallas_call x1, Pallas kernels, forward_pass(): pl.pallas_call(functools.partial(forward_kernel, count), out_shape=outs,...  392 us
    ppermute x58, waiting for transfers between devices, exchange(): return lax.ppermute(x, 'wide', [(w, w ^ distance) for w in range(count)])  230 us
    ppermute x58, starting transfers between devices, exchange(): return lax.ppermute(x, 'wide', [(w, w ^ distance) for w in range(count)])  96.4 us
    ppermute x8, starting transfers between devices, collect_tokens(): parts.append(lax.ppermute(piece, 'wide', pairs))  25.9 us
    psum x4, blocking collectives, back_norm(): dots = lax.psum(dots, 'narrow')  23.9 us
    unnamed x216, local copies, waits for them, and re-layouts  23.1 us
  transfers between devices with their start and end apart: 74, of which 28 were waited for; matrix products, arithmetic and copies ran while one was open for 15% of the time, Pallas kernels for 0%

profile of v2, /device:TPU:0, one launch (start us, length us, event | category | flops | bytes accessed | tf_op | source)
XLA Modules:
  0.0 1093.1 jit_solution(14939558743701787299)
XLA Ops:
  25.0 392.1 %forward.1 = (bf16[2,1536,768]{2,1,0:T(8,128)(2,1)}, bf16[2,1536,384]{2,1,0:T(8,128)(2,1)}, bf16[2,1536,1024]{2,1,0:T(8,128)(2,1)}, bf16[2,1536,1024]{2,1,0:T(8,...) custom-call(bf16[4,128,384]{2,1,0:T(8,128)(2,1)} %tokens.1, ...), custom_call_target="tpu_custom_call" | custom-call | tf_op jit(solution)/shard_map/forward/pallas_call | solution.py:755
  420.0 6.3 slice_bitcast_fusion.1
  429.8 13.6 %all-gather.5.cloned.1.call-done = bf16[512,1536]{1,0:T(8,128)(2,1)} async-done(((bf16[512,384]{1,0:T(8,128)(2,1)}), bf16[512,1536]{1,0:T(8,128)(2,1)}) %all-gather.5.cloned.1.call-update) | async-done | bytes 1572880 | tf_op jit(solution)/shard_map/all_gather | solution.py:213
  443.4 7.5 multiply_convert_fusion.3
  469.1 18.7 %reduce-scatter.13.cloned.1.call-done = bf16[384,512]{1,0:T(8,128)(2,1)} async-done(((bf16[1536,512]{1,0:T(8,128)(2,1)}), bf16[384,512]{1,0:T(8,128)(2,1)}) %reduce-scatter.13.cloned.1.call-update) | async-done | bytes 393232
  535.5 8.3 collective-permute-done.4
  608.7 50.1 %collective-permute-done.62 = bf16[192,1024]{1,0:T(8,128)(2,1)S(1)} collective-permute-done((bf16[192,1024]{1,0:T(8,128)(2,1)}, bf16[192,1024]{1,0:T(8,128)(2,1)S(1)}, u32[]{:S(2)}, u32[]{:S(2)}) %collective-permute-start.62) | collective-permute-done | bytes 393248 | tf_op jit(solution)/shard_map/ppermute | solution.py:34
  660.3 6.9 collective-permute-done.64
  681.3 12.3 %collective-permute-done.61 = bf16[192,1024]{1,0:T(8,128)(2,1)S(1)} collective-permute-done((bf16[192,1024]{1,0:T(8,128)(2,1)S(1)}, bf16[192,1024]{1,0:T(8,128)(2,1)S(1)}, u32[]{:S(2)}, u32[]{:S(2)}) %collective-permute-start.61) | collective-permute-done | bytes 393248 | tf_op jit(solution)/shard_map/ppermute | solution.py:34
  693.7 7.8 collective-permute-done.63
  707.4 8.2 multiply_convert_fusion.1
  727.0 33.6 %collective-permute-done.56 = bf16[192,2048]{1,0:T(8,128)(2,1)} collective-permute-done((bf16[192,2048]{1,0:T(8,128)(2,1)}, bf16[192,2048]{1,0:T(8,128)(2,1)}, u32[]{:S(2)}, u32[]{:S(2)}) %collective-permute-start.56) | collective-permute-done | bytes 786464 | tf_op jit(solution)/shard_map/ppermute | solution.py:34
  764.8 14.7 %collective-permute-start.47 = (bf16[192,384]{1,0:T(8,128)(2,1)S(1)}, bf16[192,384]{1,0:T(8,128)(2,1)S(1)}, u32[]{:S(2)}, u32[]{:S(2)}) collective-permute-start(bf16[192,384]{1,0:T(8,128)(2,1)S(1)} %get-tuple-element.155), channel_id=1, source_target_pairs={{0,8},{4,12},{8,0},{12,4},{16,24},{20,28},{24,16},{28,20},{1,9},{5... | collective-permute-start | bytes 442376 | tf_op jit(solution)/shard_map/ppermute | solution.py:34
  794.3 6.3 collective-permute-done.41
  848.2 7.0 collective-permute-done.36
  858.1 13.9 %collective-permute-done.25 = bf16[192,2048]{1,0:T(8,128)(2,1)S(1)} collective-permute-done((bf16[192,2048]{1,0:T(8,128)(2,1)S(1)}, bf16[192,2048]{1,0:T(8,128)(2,1)S(1)}, u32[]{:S(2)}, u32[]{:S(2)}) %collective-permute-start.25) | collective-permute-done | bytes 786464 | tf_op jit(solution)/shard_map/ppermute | solution.py:34
  872.0 16.8 %collective-permute-done.27 = bf16[192,2048]{1,0:T(8,128)(2,1)S(1)} collective-permute-done((bf16[192,2048]{1,0:T(8,128)(2,1)S(1)}, bf16[192,2048]{1,0:T(8,128)(2,1)S(1)}, u32[]{:S(2)}, u32[]{:S(2)}) %collective-permute-start.27) | collective-permute-done | bytes 786464 | tf_op jit(solution)/shard_map/ppermute | solution.py:34
  888.9 16.8 %collective-permute-done.29 = bf16[192,2048]{1,0:T(8,128)(2,1)S(1)} collective-permute-done((bf16[192,2048]{1,0:T(8,128)(2,1)S(1)}, bf16[192,2048]{1,0:T(8,128)(2,1)S(1)}, u32[]{:S(2)}, u32[]{:S(2)}) %collective-permute-start.29) | collective-permute-done | bytes 786464 | tf_op jit(solution)/shard_map/ppermute | solution.py:34
  922.5 6.7 fusion.101
  979.5 15.4 %collective-permute-start.19 = (bf16[192,384]{1,0:T(8,128)(2,1)S(1)}, bf16[192,384]{1,0:T(8,128)(2,1)S(1)}, u32[]{:S(2)}, u32[]{:S(2)}) collective-permute-start(bf16[192,384]{1,0:T(8,128)(2,1)S(1)} %get-tuple-element.162), channel_id=1, source_target_pairs={{0,8},{4,12},{8,0},{12,4},{16,24},{20,28},{24,16},{28,20},{1,9},{5... | collective-permute-start | bytes 442376 | tf_op jit(solution)/shard_map/ppermute | solution.py:34
  1009.7 6.3 collective-permute-done.13
  1034.6 8.3 collective-permute-done.14
  1050.0 8.5 collective-permute-start.7
  1062.7 20.8 %psum.39 = f32[4,384]{1,0:T(4,128)S(1)} all-reduce(f32[4,384]{1,0:T(4,128)S(1)} %pad_maximum_fusion.19), channel_id=1, replica_groups=mesh['wide'=8,'narrow'=4] {'wide'}, use_global_device_ids=true, to_apply=%region_22.23 | all-reduce | flops 1536 | bytes 12288 | tf_op jit(solution)/shard_map/psum | solution.py:847
  (513 shorter events, 369.4 us)
Async XLA Ops:
  7.2 436.2 %all-gather.5.cloned.1.call-start = ((), (), s32[]{:S(2)}) async-start(), calls=%async_computation.4 | async-start | bytes 1966080 | tf_op jit(solution)/shard_map/all_gather | solution.py:213
  417.2 70.5 %reduce-scatter.13.cloned.1.call-start = ((), (), s32[]{:S(2)}) async-start(), calls=%async_computation.8 | async-start | bytes 1966080
  459.4 51.6 %all-gather.7.cloned.1.call-start = ((), (), s32[]{:S(2)}) async-start(), calls=%async_computation.5 | async-start | bytes 1966080 | tf_op jit(solution)/shard_map/all_gather | solution.py:231
  491.2 100.5 %reduce-scatter.15.cloned.1.call-start = ((), (), s32[]{:S(2)}) async-start(), calls=%async_computation.9 | async-start | bytes 1966080
  550.1 157.3 %all-gather.9.cloned.1.call-start = ((), (), s32[]{:S(2)}) async-start(), calls=%async_computation.6 | async-start | bytes 1966080 | tf_op jit(solution)/shard_map/all_gather | solution.py:213
  595.6 228.8 %reduce-scatter.17.cloned.1.call-start = ((), (), s32[]{:S(2)}) async-start(), calls=%async_computation.10 | async-start | bytes 1966080
  595.9 74.3 %collective-permute-start.53 = (bf16[192,2048]{1,0:T(8,128)(2,1)}, bf16[192,2048]{1,0:T(8,128)(2,1)}, u32[]{:S(2)}, u32[]{:S(2)}) collective-permute-start(bf16[192,2048]{1,0:T(8,128)(2,1)} %get-tuple-element.85), channel_id=1, source_target_pairs={{0,4},{4,0},{8,12},{12,8},{16,20},{20,16},{24,28},{28,24},{1,5},{5... | collective-permute-start | bytes 2359304 | tf_op jit(solution)/shard_map/ppermute | solution.py:34
  597.5 75.9 %collective-permute-start.55 = (bf16[192,2048]{1,0:T(8,128)(2,1)}, bf16[192,2048]{1,0:T(8,128)(2,1)}, u32[]{:S(2)}, u32[]{:S(2)}) collective-permute-start(bf16[192,2048]{1,0:T(8,128)(2,1)} %get-tuple-element.84), channel_id=1, source_target_pairs={{0,4},{4,0},{8,12},{12,8},{16,20},{20,16},{24,28},{28,24},{1,5},{5... | collective-permute-start | bytes 2359304 | tf_op jit(solution)/shard_map/ppermute | solution.py:34
  598.0 75.4 %collective-permute-start.57 = (bf16[192,2048]{1,0:T(8,128)(2,1)}, bf16[192,2048]{1,0:T(8,128)(2,1)}, u32[]{:S(2)}, u32[]{:S(2)}) collective-permute-start(bf16[192,2048]{1,0:T(8,128)(2,1)} %get-tuple-element.83), channel_id=1, source_target_pairs={{0,4},{4,0},{8,12},{12,8},{16,20},{20,16},{24,28},{28,24},{1,5},{5... | collective-permute-start | bytes 2359304 | tf_op jit(solution)/shard_map/ppermute | solution.py:34
  604.2 54.6 %collective-permute-start.62 = (bf16[192,1024]{1,0:T(8,128)(2,1)}, bf16[192,1024]{1,0:T(8,128)(2,1)S(1)}, u32[]{:S(2)}, u32[]{:S(2)}) collective-permute-start(bf16[192,1024]{1,0:T(8,128)(2,1)} %get-tuple-element.119), channel_id=1, source_target_pairs={{0,4},{4,0},{8,12},{12,8},{16,20},{20,16},{24,28},{28,24},{1,5},{5... | collective-permute-start | bytes 1179656 | tf_op jit(solution)/shard_map/ppermute | solution.py:34
  604.8 62.4 %collective-permute-start.64 = (bf16[192,1024]{1,0:T(8,128)(2,1)S(1)}, bf16[192,1024]{1,0:T(8,128)(2,1)S(1)}, u32[]{:S(2)}, u32[]{:S(2)}) collective-permute-start(bf16[192,1024]{1,0:T(8,128)(2,1)S(1)} %copy-done.67), channel_id=1, source_target_pairs={{0,4},{4,0},{8,12},{12,8},{16,20},{20,16},{24,28},{28,24},{1,5},{5... | collective-permute-start | bytes 1179656 | tf_op jit(solution)/shard_map/ppermute | solution.py:34
  667.2 57.5 %collective-permute-start.52 = (bf16[192,2048]{1,0:T(8,128)(2,1)}, bf16[192,2048]{1,0:T(8,128)(2,1)S(1)}, u32[]{:S(2)}, u32[]{:S(2)}) collective-permute-start(bf16[192,2048]{1,0:T(8,128)(2,1)} %get-tuple-element.82), channel_id=1, source_target_pairs={{0,4},{4,0},{8,12},{12,8},{16,20},{20,16},{24,28},{28,24},{1,5},{5... | collective-permute-start | bytes 2359304 | tf_op jit(solution)/shard_map/ppermute | solution.py:34
  693.7 66.9 %collective-permute-start.56 = (bf16[192,2048]{1,0:T(8,128)(2,1)}, bf16[192,2048]{1,0:T(8,128)(2,1)}, u32[]{:S(2)}, u32[]{:S(2)}) collective-permute-start(bf16[192,2048]{1,0:T(8,128)(2,1)} %get-tuple-element.88), channel_id=1, source_target_pairs={{0,16},{4,20},{8,24},{12,28},{16,0},{20,4},{24,8},{28,12},{1,17},{... | collective-permute-start | bytes 2359304 | tf_op jit(solution)/shard_map/ppermute | solution.py:34
  701.4 59.1 %collective-permute-start.58 = (bf16[192,2048]{1,0:T(8,128)(2,1)}, bf16[192,2048]{1,0:T(8,128)(2,1)}, u32[]{:S(2)}, u32[]{:S(2)}) collective-permute-start(bf16[192,2048]{1,0:T(8,128)(2,1)} %get-tuple-element.87), channel_id=1, source_target_pairs={{0,24},{4,28},{8,16},{12,20},{16,8},{20,12},{24,0},{28,4},{1,25},{... | collective-permute-start | bytes 2359304 | tf_op jit(solution)/shard_map/ppermute | solution.py:34
  705.6 58.2 %collective-permute-start.46 = (bf16[192,384]{1,0:T(8,128)(2,1)}, bf16[192,384]{1,0:T(8,128)(2,1)}, u32[]{:S(2)}, u32[]{:S(2)}) collective-permute-start(bf16[192,384]{1,0:T(8,128)(2,1)} %get-tuple-element.154), channel_id=1, source_target_pairs={{0,4},{4,0},{8,12},{12,8},{16,20},{20,16},{24,28},{28,24},{1,5},{5... | collective-permute-start | bytes 442376 | tf_op jit(solution)/shard_map/ppermute | solution.py:34
  724.2 195.5 %all-gather.11.cloned.1.call-start = ((), (), s32[]{:S(2)}) async-start(), calls=%async_computation.7 | async-start | bytes 1966080 | tf_op jit(solution)/shard_map/all_gather | solution.py:231
  827.8 217.7 %reduce-scatter.19.cloned.1.call-start = ((), (), s32[]{:S(2)}) async-start(), calls=%async_computation.11 | async-start | bytes 1966080
  838.2 50.7 %collective-permute-start.27 = (bf16[192,2048]{1,0:T(8,128)(2,1)S(1)}, bf16[192,2048]{1,0:T(8,128)(2,1)S(1)}, u32[]{:S(2)}, u32[]{:S(2)}) collective-permute-start(bf16[192,2048]{1,0:T(8,128)(2,1)S(1)} %get-tuple-element.107), channel_id=1, source_target_pairs={{0,4},{4,0},{8,12},{12,8},{16,20},{20,16},{24,28},{28,24},{1,5},{5... | collective-permute-start | bytes 2359304 | tf_op jit(solution)/shard_map/ppermute | solution.py:34
  838.7 67.0 %collective-permute-start.29 = (bf16[192,2048]{1,0:T(8,128)(2,1)S(1)}, bf16[192,2048]{1,0:T(8,128)(2,1)S(1)}, u32[]{:S(2)}, u32[]{:S(2)}) collective-permute-start(bf16[192,2048]{1,0:T(8,128)(2,1)S(1)} %get-tuple-element.106), channel_id=1, source_target_pairs={{0,4},{4,0},{8,12},{12,8},{16,20},{20,16},{24,28},{28,24},{1,5},{5... | collective-permute-start | bytes 2359304 | tf_op jit(solution)/shard_map/ppermute | solution.py:34
  846.7 67.4 %collective-permute-start.31 = (bf16[192,1024]{1,0:T(8,128)(2,1)S(1)}, bf16[192,1024]{1,0:T(8,128)(2,1)S(1)}, u32[]{:S(2)}, u32[]{:S(2)}) collective-permute-start(bf16[192,1024]{1,0:T(8,128)(2,1)S(1)} %copy-done.68), channel_id=1, source_target_pairs={{0,4},{4,0},{8,12},{12,8},{16,20},{20,16},{24,28},{28,24},{1,5},{5... | collective-permute-start | bytes 1179656 | tf_op jit(solution)/shard_map/ppermute | solution.py:34
  855.2 112.1 %collective-permute-start.24 = (bf16[192,2048]{1,0:T(8,128)(2,1)}, bf16[192,2048]{1,0:T(8,128)(2,1)}, u32[]{:S(2)}, u32[]{:S(2)}) collective-permute-start(bf16[192,2048]{1,0:T(8,128)(2,1)} %get-tuple-element.105), channel_id=1, source_target_pairs={{0,4},{4,0},{8,12},{12,8},{16,20},{20,16},{24,28},{28,24},{1,5},{5... | collective-permute-start | bytes 2359304 | tf_op jit(solution)/shard_map/ppermute | solution.py:34
  914.1 53.7 %collective-permute-start.26 = (bf16[192,2048]{1,0:T(8,128)(2,1)}, bf16[192,2048]{1,0:T(8,128)(2,1)}, u32[]{:S(2)}, u32[]{:S(2)}) collective-permute-start(bf16[192,2048]{1,0:T(8,128)(2,1)} %get-tuple-element.109), channel_id=1, source_target_pairs={{0,8},{4,12},{8,0},{12,4},{16,24},{20,28},{24,16},{28,20},{1,9},{5... | collective-permute-start | bytes 2359304 | tf_op jit(solution)/shard_map/ppermute | solution.py:34
  914.1 60.7 %collective-permute-start.28 = (bf16[192,2048]{1,0:T(8,128)(2,1)}, bf16[192,2048]{1,0:T(8,128)(2,1)}, u32[]{:S(2)}, u32[]{:S(2)}) collective-permute-start(bf16[192,2048]{1,0:T(8,128)(2,1)} %get-tuple-element.111), channel_id=1, source_target_pairs={{0,16},{4,20},{8,24},{12,28},{16,0},{20,4},{24,8},{28,12},{1,17},{... | collective-permute-start | bytes 2359304 | tf_op jit(solution)/shard_map/ppermute | solution.py:34
  916.1 58.7 %collective-permute-start.30 = (bf16[192,2048]{1,0:T(8,128)(2,1)}, bf16[192,2048]{1,0:T(8,128)(2,1)}, u32[]{:S(2)}, u32[]{:S(2)}) collective-permute-start(bf16[192,2048]{1,0:T(8,128)(2,1)} %get-tuple-element.110), channel_id=1, source_target_pairs={{0,24},{4,28},{8,16},{12,20},{16,8},{20,12},{24,0},{28,4},{1,25},{... | collective-permute-start | bytes 2359304 | tf_op jit(solution)/shard_map/ppermute | solution.py:34
  (154 other events, 2719.8 us)
Sparse Core Ops, SparseCore 0:
  417.3 25.9 all-gather.4
  459.6 28.1 reduce-scatter.12
  491.4 19.6 all-gather.6
  550.2 28.1 reduce-scatter.14
  595.7 19.4 all-gather.8
  724.4 34.3 reduce-scatter.16
  827.9 17.6 all-gather.10
  964.7 31.7 reduce-scatter.18

commit v3 on v2

--- a/solution.py
+++ b/solution.py
@@ -25,238 +25,12 @@
     return lax.dot_general(left, right, (((1,), (1,)), ((), ())), preferred_element_type=F32)
 
 
-def dot_first(left, right):
-    return lax.dot_general(left, right, (((0,), (0,)), ((), ())), preferred_element_type=F32)
-
-
-def exchange(x, distance):
-    count = lax.axis_size("wide")
-    return lax.ppermute(x, "wide", [(w, w ^ distance) for w in range(count)])
-
-
 def bits_below(count):
     found, bit = [], 1
     while bit < count:
         found.append(bit)
         bit *= 2
     return found
-
-
-def gather_blocks(block):
-    count = lax.axis_size("wide")
-    inner = count // OUTER
-    blocks = {0: block}
-    for outer in range(1, OUTER):
-        blocks[outer * inner] = exchange(block, outer * inner)
-    for bit in bits_below(inner):
-        for j in sorted(blocks):
-            blocks[j + bit] = exchange(blocks[j], bit)
-    return [blocks[j] for j in range(count)]
-
-
-def natural(blocks):
-    stacked = jnp.stack(blocks)
-    count = stacked.shape[0]
-    me = lax.axis_index("wide")
-    picked = [lax.dynamic_index_in_dim(stacked, k ^ me, 0, keepdims=False) for k in range(count)]
-    return jnp.concatenate(picked, axis=0)
-
-
-def reduce_blocks(gradient):
-    count = lax.axis_size("wide")
-    inner = count // OUTER
-    me = lax.axis_index("wide")
-    split = gradient.reshape(count, gradient.shape[0] // count, gradient.shape[1])
-    blocks = {j: lax.dynamic_index_in_dim(split, me ^ j, 0, keepdims=False) for j in range(count)}
-    for bit in reversed(bits_below(inner)):
-        moved = {}
-        for j in sorted(blocks):
-            if j % (2 * bit) < bit:
-                got = exchange(blocks[j + bit], bit)
-                moved[j] = (blocks[j].astype(F32) + got.astype(F32)).astype(BF)
-        blocks = moved
-    total = blocks[0].astype(F32)
-    for outer in range(1, OUTER):
-        total = total + exchange(blocks[outer * inner], outer * inner).astype(F32)
-    return total
-
-
-def spread_tokens(x):
-    batches = x.shape[0]
-    count = lax.axis_size("wide")
-    group = count // batches
-    me = lax.axis_index("wide")
-    rank = me % batches
-    own = me // group
-    parts = []
-    for j in range(batches):
-        piece = lax.dynamic_index_in_dim(x, (rank + j) % batches, 0, keepdims=False)
-        pairs = [
-            (w, ((w % batches + j) % batches) * group + w // batches) for w in range(count)
-        ]
-        parts.append(lax.ppermute(piece, "wide", pairs))
-    stacked = jnp.stack(parts)
-    picked = [
-        lax.dynamic_index_in_dim(stacked, (own - r) % batches, 0, keepdims=False)
-        for r in range(batches)
-    ]
-    return jnp.stack(picked)
-
-
-def collect_tokens(x):
-    batches = x.shape[0]
-    count = lax.axis_size("wide")
-    group = count // batches
-    me = lax.axis_index("wide")
-    rank = me % batches
-    own = me // group
-    parts = []
-    for j in range(batches):
-        piece = lax.dynamic_index_in_dim(x, (own - j) % batches, 0, keepdims=False)
-        pairs = [
-            (((w % batches + j) % batches) * group + w // batches, w) for w in range(count)
-        ]
-        parts.append(lax.ppermute(piece, "wide", pairs))
-    stacked = jnp.stack(parts)
-    picked = [
-        lax.dynamic_index_in_dim(stacked, (b - rank) % batches, 0, keepdims=False)
-        for b in range(batches)
-    ]
-    return jnp.stack(picked)
-
-
-def rotate(values, cosine, sine, heads):
-    rows = values.shape[0]
-    split = values.reshape(rows, heads, 2, HEAD_DIM // 2)
-    u, w = split[:, :, 0], split[:, :, 1]
-    c, s = cosine[:, None, :], sine[:, None, :]
-    return jnp.stack([u * c - w * s, w * c + u * s], axis=2).reshape(rows, -1)
-
-
-def normed(x, gain, gain_full):
-    gathered = lax.all_gather((x * gain).astype(BF), "narrow", axis=1, tiled=True)
-    plain = gathered.astype(F32) / gain_full
-    inverse = lax.rsqrt(jnp.mean(plain * plain, axis=1, keepdims=True) + EPSILON)
-    return gathered, inverse
-
-
-def scatter_narrow(partial_sum):
-    return lax.psum_scatter(
-        partial_sum.astype(BF), "narrow", scatter_dimension=1, tiled=True
-    ).astype(F32)
-
-
-def group_gather(x, group):
-    blocks = [x] + [exchange(x, d) for d in range(1, group)]
-    stacked = jnp.stack(blocks)
-    me = lax.axis_index("wide") % group
-    return jnp.concatenate(
-        [lax.dynamic_index_in_dim(stacked, k ^ me, 0, keepdims=False) for k in range(group)], axis=0
-    )
-
-
-def group_reduce(x, group):
-    me = lax.axis_index("wide") % group
-    split = x.reshape(group, x.shape[0] // group, x.shape[1])
-    total = lax.dynamic_index_in_dim(split, me, 0, keepdims=False)
-    for d in range(1, group):
-        piece = lax.dynamic_index_in_dim(split, me ^ d, 0, keepdims=False)
-        total = total + exchange(piece.astype(BF), d).astype(F32)
-    return total
-
-
-def attention_forward(x, gain, gain_full, w_qkv, w_out, setup):
-    cosine, sine, causal, group = setup
-    rows = x.shape[0]
-    heads = w_out.shape[1] // HEAD_DIM
-    kv = (w_qkv.shape[1] - w_out.shape[1]) // 2 // HEAD_DIM
-    gathered, inverse = normed(x, gain, gain_full)
-    raw = dot(gathered, w_qkv) * inverse
-    cut = heads * HEAD_DIM
-    q = rotate(raw[:, :cut], cosine, sine, heads).astype(BF)
-    k = rotate(raw[:, cut : cut + kv * HEAD_DIM], cosine, sine, kv).astype(BF)
-    v = raw[:, cut + kv * HEAD_DIM :].astype(BF)
-    kv_all = group_gather(jnp.concatenate([k, v], axis=1), group)
-    length = kv_all.shape[0]
-    kh = kv_all[:, : kv * HEAD_DIM].reshape(length, kv, HEAD_DIM)
-    vh = kv_all[:, kv * HEAD_DIM :].reshape(length, kv, HEAD_DIM)
-    qh = q.reshape(rows, kv, heads // kv, HEAD_DIM)
-    s = jnp.einsum("sgrd,lgd->grsl", qh, kh, preferred_element_type=F32) * SCALE
-    s = jnp.where(causal, s, NEGATIVE)
-    top = jnp.max(s, axis=-1, keepdims=True)
-    lse = top + jnp.log(jnp.sum(jnp.exp(s - top), axis=-1, keepdims=True))
-    p = jnp.exp(s - lse).astype(BF)
-    o = jnp.einsum("grsl,lgd->sgrd", p, vh, preferred_element_type=F32).reshape(rows, -1).astype(BF)
-    h = x + scatter_narrow(dot_last(o, w_out))
-    return h, (x, gathered, inverse, q, k, v, kv_all, lse, o)
-
-
-def feed_forward(h, gain, gain_full, w_gu, w_down):
-    gathered, inverse = normed(h, gain, gain_full)
-    raw = dot(gathered, w_gu) * inverse
-    half = raw.shape[1] // 2
-    g, u = raw[:, :half], raw[:, half:]
-    c = (g * jax.nn.sigmoid(g) * u).astype(BF)
-    y = h + scatter_narrow(dot_last(c, w_down))
-    return y, (h, gathered, inverse, g, u, c)
-
-
-def back_norm(back, total, x, inverse, gain, dots):
-    width = x.shape[1] * lax.axis_size("narrow")
-    dots = lax.psum(dots, "narrow")
-    result = back + total * gain - x * (inverse * inverse * dots / width)
-    return result, jnp.sum(total * x, axis=0)
-
-
-def feed_backward(dy, saved, gain, w_gu, w_down):
-    h, gathered, inverse, g, u, c = saved
-    low = lax.all_gather(dy.astype(BF), "narrow", axis=1, tiled=True)
-    dc = dot(low, w_down)
-    s = jax.nn.sigmoid(g)
-    dg = dc * u * s * (1.0 + g * (1.0 - s))
-    du = dc * g * s
-    dots = jnp.sum(dg * g + du * u, axis=1, keepdims=True)
-    scaled = jnp.concatenate([dg * inverse, du * inverse], axis=1).astype(BF)
-    total = scatter_narrow(dot_last(scaled, w_gu))
-    dh, dgain = back_norm(dy, total, h, inverse, gain, dots)
-    return dh, dgain, dot_first(gathered, scaled).astype(BF), dot_first(low, c).astype(BF)
-
-
-def attention_backward(dh, saved, gain, w_qkv, w_out, setup):
-    cosine, sine, causal, group = setup
-    x, gathered, inverse, q, k, v, kv_all, lse, o = saved
-    rows = x.shape[0]
-    heads = w_out.shape[1] // HEAD_DIM
-    kv = k.shape[1] // HEAD_DIM
-    low = lax.all_gather(dh.astype(BF), "narrow", axis=1, tiled=True)
-    do = dot(low, w_out).astype(BF)
-    length = kv_all.shape[0]
-    kh = kv_all[:, : kv * HEAD_DIM].reshape(length, kv, HEAD_DIM)
-    vh = kv_all[:, kv * HEAD_DIM :].reshape(length, kv, HEAD_DIM)
-    qh = q.reshape(rows, kv, heads // kv, HEAD_DIM)
-    doh = do.reshape(rows, kv, heads // kv, HEAD_DIM)
-    s = jnp.einsum("sgrd,lgd->grsl", qh, kh, preferred_element_type=F32) * SCALE
-    s = jnp.where(causal, s, NEGATIVE)
-    p = jnp.exp(s - lse)
-    dp = jnp.einsum("sgrd,lgd->grsl", doh, vh, preferred_element_type=F32)
-    ds = (p * (dp - jnp.sum(p * dp, axis=-1, keepdims=True))).astype(BF)
-    dq = jnp.einsum("grsl,lgd->sgrd", ds, kh, preferred_element_type=F32).reshape(rows, -1) * SCALE
-    dk = jnp.einsum("grsl,sgrd->lgd", ds, qh, preferred_element_type=F32).reshape(length, -1) * SCALE
-    dv = jnp.einsum("grsl,sgrd->lgd", p.astype(BF), doh, preferred_element_type=F32)
-    dkv = group_reduce(jnp.concatenate([dk, dv.reshape(length, -1)], axis=1), group)
-    dk, dv = dkv[:, : kv * HEAD_DIM], dkv[:, kv * HEAD_DIM :]
-    dots = (
-        jnp.sum(dq * q.astype(F32), axis=1, keepdims=True)
-        + jnp.sum(dk * k.astype(F32), axis=1, keepdims=True)
-        + jnp.sum(dv * v.astype(F32), axis=1, keepdims=True)
-    )
-    raw = jnp.concatenate(
-        [rotate(dq, cosine, -sine, heads), rotate(dk, cosine, -sine, kv), dv], axis=1
-    )
-    scaled = (raw * inverse).astype(BF)
-    total = scatter_narrow(dot_last(scaled, w_qkv))
-    dx, dgain = back_norm(dh, total, x, inverse, gain, dots)
-    return dx, dgain, dot_first(gathered, scaled).astype(BF), dot_first(low, o).astype(BF)
 
 
 MESH = pl.DeviceIdType.MESH
@@ -765,22 +539,657 @@
     )(tokens, cotangent, gains, cosine, sine, select, *packs)
 
 
+def dot_rows(left, right):
+    return lax.dot_general(left, right, (((0,), (0,)), ((), ())), preferred_element_type=F32)
+
+
+ORDER = (DOWN, GATE, UP, OUT, QKV)
+
+
+def backward_kernel(
+    count,
+    gains, cosine, sine, select,
+    a_qkv, a_out, a_gate, a_up, a_down,
+    i_xall, i_resid, i_rinv, i_q, i_kv, i_mix, i_g, i_u, i_c, i_dy,
+    g_qkv, g_out, g_gate, g_up, g_down, o_y, o_dx, o_gain,
+    d_qkv, d_out, d_gate, d_up, d_down,
+    x_qkv, x_out, x_gate, x_up, x_down,
+    z_qkv, z_out, z_gate, z_up, z_down, o_kin,
+    w_gate, w_up, w_down, xmid, xmix, resid, rinv, gst, ust, cst, dus, low, turned, qpad, kvpad, mix,
+    dcur, own, stage, crecv, yrecv, dopad, dqpad, dkv, ksend_buf, scaled, piece, have, got, final,
+    dots, gsum, gall,
+    load, agsend, agrecv, rsend, rrecv, msend, mrecv, ksend, krecv,
+    xsend, xrecv, zsend, zrecv, local, ysend, yrec, txsend, txrecv, gsend, grecv,
+):
+    me, n = lax.axis_index("wide"), lax.axis_index("narrow")
+    wide = Wide(count)
+    inner = wide.inner
+    batches, s_dev, width = i_dy.shape
+    rows = batches * s_dev
+    group = count // batches
+    weights = (a_qkv, a_out, a_gate, a_up, a_down)
+    results = (g_qkv, g_out, g_gate, g_up, g_down)
+    grads = (d_qkv, d_out, d_gate, d_up, d_down)
+    xins = (x_qkv, x_out, x_gate, x_up, x_down)
+    zins = (z_qkv, z_out, z_gate, z_up, z_down)
+    kr = g_qkv.shape[1]
+    heads = qpad.shape[1] // 128
+    kv = kvpad.shape[1] // 256
+    length = kvpad.shape[0]
+    ff = cst.shape[1]
+    cut = heads * HEAD_DIM
+    kv_cut = kv * HEAD_DIM
+    core, other, cross = flip(n, 1), flip(n, 2), flip(n, 3)
+    mine = me % group
+    enter(count, me, n)
+
+    def loads(l):
+        a = 2 * l
+        return {
+            "down": (a_down.at[l], w_down), "gate": (a_gate.at[l], w_gate), "up": (a_up.at[l], w_up),
+            "xmid": (i_xall.at[a + 1], xmid), "xmix": (i_xall.at[a], xmix),
+            "res1": (i_resid.at[a + 1], resid.at[1]), "res0": (i_resid.at[a], resid.at[0]),
+            "inv1": (i_rinv.at[a + 1], rinv.at[1]), "inv0": (i_rinv.at[a], rinv.at[0]),
+            "g": (i_g.at[l], gst), "u": (i_u.at[l], ust), "c": (i_c.at[l], cst),
+            "q": (i_q.at[l], qpad), "kv": (i_kv.at[l], kvpad), "mix": (i_mix.at[l], mix),
+            "qkv": (a_qkv.at[l], w_down.at[:, : a_qkv.shape[2]]),
+            "out": (a_out.at[l], w_gate.at[:, : a_out.shape[2]]),
+        }
+
+    names = list(loads(0))
+
+    def load_of(l, name):
+        src, dst = loads(l)[name]
+        return pltpu.make_async_copy(src, dst, load.at[names.index(name)])
+
+    def fetch(l, *wanted):
+        for name in wanted:
+            load_of(l, name).start()
+
+    def ready(l, *wanted):
+        for name in wanted:
+            load_of(l, name).wait()
+
+    def collect(source, target, send, recv, phase):
+        for r in range(batches):
+            to = mine * batches + r
+            part = source.at[pl.ds(r * s_dev, s_dev)]
+
+            @pl.when(to != me)
+            def _():
+                if phase == 0:
+                    remote(part, target.at[me // group], send.at[r], recv.at[me // group], (to, n)).start()
+                elif phase == 2:
+                    remote(part, target.at[0], send.at[r], recv.at[0], (to, n)).wait_send()
+
+            if phase == 0:
+
+                @pl.when(to == me)
+                def _():
+                    pltpu.make_async_copy(part, target.at[me // group], recv.at[me // group]).start()
+
+        if phase == 1:
+            for b in range(batches):
+                origin = b * group + me // batches
+                part = source.at[pl.ds(0, s_dev)]
+
+                @pl.when(origin != me)
+                def _():
+                    remote(part, target.at[b], send.at[0], recv.at[b], (origin, n)).wait_recv()
+
+                @pl.when(origin == me)
+                def _():
+                    pltpu.make_async_copy(part, target.at[b], recv.at[b]).wait()
+
+    def ag(k):
+        def own_copy(dist):
+            ref = low.at[k, n]
+            return remote(ref, ref, agsend.at[k, dist], agrecv.at[k, dist], (me, flip(n, dist)))
+
+        def into(dist):
+            ref = low.at[k, flip(n, dist)]
+            return remote(ref, ref, agsend.at[k, dist], agrecv.at[k, dist], (me, flip(n, dist)))
+
+        def body(r):
+            low[k, n, r] = dcur[r].astype(BF)
+
+        each_tile(rows, 128, body)
+        own_copy(2).start()
+        own_copy(1).start()
+        into(2).wait_recv()
+        ref = low.at[k, other]
+        passed = remote(ref, ref, agsend.at[k, 3], agrecv.at[k, 3], (me, core))
+        passed.start()
+        into(1).wait_recv()
+        ref = low.at[k, cross]
+        remote(ref, ref, agsend.at[k, 3], agrecv.at[k, 3], (me, core)).wait_recv()
+        own_copy(2).wait_send()
+        own_copy(1).wait_send()
+        passed.wait_send()
+
+    def turn(ref):
+        for s in range(4):
+            turned[s * width : (s + 1) * width] = ref[s].T
+
+    def dots_copy(k, dist, incoming):
+        ref = dots.at[k, flip(n, dist) if incoming else n]
+        return remote(ref, ref, msend.at[k, dist], mrecv.at[k, dist], (me, flip(n, dist)))
+
+    def row_sums(product):
+        ones = jnp.ones((8, product.shape[1]), BF)
+        high = product.astype(BF)
+        rest = (product - high.astype(F32)).astype(BF)
+        return dot_last(ones, high) + dot_last(ones, rest)
+
+    def rs_core(k, j):
+        return remote(stage.at[j], crecv.at[k, j], rsend.at[k, j], rrecv.at[k, j], (me, core))
+
+    def rs_other(k):
+        return remote(stage.at[2], yrecv.at[k], rsend.at[k, 2], rrecv.at[k, 2], (me, other))
+
+    def reduce_narrow(k, a, product):
+        for d in (1, 2, 3):
+            dots_copy(k, d, False).start()
+        for j, b in ((1, cross), (0, core)):
+
+            def body(r, j=j, b=b):
+                stage[j, r] = product(b, r).astype(BF)
+
+            each_tile(rows, TILE, body)
+            rs_core(k, j).start()
+
+        def body_other(r):
+            own[r] = product(other, r)
+
+        each_tile(rows, TILE, body_other)
+        rs_core(k, 1).wait_recv()
+
+        def add_other(r):
+            stage[2, r] = (own[r] + crecv[k, 1, r].astype(F32)).astype(BF)
+
+        each_tile(rows, 128, add_other)
+        rs_other(k).start()
+
+        def body_own(r):
+            own[r] = product(n, r)
+
+        each_tile(rows, TILE, body_own)
+        rs_core(k, 0).wait_recv()
+        for d in (1, 2, 3):
+            dots_copy(k, d, True).wait_recv()
+        rs_other(k).wait_recv()
+        gain = gains[pl.ds(a, 1), :]
+        gsum[pl.ds(a, 1), :] = jnp.zeros((1, width), F32)
+
+        def add_own(r):
+            total = own[r] + crecv[k, 0, r].astype(F32) + yrecv[k, r].astype(F32)
+            x = resid[1 - k, r]
+            m = (dots[k, 0, :, r] + dots[k, 1, :, r]) + (dots[k, 2, :, r] + dots[k, 3, :, r])
+            column = m.T[:, 0:1]
+            inverse = rinv[1 - k, r]
+            dcur[r] = dcur[r] + total * gain - x * (inverse * inverse * column * (1.0 / (4 * width)))
+            gsum[pl.ds(a, 1), :] += jnp.sum(total * x, axis=0, keepdims=True)
+
+        each_tile(rows, 128, add_own)
+        rs_core(k, 1).wait_send()
+        rs_core(k, 0).wait_send()
+        rs_other(k).wait_send()
+        for d in (1, 2, 3):
+            dots_copy(k, d, False).wait_send()
+
+    def fold_slot(bit, j):
+        base = sum(OUTER * b for b in wide.bits if b > bit)
+        return base + (j // inner) * bit + j % inner
+
+    def x_copy(l, c, bit, j):
+        slot = fold_slot(bit, j - bit)
+        return remote(
+            grads[c].at[l, rows_of(flip(me, j), kr)], xins[c].at[l, slot],
+            xsend.at[l * PIECES + c, slot], xrecv.at[l * PIECES + c, slot], (flip(me, bit), n),
+        )
+
+    def x_in(l, c, bit, j):
+        slot = fold_slot(bit, j)
+        ref = xins[c].at[l, slot]
+        return remote(
+            ref, ref, xsend.at[l * PIECES + c, slot], xrecv.at[l * PIECES + c, slot], (flip(me, bit), n)
+        )
+
+    def z_copy(l, c, o):
+        return remote(
+            grads[c].at[l, rows_of(flip(me, o * inner), kr)], zins[c].at[l, o - 1],
+            zsend.at[l * PIECES + c, o], zrecv.at[l * PIECES + c, o], (flip(me, o * inner), n),
+        )
+
+    def z_in(l, c, o):
+        ref = zins[c].at[l, o - 1]
+        return remote(
+            ref, ref, zsend.at[l * PIECES + c, o], zrecv.at[l * PIECES + c, o], (flip(me, o * inner), n)
+        )
+
+    def upper(bit):
+        return [j for j in range(count) if bit <= j % inner < 2 * bit]
+
+    def lower(bit):
+        return [j for j in range(count) if j % inner < bit]
+
+    falling = list(reversed(wide.bits))
+
+    def x_send(l, c):
+        for j in upper(falling[0]):
+            x_copy(l, c, falling[0], j).start()
+
+    def x_fold(l, c):
+        columns = grads[c].shape[2]
+        for at, bit in enumerate(falling):
+            blocks = lower(bit)
+            for j in blocks:
+                x_in(l, c, bit, j).wait_recv()
+            pairs = []
+            for i, j in enumerate(blocks):
+                block = grads[c].at[l, rows_of(flip(me, j), kr)]
+                mine_at = have.at[pl.ds(i * kr, kr), pl.ds(0, columns)]
+                theirs_at = got.at[pl.ds(i * kr, kr), pl.ds(0, columns)]
+                pairs.append((block, mine_at, theirs_at, xins[c].at[l, fold_slot(bit, j)]))
+            for i, (block, mine_at, theirs_at, arrived) in enumerate(pairs):
+                pltpu.make_async_copy(block, mine_at, local.at[0, i]).start()
+                pltpu.make_async_copy(arrived, theirs_at, local.at[1, i]).start()
+            for i, (block, mine_at, theirs_at, arrived) in enumerate(pairs):
+                pltpu.make_async_copy(block, mine_at, local.at[0, i]).wait()
+                pltpu.make_async_copy(arrived, theirs_at, local.at[1, i]).wait()
+
+            def body(r):
+                have[r, :columns] = (
+                    have[r, :columns].astype(F32) + got[r, :columns].astype(F32)
+                ).astype(BF)
+
+            each_tile(len(blocks) * kr, 64, body)
+            for i, (block, mine_at, theirs_at, arrived) in enumerate(pairs):
+                pltpu.make_async_copy(mine_at, block, local.at[0, i]).start()
+            for i, (block, mine_at, theirs_at, arrived) in enumerate(pairs):
+                pltpu.make_async_copy(mine_at, block, local.at[0, i]).wait()
+            if at + 1 < len(falling):
+                for j in upper(falling[at + 1]):
+                    x_copy(l, c, falling[at + 1], j).start()
+        for o in range(1, OUTER):
+            z_copy(l, c, o).start()
+
+    def z_finish(l, c):
+        columns = grads[c].shape[2]
+        for o in range(1, OUTER):
+            z_in(l, c, o).wait_recv()
+        moves = [(grads[c].at[l, rows_of(me, kr)], have.at[pl.ds(0, kr), pl.ds(0, columns)])]
+        for o in range(1, OUTER):
+            moves.append((zins[c].at[l, o - 1], got.at[pl.ds((o - 1) * kr, kr), pl.ds(0, columns)]))
+        for i, (src, dst) in enumerate(moves):
+            pltpu.make_async_copy(src, dst, local.at[0, i]).start()
+        for i, (src, dst) in enumerate(moves):
+            pltpu.make_async_copy(src, dst, local.at[0, i]).wait()
+
+        def body(i, carry):
+            r = pl.ds(pl.multiple_of(i * 16, 16), 16)
+            total = have[r, :columns].astype(F32)
+            for o in range(OUTER - 1):
+                at = pl.ds(pl.multiple_of(o * kr + i * 16, 16), 16)
+                total = total + got[at, :columns].astype(F32)
+            final[r, :columns] = total
+            return carry
+
+        lax.fori_loop(0, kr // 16, body, 0)
+        put = pltpu.make_async_copy(final.at[:, pl.ds(0, columns)], results[c].at[l], local.at[1, 0])
+        put.start()
+        put.wait()
+
+    def gradient(l, c, right, start, columns):
+        step = min(columns, TILE) if columns % TILE == 0 else 128
+
+        def put(s):
+            at = rows_of(s, width)
+            return pltpu.make_async_copy(
+                piece.at[at, pl.ds(0, columns)], grads[c].at[l, at], local.at[1, 0]
+            )
+
+        def body(s, carry):
+            def tile(j, carry):
+                lanes = pl.ds(pl.multiple_of(j * step, step), step)
+                piece[rows_of(s, width), lanes] = dot(
+                    turned[rows_of(s, width)], right(lanes)
+                ).astype(BF)
+                return carry
+
+            lax.fori_loop(0, columns // step, tile, 0)
+            put(s).start()
+            return carry
+
+        lax.fori_loop(0, 4, body, 0)
+        for s in range(4):
+            put(s).wait()
+        x_send(l, c)
+
+    fetch(1, *[name for name in names if name not in ("qkv", "out")])
+    collect(i_resid.at[4], o_y, ysend, yrec, 0)
+    for b in range(batches):
+        pltpu.make_async_copy(i_dy.at[b], low.at[1, 0, pl.ds(b * s_dev, s_dev)], local.at[0, b]).start()
+    for b in range(batches):
+        pltpu.make_async_copy(i_dy.at[b], low.at[1, 0, pl.ds(b * s_dev, s_dev)], local.at[0, b]).wait()
+
+    def widen(r):
+        dcur[r] = low[1, 0, r].astype(F32)
+
+    each_tile(rows, 128, widen)
+    gsum[...] = jnp.zeros_like(gsum)
+
+    tile_q = TILE if length <= 2048 else 128
+
+    def attention_back():
+        dqpad[...] = jnp.zeros_like(dqpad)
+
+        def per_kv(g, carry):
+            dkv[...] = jnp.zeros_like(dkv)
+            k_lanes, v_lanes = rows_of(g, 128), rows_of(kv + g, 128)
+
+            def step(i, carry):
+                h = g * (heads // kv) + i // (rows // tile_q)
+                part = i % (rows // tile_q)
+                r = rows_of(part, tile_q)
+                lanes = rows_of(h, 128)
+                k, v = kvpad[:, k_lanes], kvpad[:, v_lanes]
+                q, do = qpad[r, lanes], dopad[r, lanes]
+                s = dot_last(k, q) * SCALE
+                pos = mine * rows + part * tile_q + lax.broadcasted_iota(jnp.int32, s.shape, 1)
+                s = jnp.where(lax.broadcasted_iota(jnp.int32, s.shape, 0) <= pos, s, NEGATIVE)
+                e = jnp.exp(s - jnp.max(s, axis=0, keepdims=True))
+                p = e * (1.0 / jnp.sum(e, axis=0, keepdims=True))
+                dp = dot_last(v, do)
+                ds = (p * (dp - jnp.sum(p * dp, axis=0, keepdims=True))).astype(BF)
+                dqpad[r, lanes] = dot_rows(ds, k) * SCALE
+                dkv[:, :128] += dot(ds, q) * SCALE
+                dkv[:, 128:] += dot(p.astype(BF), do)
+                return carry
+
+            lax.fori_loop(0, (heads // kv) * (rows // tile_q), step, 0)
+            ksend_buf[:, k_lanes] = dkv[:, :128].astype(BF)
+            ksend_buf[:, v_lanes] = dkv[:, 128:].astype(BF)
+            return carry
+
+        lax.fori_loop(0, kv, per_kv, 0)
+
+    def k_copy(l, d):
+        return remote(
+            ksend_buf.at[rows_of(flip(mine, d), rows)], o_kin.at[l, d - 1],
+            ksend.at[l, d], krecv.at[l, d], (flip(me, d), n),
+        )
+
+    def k_in(l, d):
+        return remote(
+            o_kin.at[l, d - 1], o_kin.at[l, d - 1], ksend.at[l, d], krecv.at[l, d],
+            (flip(me, d), n),
+        )
+
+    def layer(step, carry):
+        l = 1 - step
+
+        @pl.when(l == 0)
+        def _():
+            fetch(0, *[name for name in names if name not in ("qkv", "out")])
+
+        ag(0)
+        turn(low.at[0])
+        ready(l, "c")
+        gradient(l, DOWN, lambda lanes: cst[:, lanes], 0, ff)
+
+        @pl.when(l == 0)
+        def _():
+            x_fold(1, UP)
+
+        ready(l, "down", "g", "u", "inv1")
+        dots[0, n] = jnp.zeros_like(dots[0, n])
+
+        def hidden(j, carry):
+            columns = rows_of(j, TILE)
+
+            def body(r):
+                dc = 0.0
+                for s in range(4):
+                    dc = dc + dot(low[0, s, r], w_down[s * width : (s + 1) * width, columns])
+                g, u = gst[r, columns], ust[r, columns]
+                sig = 1.0 / (1.0 + jnp.exp(-g))
+                dg = dc * u * sig * (1.0 + g * (1.0 - sig))
+                du = dc * g * sig
+                dots[0, n, :, r] += row_sums(dg * g + du * u)
+                inverse = rinv[1, r]
+                cst[r, columns] = (dg * inverse).astype(BF)
+                dus[r, columns] = (du * inverse).astype(BF)
+
+            each_tile(rows, TILE, body)
+            return carry
+
+        lax.fori_loop(0, ff // TILE, hidden, 0)
+        fetch(l, "qkv")
+        ready(l, "xmid", "gate", "up", "res1")
+        turn(xmid)
+        gradient(l, GATE, lambda lanes: cst[:, lanes], 0, ff)
+        reduce_narrow(
+            0,
+            2 * l + 1,
+            lambda b, r: dot_last(cst[r], w_gate[rows_of(b, width)])
+            + dot_last(dus[r], w_up[rows_of(b, width)]),
+        )
+        fetch(l, "out")
+        gradient(l, UP, lambda lanes: dus[:, lanes], 0, ff)
+
+        @pl.when(l == 0)
+        def _():
+            x_fold(1, OUT)
+            z_finish(1, GATE)
+
+        @pl.when(l == 1)
+        def _():
+            x_fold(1, DOWN)
+
+        ag(1)
+        ready(l, "mix", "q", "kv", "out", "inv0")
+        turn(low.at[1])
+        gradient(l, OUT, lambda lanes: mix[:, lanes], 0, cut)
+
+        def back_mix(r):
+            do = 0.0
+            for s in range(4):
+                do = do + dot(low[1, s, r], w_gate[s * width : (s + 1) * width, :cut])
+            dopad[r] = dot(do.astype(BF), select[...]).astype(BF)
+
+        each_tile(rows, TILE, back_mix)
+
+        @pl.when(l == 0)
+        def _():
+            z_finish(1, UP)
+            x_fold(1, QKV)
+
+        attention_back()
+        for d in range(1, group):
+            k_copy(l, d).start()
+
+        @pl.when(l == 1)
+        def _():
+            x_fold(1, GATE)
+
+        @pl.when(l == 0)
+        def _():
+            z_finish(1, OUT)
+            x_fold(0, DOWN)
+
+        split = kv * 128
+
+        def own_rows(r):
+            base = pl.multiple_of(mine * rows, rows) + r.start
+            return pl.ds(pl.multiple_of(base, TILE), TILE)
+
+        def below(r):
+            return pl.ds(pl.multiple_of(rows + r.start, TILE), TILE)
+
+        def first_part(r):
+            dkv[r] = ksend_buf[own_rows(r), :split].astype(F32)
+            dkv[below(r)] = ksend_buf[own_rows(r), split:].astype(F32)
+
+        each_tile(rows, TILE, first_part)
+        for d in range(1, group):
+            k_in(l, d).wait_recv()
+            taken = pltpu.make_async_copy(o_kin.at[l, d - 1], dopad, local.at[1, 0])
+            taken.start()
+            taken.wait()
+
+            def next_part(r):
+                dkv[r] += dopad[r, :split].astype(F32)
+                dkv[below(r)] += dopad[r, split:].astype(F32)
+
+            each_tile(rows, TILE, next_part)
+
+        def inputs_back(r):
+            at = own_rows(r)
+            dk = jnp.concatenate([dkv[r], dkv[below(r)]], axis=1)
+            dq = dqpad[r]
+            dots[1, n, :, r] = row_sums(dq * qpad[r].astype(F32)) + row_sums(dk * kvpad[at].astype(F32))
+            inverse = rinv[0, r]
+            c, s = cosine[r, :cut], sine[r, :cut]
+            lane = lax.broadcasted_iota(jnp.int32, c.shape, 1)
+            for half, value in ((0, dq), (1, dk)):
+                high = value.astype(BF)
+                rest = (value - high.astype(F32)).astype(BF)
+                flat = dot_last(high, select[...]) + dot_last(rest, select[...])
+                if half:
+                    c = jnp.where(lane < kv_cut, c, 1.0)
+                    s = jnp.where(lane < kv_cut, s, 0.0)
+                scaled[r, half * cut : (half + 1) * cut] = (rotated(flat, c, -s) * inverse).astype(BF)
+
+        each_tile(rows, TILE, inputs_back)
+        for d in range(1, group):
+            k_copy(l, d).wait_send()
+        ready(l, "xmix", "qkv", "res0")
+        turn(xmix)
+        gradient(l, QKV, lambda lanes: scaled[:, lanes], 0, 2 * cut)
+        reduce_narrow(
+            1, 2 * l, lambda b, r: dot_last(scaled[r], w_down[rows_of(b, width), : 2 * cut])
+        )
+
+        @pl.when(l == 1)
+        def _():
+            z_finish(1, DOWN)
+
+        return carry
+
+    lax.fori_loop(0, 2, layer, 0)
+    collect(dcur, o_dx, txsend, txrecv, 0)
+
+    def gain_copy(d, incoming):
+        ref = gall.at[flip(me, d) if incoming else me]
+        return remote(ref, ref, gsend.at[d], grecv.at[d], (flip(me, d), n))
+
+    gall[me] = gsum[...]
+    for d in range(1, count):
+        gain_copy(d, False).start()
+    z_finish(1, QKV)
+    x_fold(0, GATE)
+    z_finish(0, DOWN)
+    x_fold(0, UP)
+    z_finish(0, GATE)
+    x_fold(0, OUT)
+    x_fold(0, QKV)
+    z_finish(0, UP)
+    z_finish(0, OUT)
+    for d in range(1, count):
+        gain_copy(d, True).wait_recv()
+    o_gain[...] = jnp.sum(gall[...], axis=0)
+    collect(i_resid.at[4], o_y, ysend, yrec, 1)
+    collect(dcur, o_dx, txsend, txrecv, 1)
+    collect(i_resid.at[4], o_y, ysend, yrec, 2)
+    collect(dcur, o_dx, txsend, txrecv, 2)
+    for d in range(1, count):
+        gain_copy(d, False).wait_send()
+
+    z_finish(0, QKV)
+
+    def drain(l, carry):
+        for c in range(PIECES):
+            for bit in falling:
+                for j in upper(bit):
+                    x_copy(l, c, bit, j).wait_send()
+            for o in range(1, OUTER):
+                z_copy(l, c, o).wait_send()
+        return carry
+
+    lax.fori_loop(0, 2, drain, 0)
+
+
+def backward_pass(gains, cosine, sine, select, weights, saved, heads, kv):
+    count = lax.axis_size("wide")
+    xall, resid, rinv, q, kvp, mix, g, u, c, dy = saved
+    batches, s_dev, width = dy.shape
+    rows, group = batches * s_dev, count // batches
+    length = rows * group
+    kr = weights[0].shape[1] // count
+    ff = c.shape[2]
+    inner = count // OUTER
+    sd, vm, dma = jax.ShapeDtypeStruct, pltpu.VMEM, pltpu.SemaphoreType.DMA
+    sizes = [w.shape[2] for w in weights]
+    full = kr * count
+    outs = (
+        [sd((2, kr, s), F32) for s in sizes]
+        + [sd((batches, s_dev, width), F32)] * 2
+        + [sd((8, width), F32)]
+        + [sd((2, full, s), BF) for s in sizes]
+        + [sd((2, OUTER * (inner - 1), kr, s), BF) for s in sizes]
+        + [sd((2, OUTER - 1, kr, s), BF) for s in sizes]
+        + [sd((2, max(group - 1, 1), rows, kv * 256), BF)]
+    )
+    half = max(1, inner // 2) * OUTER * kr
+    scratch = [
+        vm((full, ff), BF), vm((full, ff), BF), vm((full, ff), BF),
+        vm((4, rows, width), BF), vm((4, rows, width), BF),
+        vm((2, rows, width), F32), vm((2, rows, 1), F32),
+        vm((rows, ff), F32), vm((rows, ff), F32), vm((rows, ff), BF), vm((rows, ff), BF),
+        vm((2, 4, rows, width), BF), vm((4 * width, rows), BF),
+        vm((rows, heads * 128), BF), vm((length, kv * 256), BF), vm((rows, heads * HEAD_DIM), BF),
+        vm((rows, width), F32), vm((rows, width), F32), vm((3, rows, width), BF),
+        vm((2, 2, rows, width), BF), vm((2, rows, width), BF),
+        vm((rows, heads * 128), BF), vm((rows, heads * 128), F32), vm((length, 256), F32),
+        vm((length, kv * 256), BF),
+        vm((rows, 2 * heads * HEAD_DIM), BF),
+        vm((full, ff), BF), vm((half, ff), BF), vm((max(half, (OUTER - 1) * kr), ff), BF), vm((kr, ff), F32),
+        vm((2, 4, 8, rows), F32), vm((8, width), F32), vm((count, 8, width), F32),
+        dma((17,)), dma((2, 4)), dma((2, 4)), dma((2, 3)), dma((2, 3)), dma((2, 4)), dma((2, 4)),
+        dma((2, group)), dma((2, group)),
+        dma((2 * PIECES, OUTER * (inner - 1))), dma((2 * PIECES, OUTER * (inner - 1))),
+        dma((2 * PIECES, OUTER)), dma((2 * PIECES, OUTER)),
+        dma((2, count)), dma((batches,)), dma((batches,)), dma((batches,)), dma((batches,)),
+        dma((count,)), dma((count,)),
+    ]
+    hbm = pl.BlockSpec(memory_space=pl.ANY)
+    vmem = pl.BlockSpec(memory_space=pltpu.VMEM)
+    return pl.pallas_call(
+        functools.partial(backward_kernel, count),
+        out_shape=outs,
+        in_specs=[vmem] * 4 + [hbm] * (PIECES + len(saved)),
+        out_specs=[hbm] * (PIECES + 2) + [vmem] + [hbm] * (3 * PIECES + 1),
+        scratch_shapes=scratch,
+        compiler_params=pltpu.CompilerParams(
+            collective_id=1, has_side_effects=True, vmem_limit_bytes=60 * 1024 * 1024
+        ),
+        name="backward",
+    )(gains, cosine, sine, select, *weights, *saved)
+
+
 def per_device(tokens, cotangent, *weights):
     layers = [weights[:9], weights[9:]]
     batches, s_dev, width = tokens.shape
-    count = lax.axis_size("wide")
-    group = count // batches
-    me = lax.axis_index("wide")
+    group = lax.axis_size("wide") // batches
     rows = batches * s_dev
     halfway = HEAD_DIM // 2
     heads = layers[0][1].shape[1] // HEAD_DIM
     kv = layers[0][2].shape[1] // HEAD_DIM
     frequency = jnp.power(F32(THETA), -(jnp.arange(halfway, dtype=F32) * 2.0 / HEAD_DIM))
-    pos = (me % group) * rows + jnp.arange(rows, dtype=jnp.int32)
+    pos = (lax.axis_index("wide") % group) * rows + jnp.arange(rows, dtype=jnp.int32)
     angle = pos.astype(F32)[:, None] * frequency[None, :]
-    causal = jnp.arange(rows * group, dtype=jnp.int32)[None, :] <= pos[:, None]
     cos, sin = jnp.cos(angle), jnp.sin(angle)
-    setup = (cos, sin, causal, group)
     cut = kv * HEAD_DIM
     cosine = jnp.concatenate([cos] * (2 * (heads + kv)) + [jnp.ones((rows, cut), F32)], axis=1)
     sine = jnp.concatenate([-sin, sin] * (heads + kv) + [jnp.zeros((rows, cut), F32)], axis=1)
@@ -788,7 +1197,6 @@
     select = (
         (place // HEAD_DIM * 128 + place % HEAD_DIM)[:, None] == jnp.arange(heads * 128)[None, :]
     ).astype(BF)
-
     gains = jnp.stack([layers[0][0], layers[0][5], layers[1][0], layers[1][5]])
     gains_in = jnp.concatenate([gains, jnp.ones_like(gains)], axis=0)
     packs = [
@@ -799,56 +1207,19 @@
         jnp.stack([w[8].T for w in layers]),
     ]
     outs = forward_pass(tokens, cotangent, gains_in, cosine, sine, select, packs, heads, kv)
-    a_qkv, a_out, a_gate, a_up, a_down = outs[:PIECES]
+    whole = outs[:PIECES]
     o_xall, o_resid, o_rinv, o_q, o_kv, o_mix, o_lse, o_g, o_u, o_c, o_dy = outs[PIECES:]
-    saved = []
-    unpad = lambda x, m: x.reshape(x.shape[0], m, 128)[:, :, :HEAD_DIM].reshape(x.shape[0], -1)
-    for i in range(2):
-        full = lambda a: jnp.concatenate([o_xall[a, s] for s in range(4)], axis=1)
-        kv_all = unpad(o_kv[i], 2 * kv)
-        own = lax.dynamic_slice_in_dim(kv_all, (me % group) * rows, rows, 0)
-        lse = o_lse[i].reshape(kv, heads // kv, rows, 1)
-        s1 = (
-            o_resid[2 * i], full(2 * i), o_rinv[2 * i], unpad(o_q[i], heads),
-            own[:, :cut], own[:, cut:], kv_all, lse, o_mix[i],
-        )
-        s2 = (o_resid[2 * i + 1], full(2 * i + 1), o_rinv[2 * i + 1], o_g[i], o_u[i], o_c[i])
-        saved.append((s1, s2))
-    gathered = [
-        (a_qkv[i], a_out[i], jnp.concatenate([a_gate[i], a_up[i]], axis=1), a_down[i])
-        for i in range(2)
-    ]
-    y = o_resid[4]
-    output = collect_tokens(y.reshape(batches, s_dev, width))
-    dy = o_dy.reshape(rows, width).astype(F32)
-    grads, dgains = [None, None], [None] * 4
-    for i in (1, 0):
-        w_qkv, w_out, w_gu, w_down = gathered[i]
-        s1, s2 = saved[i]
-        dh, dgains[2 * i + 1], d_gu, d_down = feed_backward(dy, s2, gains[2 * i + 1], w_gu, w_down)
-        r_down = reduce_blocks(d_down)
-        r_gu = reduce_blocks(d_gu)
-        dy, dgains[2 * i], d_qkv, d_out = attention_backward(dh, s1, gains[2 * i], w_qkv, w_out, setup)
-        r_out = reduce_blocks(d_out)
-        r_qkv = reduce_blocks(d_qkv)
-        cut_q = layers[i][1].shape[1]
-        cut_k = cut_q + layers[i][2].shape[1]
-        half = r_gu.shape[1] // 2
-        grads[i] = (
-            r_qkv[:, :cut_q],
-            r_qkv[:, cut_q:cut_k],
-            r_qkv[:, cut_k:],
-            r_out.T,
-            r_gu[:, :half],
-            r_gu[:, half:],
-            r_down.T,
-        )
-    input_back = collect_tokens(dy.reshape(batches, s_dev, width))
-    dg = lax.psum(jnp.stack(dgains), "wide")
+    saved = (o_xall, o_resid, o_rinv, o_q, o_kv, o_mix, o_g, o_u, o_c, o_dy)
+    back = backward_pass(gains_in, cosine, sine, select, whole, saved, heads, kv)
+    g_qkv, g_out, g_gate, g_up, g_down, output, input_back, dgain = back[:8]
     results = [output, input_back]
-    for i in range(2):
-        a = grads[i]
-        results += [dg[2 * i], a[0], a[1], a[2], a[3], dg[2 * i + 1], a[4], a[5], a[6]]
+    for i, w in enumerate(layers):
+        cut_q = w[1].shape[1]
+        cut_k = cut_q + w[2].shape[1]
+        results += [
+            dgain[2 * i], g_qkv[i][:, :cut_q], g_qkv[i][:, cut_q:cut_k], g_qkv[i][:, cut_k:],
+            g_out[i].T, dgain[2 * i + 1], g_gate[i], g_up[i], g_down[i].T,
+        ]
     return tuple(results)
 
 

time: 1110 us -> 930 us (0.84); the launches traced: 1090 us -> 925 us
  Pallas kernels: 392 us -> 891 us
  waiting for transfers between devices: 270 us -> 0 us
  starting transfers between devices: 124 us -> 0 us
  matrix products: 92.2 us -> 0 us
  local copies, waits for them, and re-layouts: 91.2 us -> 25.7 us
  other arithmetic: 63 us -> 8.02 us
  blocking collectives: 44.7 us -> 0 us
  between operations: 16.6 us -> 0.8 us
    pallas_call x0 -> x1, Pallas kernels: none -> 499 us  [backward_pass(): pl.pallas_call(functools.partial(backward_kernel, count), out_shape=outs,...]
    ppermute x66 -> x0, waiting for transfers between devices: 231 us -> none  [the longest x58 230 us: exchange(): return lax.ppermute(x, 'wide', [(w, w ^ distance) for w in range(count)])]
    ppermute x66 -> x0, starting transfers between devices: 122 us -> none  [the longest x58 96.4 us: exchange(): return lax.ppermute(x, 'wide', [(w, w ^ distance) for w in range(count)])]
    dot_general x26 -> x0, matrix products: 92.2 us -> none  [the longest x4 21.1 us: dot(): return jnp.dot(left, right, preferred_element_type=F32)]
    psum x5 -> x0, blocking collectives: 44.7 us -> none  [the longest x4 23.9 us: back_norm(): dots = lax.psum(dots, 'narrow')]
    convert_element_type x15 -> x0, other arithmetic: 26 us -> none  [the longest x8 12.5 us: reduce_blocks(): moved[j] = (blocks[j].astype(F32) + got.astype(F32)).astype(BF)]
    squeeze x13 -> x3, local copies, waits for them, and re-layouts: 25 us -> 3.92 us  [the longest x1 1.44 us: per_device(): g_qkv[i][:, :cut_q]]
    unnamed x216 -> x24, local copies, waits for them, and re-layouts: 23.1 us -> 2.54 us
  transfers between devices with their start and end apart: 74 -> 0, of which waited for: 28 -> 0; matrix products, arithmetic and copies ran while one was open for 15% -> 0% of each run, Pallas kernels for 0% -> 0%
where the time goes in v3:
time: 930 us; the launch traced here: 925 us
  Pallas kernels  891 us (96%)
  local copies, waits for them, and re-layouts  25.7 us (3%)
    pallas_call x1, Pallas kernels, backward_pass(): pl.pallas_call(functools.partial(backward_kernel, count), out_shape=outs,...  499 us
    pallas_call x1, Pallas kernels, forward_pass(): pl.pallas_call(functools.partial(forward_kernel, count), out_shape=outs,...  392 us

profile of v3, /device:TPU:0, one launch (start us, length us, event | category | flops | bytes accessed | tf_op | source)
XLA Modules:
  0.0 925.3 jit_solution(17415649554987525737)
XLA Ops:
  4.1 1.7 pad_maximum_fusion.4.p_out
  5.8 0.9 fusion.select
  6.7 1.3 maximum_bitcast_fusion
  8.0 0.9 pad_maximum_fusion.3.p_qkv
  8.8 1.0 multiply_sine_fusion
  9.9 4.1 concatenate.17.sine
  14.0 0.9 pad_maximum_fusion.2.p_down
  15.0 4.1 concatenate.16.cosine
  19.1 1.3 pad_maximum_fusion
  20.4 392.1 %forward.1 = (bf16[2,1536,768]{2,1,0:T(8,128)(2,1)}, bf16[2,1536,384]{2,1,0:T(8,128)(2,1)}, bf16[2,1536,1024]{2,1,0:T(8,128)(2,1)}, bf16[2,1536,1024]{2,1,0:T(8,...) custom-call(bf16[4,128,384]{2,1,0:T(8,128)(2,1)} %tokens.1, ...), custom_call_target="tpu_custom_call" | custom-call | tf_op jit(solution)/shard_map/forward/pallas_call | solution.py:529
  412.5 498.6 %backward.1 = (f32[2,192,768]{2,1,0:T(8,128)}, f32[2,192,384]{2,1,0:T(8,128)}, f32[2,192,1024]{2,1,0:T(8,128)}, f32[2,192,1024]{2,1,0:T(8,128)}, f32[2,192,1024]...) custom-call(f32[8,384]{1,0:T(8,128)} %concatenate.15.gains, ...), custom_call_target="tpu_custom_call" | custom-call | tf_op jit(solution)/shard_map/backward/pallas_call | solution.py:1168
  911.2 1.5 slice_reduce_fusion
  912.6 1.9 slice_bitcast_fusion.8
  914.5 1.4 slice_bitcast_fusion.6
  916.0 0.7 slice.87
  916.7 0.8 fusion.11
  917.5 0.7 slice.84
  918.2 0.8 fusion.12
  919.0 1.2 slice_bitcast_fusion.2
  920.3 1.2 slice_bitcast_fusion.1
  921.5 0.7 copy-done
  922.3 1.2 slice_bitcast_fusion
  923.5 0.9 copy.42
  924.4 0.9 copy.43
  (32 shorter events, 3.5 us)
Async XLA Ops:
  9.9 4.1 copy-start.9
  9.9 4.1 copy-start.10
  15.0 4.1 copy-start.5
  15.0 4.1 copy-start.6
  15.0 4.1 copy-start.7
  15.0 4.1 copy-start.8
  914.5 4.5 copy-start.2
  917.5 2.8 copy-start.1
  920.3 2.0 copy-start
  921.5 2.0 copy-start.4
  922.2 2.1 copy-start.3

commit v4 on v3

--- a/solution.py
+++ b/solution.py
@@ -37,6 +37,8 @@
 QKV, OUT, GATE, UP, DOWN = range(5)
 PIECES = 5
 TILE = 256
+AHEAD = 2
+NEAR_AHEAD = 3
 
 
 def flip(index, distance):
@@ -59,15 +61,14 @@
         rest = [j for j in range(1, count) if j % self.inner]
         rest.sort(key=lambda j: (top_bit(j % self.inner), j))
         self.direct, self.rest = direct, rest
-
-    def via(self, j):
-        low = j % self.inner
-        return top_bit(low) if low else j
-
-    def sends(self, i):
-        low = i % self.inner
-        bits = [b for b in self.bits if low == 0 or b > top_bit(low)]
-        return (self.direct + bits) if i == 0 else bits
+        self.near = [j for j in rest if j < self.inner]
+
+    def higher(self, low):
+        return [b for b in self.bits if low == 0 or b > top_bit(low)]
+
+
+def is_middle(me, inner):
+    return ((me // inner + 1) // 2) % 2 == 1
 
 
 def rows_of(index, size):
@@ -108,15 +109,15 @@
 
 def forward_kernel(
     count,
-    tokens, cotangent, gains, cosine, sine, select,
+    tokens, cotangent, gains, frequency, select,
     p_qkv, p_out, p_gate, p_up, p_down,
     a_qkv, a_out, a_gate, a_up, a_down,
-    o_xall, o_resid, o_rinv, o_q, o_kv, o_mix, o_lse, o_g, o_u, o_c, o_dy,
+    o_xall, o_resid, o_rinv, o_q, o_kv, o_mix, o_g, o_u, o_c, o_low, o_cos, o_sin, o_y, o_down,
     w_qkv, w_out, w_gate, w_up, w_down,
-    tok, gall, xall, resid, rinv, qpad, kvall, kvpad, mixpad, mix, lse, gst, ust, cst,
+    tok, gall, xall, resid, rinv, qpad, kvall, kvpad, mixpad, mix, cosine, sine, gst, ust, cst,
     own, stage, crecv, yrecv,
-    bsend, brecv, bown, load, tsend, trecv, dsend, drecv, gsend, grecv,
-    agsend, agrecv, ksend, krecv, rsend, rrecv, save,
+    bsend, brecv, bown, load, tsend, trecv, dsend, drecv, lsend, lrecv, gsend, grecv,
+    agsend, agrecv, ksend, krecv, rsend, rrecv, save, tablesem, lowsem,
 ):
     me, n = lax.axis_index("wide"), lax.axis_index("narrow")
     wide = Wide(count)
@@ -173,55 +174,136 @@
     for d in (1, 2, 3):
         gain_copy(d).start()
 
-    def piece_copy(l, c, i, dist):
+    inner = wide.inner
+    middle = is_middle(me, inner)
+
+    def piece_copy(l, c, i, dist, slot=None):
         block = rows_of(flip(me, i), kr)
         src = packs[c].at[l] if i == 0 else alls[c].at[l, block]
         t, j = l * PIECES + c, i ^ dist
-        return remote(src, alls[c].at[l, block], bsend.at[t, j], brecv.at[t, j], (flip(me, dist), n))
+        slot = j if slot is None else slot
+        return remote(
+            src, alls[c].at[l, block], bsend.at[t, slot], brecv.at[t, j], (flip(me, dist), n)
+        )
 
     def piece_in(l, c, j):
         block = rows_of(flip(me, j), kr)
         dst = alls[c].at[l, block]
         t = l * PIECES + c
-        return remote(dst, dst, bsend.at[t, j], brecv.at[t, j], (flip(me, wide.via(j)), n))
+        return remote(dst, dst, bsend.at[t, j], brecv.at[t, j], (flip(me, inner), n))
 
     def piece_own(l, c):
         return pltpu.make_async_copy(
             packs[c].at[l], alls[c].at[l, rows_of(me, kr)], bown.at[l * PIECES + c]
         )
 
-    def send_own(l, c):
-        for dist in wide.sends(0):
-            piece_copy(l, c, 0, dist).start()
+    def far_sends(l, c, low, action):
+        action(piece_copy(l, c, low, inner))
+        action(piece_copy(l, c, low, 2 * inner))
+
+        @pl.when(middle)
+        def _():
+            action(piece_copy(l, c, low, 3 * inner))
+
+    def pass_on(l, c, low, action):
+        @pl.when(middle)
+        def _():
+            action(piece_copy(l, c, 2 * inner + low, inner, count + low))
+
+    def near_sends(l, c, j, action):
+        for bit in wide.higher(j % inner):
+            action(piece_copy(l, c, j, bit))
+
+    def start(copy):
+        copy.start()
+
+    def wait_send(copy):
+        copy.wait_send()
+
+    def all_sends(l, c, action):
+        if c == QKV:
+            for low in range(inner):
+                near_sends(l, c, low, action)
+                far_sends(l, c, low, action)
+                pass_on(l, c, low, action)
+        else:
+            far_sends(l, c, 0, action)
+            pass_on(l, c, 0, action)
+            for j in range(count):
+                near_sends(l, c, j, action)
+
+    def send_far(l, c):
+        if c == QKV:
+            near_sends(l, c, 0, start)
+        far_sends(l, c, 0, start)
         piece_own(l, c).start()
 
-    def relay(l, c):
-        for j in wide.direct:
-            piece_in(l, c, j).wait_recv()
-            for dist in wide.sends(j):
-                piece_copy(l, c, j, dist).start()
-        ahead = c + 2
-        if ahead < PIECES:
-            send_own(l, ahead)
-        else:
+    def send_near(l, c):
+        if c != QKV:
+            near_sends(l, c, 0, start)
+
+    def at_piece(l, c, action):
+        if c < PIECES:
+            action(l, c)
+        elif not isinstance(l, int):
 
             @pl.when(l == 0)
             def _():
-                send_own(1, ahead - PIECES)
+                action(1, c - PIECES)
+
+        elif l == 0:
+            action(1, c - PIECES)
+
+    def relay_near(l):
+        for low in wide.near:
+            piece_in(l, QKV, low).wait_recv()
+            near_sends(l, QKV, low, start)
+            far_sends(l, QKV, low, start)
+
+    def relay(l, c):
+        for outer in (1, 2, 3):
+            for low in range(inner) if c == QKV else (0,):
+                piece_in(l, c, outer * inner + low).wait_recv()
+                if outer == 2:
+                    pass_on(l, c, low, start)
+                if c != QKV:
+                    near_sends(l, c, outer * inner, start)
+        at_piece(l, c + AHEAD, send_far)
+        at_piece(l, c + NEAR_AHEAD, send_near)
 
     def arrive(l, c):
-        for j in wide.rest:
-            piece_in(l, c, j).wait_recv()
-            for dist in wide.sends(j):
-                piece_copy(l, c, j, dist).start()
+        if c != QKV:
+            for j in wide.rest:
+                piece_in(l, c, j).wait_recv()
+                near_sends(l, c, j, start)
         piece_own(l, c).wait()
         fetch = pltpu.make_async_copy(alls[c].at[l], bufs[c], load.at[c])
         fetch.start()
         fetch.wait()
 
-    send_own(0, QKV)
-    send_own(0, OUT)
-    spread(cotangent, o_dy, dsend, drecv, True)
+    send_far(0, QKV)
+    for c in range(1, NEAR_AHEAD):
+        send_near(0, c)
+
+    def tables(r):
+        lane = lax.broadcasted_iota(jnp.int32, (128, cosine.shape[1]), 1)
+        pos = (me % group) * rows + r.start + lax.broadcasted_iota(jnp.int32, lane.shape, 0)
+        angle = pos.astype(F32) * frequency[...]
+        cosine[r] = jnp.cos(angle)
+        turn = jnp.sin(angle)
+        sine[r] = jnp.where(lane % HEAD_DIM < HEAD_DIM // 2, -turn, turn)
+
+    each_tile(rows, 128, tables)
+    saved_tables = [
+        pltpu.make_async_copy(cosine, o_cos, tablesem.at[0]),
+        pltpu.make_async_copy(sine, o_sin, tablesem.at[1]),
+    ]
+    for c in saved_tables:
+        c.start()
+    relay_near(0)
+    for c in range(1, AHEAD):
+        send_far(0, c)
+    spread(cotangent, o_low.at[n], dsend, drecv, True)
     spread_wait(tokens, tok, tsend, trecv)
     for b in range(batches):
         resid[0, b * s_dev : (b + 1) * s_dev] = tok[b].astype(F32)
@@ -268,13 +350,17 @@
 
         each_tile(rows, 128, body)
 
+    def low_copy(slot, dist, k):
+        ref = o_low.at[slot]
+        return remote(ref, ref, lsend.at[k], lrecv.at[k], (me, flip(n, dist)))
+
     def rs_core(a, k):
         return remote(stage.at[k], crecv.at[a, k], rsend.at[a, k], rrecv.at[a, k], (me, core))
 
     def rs_other(a):
         return remote(stage.at[2], yrecv.at[a], rsend.at[a, 2], rrecv.at[a, 2], (me, other))
 
-    def reduce_narrow(a, product):
+    def reduce_narrow(a, product, filler):
         for k, b in ((1, cross), (0, core)):
 
             def body(r, k=k, b=b):
@@ -299,6 +385,7 @@
             own[r] = product(n, r)
 
         each_tile(rows, TILE, body_own)
+        filler()
         rs_core(a, 0).wait_recv()
         rs_other(a).wait_recv()
 
@@ -340,7 +427,6 @@
             total = jnp.sum(jnp.exp(s - top), axis=1, keepdims=True)
             norm = top + jnp.log(total)
             p = jnp.exp(s - norm).astype(BF)
-            lse[l, h, r] = norm
             mixpad[r, lanes] = dot(p, kvpad[l, :, rows_of(kv + g, 128)]).astype(BF)
             return carry
 
@@ -363,23 +449,73 @@
             (rinv.at[2 * l], o_rinv.at[2 * l]), (rinv.at[2 * l + 1], o_rinv.at[2 * l + 1]),
             (resid.at[2 * l], o_resid.at[2 * l]), (resid.at[2 * l + 1], o_resid.at[2 * l + 1]),
             (qpad.at[l], o_q.at[l]), (kvpad.at[l], o_kv.at[l]), (mix.at[l], o_mix.at[l]),
-            (lse.at[l], o_lse.at[l]), (gst, o_g.at[l]), (ust, o_u.at[l]), (cst, o_c.at[l]),
+            (gst, o_g.at[l]), (ust, o_u.at[l]), (cst, o_c.at[l]),
         ]
         return [functools.partial(saved, s, d, i) for i, (s, d) in enumerate(pairs)]
+
+    cut = heads * HEAD_DIM
+    kv_cut = kv * HEAD_DIM
+
+    def down_gradient():
+        low_copy(core, 1, 1).wait_recv()
+        low_copy(cross, 1, 3).wait_recv()
+        for s in range(4):
+            parts = [
+                pltpu.make_async_copy(
+                    o_low.at[s, b], stage.at[0, pl.ds(b * s_dev, s_dev)], lowsem.at[b]
+                )
+                for b in range(batches)
+            ]
+            for c in parts:
+                c.start()
+            for c in parts:
+                c.wait()
+            w_up[s * width : (s + 1) * width, :rows] = stage[0].T
+
+        half = 2 * width
+
+        def put(s):
+            at = pl.ds(s * half, half)
+            return pltpu.make_async_copy(w_gate.at[at], o_down.at[1, at], lowsem.at[s])
+
+        for s in range(2):
+            at = pl.ds(s * half, half)
+
+            def tile(j, carry):
+                lanes = rows_of(j, TILE)
+                w_gate[at, lanes] = dot(w_up[at, :rows], cst[:, lanes]).astype(BF)
+                return carry
+
+            lax.fori_loop(0, w_gate.shape[1] // TILE, tile, 0)
+            put(s).start()
+        for s in range(2):
+            put(s).wait()
 
     def layer(l, carry):
         first, second = 2 * l, 2 * l + 1
         ag_start(first)
         ag_finish(first)
-        relay(l, QKV)
+
+        @pl.when(l == 0)
+        def _():
+            relay(0, QKV)
+
+        @pl.when(l == 1)
+        def _():
+            low_copy(other, 2, 2).wait_recv()
+            low_copy(other, 1, 3).start()
+
         arrive(l, QKV)
 
         def project(r):
-            cut = heads * HEAD_DIM
+            lane = lax.broadcasted_iota(jnp.int32, (TILE, cut), 1)
             for half in (1, 0):
                 columns = slice(half * cut, (half + 1) * cut)
                 raw = narrow_sum(first, w_qkv, r, columns) * rinv[first, r]
-                low = rotated(raw, cosine[r, columns], sine[r, columns]).astype(BF)
+                c, s = cosine[r], sine[r]
+                if half:
+                    c, s = jnp.where(lane < kv_cut, c, 1.0), jnp.where(lane < kv_cut, s, 0.0)
+                low = rotated(raw, c, s).astype(BF)
                 if half:
                     base = pl.multiple_of(mine * rows, rows) + r.start
                     kvall[l, pl.ds(pl.multiple_of(base, TILE), TILE)] = low
@@ -393,10 +529,9 @@
         for d in range(1, group):
             kv_in(l, d).wait_recv()
         attention(l)
-        relay(l, GATE)
         arrive(l, OUT)
         reduce_narrow(
-            first, lambda b, r: dot_last(mix[l, r], w_out[rows_of(b, width)])
+            first, lambda b, r: dot_last(mix[l, r], w_out[rows_of(b, width)]), lambda: relay(l, GATE)
         )
         ag_start(second)
         ag_finish(second)
@@ -406,7 +541,7 @@
 
         @pl.when(l == 1)
         def _():
-            for c in layer_saves(0)[10:]:
+            for c in layer_saves(0)[9:]:
                 c().wait()
 
         columns_of = lambda j: rows_of(j, TILE)
@@ -427,32 +562,55 @@
         lax.fori_loop(0, w_gate.shape[1] // TILE, hidden, 0)
         for c in layer_saves(l):
             c().start()
+
+        @pl.when(l == 0)
+        def _():
+            spread_wait(cotangent, o_low.at[n], dsend, drecv)
+            low_copy(n, 2, 2).start()
+            low_copy(n, 1, 1).start()
+
+        @pl.when(l == 0)
+        def _():
+            relay_near(1)
+
         relay(l, DOWN)
+
+        @pl.when(l == 1)
+        def _():
+            down_gradient()
+
         arrive(l, DOWN)
-        reduce_narrow(
-            second, lambda b, r: dot_last(cst[r], w_down[rows_of(b, width)])
-        )
+
+        def ahead():
+            @pl.when(l == 0)
+            def _():
+                relay(1, QKV)
+
+        reduce_narrow(second, lambda b, r: dot_last(cst[r], w_down[rows_of(b, width)]), ahead)
         return carry
 
     lax.fori_loop(0, 2, layer, 0)
-    last = saved(resid.at[4], o_resid.at[4], 13)
+    each_tile(rows, 128, lambda r: stage.__setitem__((0, r), resid[4, r].astype(BF)))
+    last = saved(stage.at[0], o_y, 12)
     last.start()
-    for c in layer_saves(0)[:10]:
+    for c in layer_saves(0)[:9]:
         c().wait()
     for c in layer_saves(1):
         c().wait()
     last.wait()
-    spread_wait(cotangent, o_dy, dsend, drecv)
+    for c in saved_tables:
+        c.wait()
+    low_copy(n, 2, 2).wait_send()
+    low_copy(n, 1, 1).wait_send()
+    low_copy(other, 1, 3).wait_send()
     spread(tokens, tok, tsend, trecv, False)
-    spread(cotangent, o_dy, dsend, drecv, False)
+    spread(cotangent, o_low.at[n], dsend, drecv, False)
     for d in (1, 2, 3):
         gain_copy(d).wait_send()
 
     def drain(l, carry):
         for c in range(PIECES):
-            for i in range(count):
-                for dist in wide.sends(i):
-                    piece_copy(l, c, i, dist).wait_send()
+            all_sends(l, c, wait_send)
         for d in range(1, group):
             kv_copy(l, d).wait_send()
         for a in (2 * l, 2 * l + 1):
@@ -464,7 +622,7 @@
     lax.fori_loop(0, 2, drain, 0)
 
 
-def forward_pass(tokens, cotangent, gains, cosine, sine, select, packs, heads, kv):
+def forward_pass(tokens, cotangent, gains, frequency, select, packs, heads, kv):
     count = lax.axis_size("wide")
     batches, s_dev, width = tokens.shape
     rows, group = batches * s_dev, count // batches
@@ -475,16 +633,19 @@
     whole = [sd((2, kr * count, p.shape[2]), BF) for p in packs]
     outs = whole + [
         sd((4, 4, rows, width), BF),
-        sd((5, rows, width), F32),
+        sd((4, rows, width), F32),
         sd((4, rows, 1), F32),
         sd((2, rows, heads * 128), BF),
         sd((2, length, kv * 256), BF),
         sd((2, rows, heads * HEAD_DIM), BF),
-        sd((2, heads, rows, 1), F32),
         sd((2, rows, ff), F32),
         sd((2, rows, ff), F32),
         sd((2, rows, ff), BF),
-        sd((batches, s_dev, width), BF),
+        sd((4, batches, s_dev, width), BF),
+        sd((rows, heads * HEAD_DIM), F32),
+        sd((rows, heads * HEAD_DIM), F32),
+        sd((rows, width), BF),
+        sd(whole[DOWN].shape, BF),
     ]
     dma = pltpu.SemaphoreType.DMA
     scratch = [pltpu.VMEM((kr * count, p.shape[2]), BF) for p in packs] + [
@@ -498,7 +659,8 @@
         pltpu.VMEM((2, length, kv * 256), BF),
         pltpu.VMEM((rows, heads * 128), BF),
         pltpu.VMEM((2, rows, heads * HEAD_DIM), BF),
-        pltpu.VMEM((2, heads, rows, 1), F32),
+        pltpu.VMEM((rows, heads * HEAD_DIM), F32),
+        pltpu.VMEM((rows, heads * HEAD_DIM), F32),
         pltpu.VMEM((rows, ff), F32),
         pltpu.VMEM((rows, ff), F32),
         pltpu.VMEM((rows, ff), BF),
@@ -506,7 +668,7 @@
         pltpu.VMEM((3, rows, width), BF),
         pltpu.VMEM((4, 2, rows, width), BF),
         pltpu.VMEM((4, rows, width), BF),
-        dma((2 * PIECES, count)),
+        dma((2 * PIECES, count + count // OUTER)),
         dma((2 * PIECES, count)),
         dma((2 * PIECES,)),
         dma((PIECES,)),
@@ -516,46 +678,87 @@
         dma((batches,)),
         dma((4,)),
         dma((4,)),
+        dma((4,)),
+        dma((4,)),
         dma((4, 4)),
         dma((4, 4)),
         dma((2, group)),
         dma((2, group)),
         dma((4, 3)),
         dma((4, 3)),
-        dma((14,)),
+        dma((13,)),
+        dma((2,)),
+        dma((max(2, batches),)),
     ]
     hbm = pl.BlockSpec(memory_space=pl.ANY)
     vmem = pl.BlockSpec(memory_space=pltpu.VMEM)
     return pl.pallas_call(
         functools.partial(forward_kernel, count),
         out_shape=outs,
-        in_specs=[hbm, hbm] + [vmem] * 4 + [hbm] * PIECES,
+        in_specs=[hbm, hbm] + [vmem] * 3 + [hbm] * PIECES,
         out_specs=[hbm] * len(outs),
         scratch_shapes=scratch,
         compiler_params=pltpu.CompilerParams(
             collective_id=0, has_side_effects=True, vmem_limit_bytes=60 * 1024 * 1024
         ),
         name="forward",
-    )(tokens, cotangent, gains, cosine, sine, select, *packs)
+    )(tokens, cotangent, gains, frequency, select, *packs)
 
 
 def dot_rows(left, right):
     return lax.dot_general(left, right, (((0,), (0,)), ((), ())), preferred_element_type=F32)
 
 
-ORDER = (DOWN, GATE, UP, OUT, QKV)
+SEND, FOLD, MERGE, FINISH = range(4)
+POINTS = {
+    "gathered": ([], [(SEND, 1, QKV), (FOLD, 1, UP)]),
+    "down": ([], []),
+    "mid_reduce": (
+        [(SEND, 1, GATE)],
+        [(MERGE, 1, QKV), (SEND, 0, GATE)],
+    ),
+    "mid_done": (
+        [],
+        [],
+    ),
+    "mix_gather": (
+        [(FOLD, 1, DOWN)],
+        [(FOLD, 0, DOWN)],
+    ),
+    "mix_back": (
+        [],
+        [],
+    ),
+    "attended": (
+        [],
+        [(FOLD, 1, OUT)],
+    ),
+    "kv_sent": (
+        [(SEND, 1, UP), (MERGE, 1, DOWN), (FOLD, 1, GATE)],
+        [(MERGE, 1, UP), (FINISH, 1, GATE), (SEND, 0, UP), (FOLD, 0, GATE), (MERGE, 1, OUT)],
+    ),
+    "kv_done": (
+        [],
+        [(MERGE, 0, DOWN)],
+    ),
+    "mix_reduce": (
+        [(MERGE, 1, GATE), (SEND, 1, OUT)],
+        [(SEND, 0, OUT), (FINISH, 1, OUT), (MERGE, 0, GATE)],
+    ),
+}
+TAIL = [(FOLD, 0, UP), (SEND, 0, QKV), (FINISH, 1, DOWN), (FINISH, 0, DOWN), (FOLD, 0, OUT), (MERGE, 0, UP), (FINISH, 1, QKV), (MERGE, 0, OUT), (FOLD, 0, QKV), (FINISH, 0, OUT), (FINISH, 1, UP), (FOLD, 1, QKV), (FINISH, 0, UP), (MERGE, 0, QKV), (FINISH, 0, GATE), (FINISH, 0, QKV)]
 
 
 def backward_kernel(
     count,
-    gains, cosine, sine, select,
+    gains, select,
     a_qkv, a_out, a_gate, a_up, a_down,
-    i_xall, i_resid, i_rinv, i_q, i_kv, i_mix, i_g, i_u, i_c, i_dy,
+    i_xall, i_resid, i_rinv, i_q, i_kv, i_mix, i_g, i_u, i_c, i_low, i_cos, i_sin, i_y, i_down,
     g_qkv, g_out, g_gate, g_up, g_down, o_y, o_dx, o_gain,
     d_qkv, d_out, d_gate, d_up, d_down,
     x_qkv, x_out, x_gate, x_up, x_down,
     z_qkv, z_out, z_gate, z_up, z_down, o_kin,
-    w_gate, w_up, w_down, xmid, xmix, resid, rinv, gst, ust, cst, dus, low, turned, qpad, kvpad, mix,
+    w_gate, w_up, w_down, xmid, xmix, resid, rinv, cosine, sine, gst, ust, cst, dus, low, turned, qpad, kvpad, mix,
     dcur, own, stage, crecv, yrecv, dopad, dqpad, dkv, ksend_buf, scaled, piece, have, got, final,
     dots, gsum, gall,
     load, agsend, agrecv, rsend, rrecv, msend, mrecv, ksend, krecv,
@@ -564,7 +767,7 @@
     me, n = lax.axis_index("wide"), lax.axis_index("narrow")
     wide = Wide(count)
     inner = wide.inner
-    batches, s_dev, width = i_dy.shape
+    batches, s_dev, width = i_low.shape[1:]
     rows = batches * s_dev
     group = count // batches
     weights = (a_qkv, a_out, a_gate, a_up, a_down)
@@ -641,7 +844,7 @@
                 def _():
                     pltpu.make_async_copy(part, target.at[b], recv.at[b]).wait()
 
-    def ag(k):
+    def ag(k, filler):
         def own_copy(dist):
             ref = low.at[k, n]
             return remote(ref, ref, agsend.at[k, dist], agrecv.at[k, dist], (me, flip(n, dist)))
@@ -656,6 +859,7 @@
         each_tile(rows, 128, body)
         own_copy(2).start()
         own_copy(1).start()
+        filler()
         into(2).wait_recv()
         ref = low.at[k, other]
         passed = remote(ref, ref, agsend.at[k, 3], agrecv.at[k, 3], (me, core))
@@ -687,7 +891,7 @@
     def rs_other(k):
         return remote(stage.at[2], yrecv.at[k], rsend.at[k, 2], rrecv.at[k, 2], (me, other))
 
-    def reduce_narrow(k, a, product):
+    def reduce_narrow(k, a, product, filler):
         for d in (1, 2, 3):
             dots_copy(k, d, False).start()
         for j, b in ((1, cross), (0, core)):
@@ -714,6 +918,7 @@
             own[r] = product(n, r)
 
         each_tile(rows, TILE, body_own)
+        filler()
         rs_core(k, 0).wait_recv()
         for d in (1, 2, 3):
             dots_copy(k, d, True).wait_recv()
@@ -737,144 +942,254 @@
         for d in (1, 2, 3):
             dots_copy(k, d, False).wait_send()
 
-    def fold_slot(bit, j):
-        base = sum(OUTER * b for b in wide.bits if b > bit)
+    middle = is_middle(me, inner)
+    falling = list(reversed(wide.bits))
+
+    def outer_first(l, c):
+        return l == 1 and c == QKV
+
+    def lows(l, c):
+        return list(range(inner)) if outer_first(l, c) else [0]
+
+    def outers(l, c):
+        return [0] if outer_first(l, c) else list(range(OUTER))
+
+    def upper(l, c, bit):
+        return [o * inner + i for o in outers(l, c) for i in range(bit, 2 * bit)]
+
+    def lower(l, c, bit):
+        return [o * inner + i for o in outers(l, c) for i in range(bit)]
+
+    def fold_slot(l, c, bit, j):
+        base = sum(len(outers(l, c)) * b for b in wide.bits if b > bit)
         return base + (j // inner) * bit + j % inner
 
+    def block(l, c, j):
+        return grads[c].at[l, rows_of(flip(me, j), kr)]
+
     def x_copy(l, c, bit, j):
-        slot = fold_slot(bit, j - bit)
+        slot = fold_slot(l, c, bit, j - bit)
+        t = l * PIECES + c
         return remote(
-            grads[c].at[l, rows_of(flip(me, j), kr)], xins[c].at[l, slot],
-            xsend.at[l * PIECES + c, slot], xrecv.at[l * PIECES + c, slot], (flip(me, bit), n),
+            block(l, c, j), xins[c].at[l, slot], xsend.at[t, slot], xrecv.at[t, slot], (flip(me, bit), n)
         )
 
     def x_in(l, c, bit, j):
-        slot = fold_slot(bit, j)
+        slot = fold_slot(l, c, bit, j)
+        t = l * PIECES + c
         ref = xins[c].at[l, slot]
+        return remote(ref, ref, xsend.at[t, slot], xrecv.at[t, slot], (flip(me, bit), n))
+
+    def z_copy(l, c, o, low):
+        t, slot = l * PIECES + c, low * OUTER + o - 1
         return remote(
-            ref, ref, xsend.at[l * PIECES + c, slot], xrecv.at[l * PIECES + c, slot], (flip(me, bit), n)
+            block(l, c, o * inner + low), zins[c].at[l, slot], zsend.at[t, slot], zrecv.at[t, slot],
+            (flip(me, o * inner), n),
         )
 
-    def z_copy(l, c, o):
+    def z_far(l, c, low):
+        t, slot = l * PIECES + c, low * OUTER + 3
         return remote(
-            grads[c].at[l, rows_of(flip(me, o * inner), kr)], zins[c].at[l, o - 1],
-            zsend.at[l * PIECES + c, o], zrecv.at[l * PIECES + c, o], (flip(me, o * inner), n),
+            block(l, c, 3 * inner + low), zins[c].at[l, slot], zsend.at[t, slot], zrecv.at[t, slot],
+            (flip(me, inner), n),
         )
 
-    def z_in(l, c, o):
-        ref = zins[c].at[l, o - 1]
-        return remote(
-            ref, ref, zsend.at[l * PIECES + c, o], zrecv.at[l * PIECES + c, o], (flip(me, o * inner), n)
-        )
-
-    def upper(bit):
-        return [j for j in range(count) if bit <= j % inner < 2 * bit]
-
-    def lower(bit):
-        return [j for j in range(count) if j % inner < bit]
-
-    falling = list(reversed(wide.bits))
+    def z_in(l, c, slot):
+        t = l * PIECES + c
+        ref = zins[c].at[l, slot]
+        return remote(ref, ref, zsend.at[t, slot], zrecv.at[t, slot], (flip(me, inner), n))
 
     def x_send(l, c):
-        for j in upper(falling[0]):
+        for j in upper(l, c, falling[0]):
             x_copy(l, c, falling[0], j).start()
+
+    def z_start(l, c):
+        for low in lows(l, c):
+            z_copy(l, c, 1, low).start()
+
+            @pl.when(middle)
+            def _():
+                z_copy(l, c, 3, low).start()
+
+            @pl.when(jnp.logical_not(middle))
+            def _():
+                z_far(l, c, low).start()
+                z_copy(l, c, 2, low).start()
+
+    def moved(pairs):
+        for k, (src, dst) in enumerate(pairs):
+            pltpu.make_async_copy(src, dst, local.at[0, k]).start()
+        for k, (src, dst) in enumerate(pairs):
+            pltpu.make_async_copy(src, dst, local.at[0, k]).wait()
+
+    def held(buffer, i, columns, size=1):
+        return buffer.at[pl.ds(i * kr, size * kr), pl.ds(0, columns)]
+
+    def add_held(count_of, columns, wide_out):
+        tile = 64 if kr % 64 == 0 else 16
+
+        def body(r):
+            total = have[r, :columns].astype(F32) + got[r, :columns].astype(F32)
+            if wide_out:
+                final[r, :columns] = total
+            else:
+                have[r, :columns] = total.astype(BF)
+
+        each_tile(count_of * kr, tile, body)
+
+    def z_merge(l, c):
+        columns = grads[c].shape[2]
+
+        @pl.when(middle)
+        def _():
+            for low in lows(l, c):
+                z_in(l, c, low * OUTER + 3).wait_recv()
+                mine_at = held(have, 0, columns)
+                far = block(l, c, 2 * inner + low)
+                moved([(far, mine_at), (zins[c].at[l, low * OUTER + 3], held(got, 0, columns))])
+                add_held(1, columns, False)
+                moved([(mine_at, far)])
+                z_copy(l, c, 2, low).start()
+
+    def put_result(l, c):
+        columns = grads[c].shape[2]
+        put = pltpu.make_async_copy(final.at[:, pl.ds(0, columns)], results[c].at[l], local.at[1, 0])
+        put.start()
+        put.wait()
 
     def x_fold(l, c):
         columns = grads[c].shape[2]
         for at, bit in enumerate(falling):
-            blocks = lower(bit)
+            blocks = lower(l, c, bit)
+            last = outer_first(l, c) and at + 1 == len(falling)
             for j in blocks:
                 x_in(l, c, bit, j).wait_recv()
             pairs = []
             for i, j in enumerate(blocks):
-                block = grads[c].at[l, rows_of(flip(me, j), kr)]
-                mine_at = have.at[pl.ds(i * kr, kr), pl.ds(0, columns)]
-                theirs_at = got.at[pl.ds(i * kr, kr), pl.ds(0, columns)]
-                pairs.append((block, mine_at, theirs_at, xins[c].at[l, fold_slot(bit, j)]))
-            for i, (block, mine_at, theirs_at, arrived) in enumerate(pairs):
-                pltpu.make_async_copy(block, mine_at, local.at[0, i]).start()
-                pltpu.make_async_copy(arrived, theirs_at, local.at[1, i]).start()
-            for i, (block, mine_at, theirs_at, arrived) in enumerate(pairs):
-                pltpu.make_async_copy(block, mine_at, local.at[0, i]).wait()
-                pltpu.make_async_copy(arrived, theirs_at, local.at[1, i]).wait()
-
-            def body(r):
-                have[r, :columns] = (
-                    have[r, :columns].astype(F32) + got[r, :columns].astype(F32)
-                ).astype(BF)
-
-            each_tile(len(blocks) * kr, 64, body)
-            for i, (block, mine_at, theirs_at, arrived) in enumerate(pairs):
-                pltpu.make_async_copy(mine_at, block, local.at[0, i]).start()
-            for i, (block, mine_at, theirs_at, arrived) in enumerate(pairs):
-                pltpu.make_async_copy(mine_at, block, local.at[0, i]).wait()
+                pairs.append((block(l, c, j), held(have, i, columns)))
+                pairs.append((xins[c].at[l, fold_slot(l, c, bit, j)], held(got, i, columns)))
+            moved(pairs)
+            add_held(len(blocks), columns, last)
+            if last:
+                put_result(l, c)
+                return
+            moved([(held(have, i, columns), block(l, c, j)) for i, j in enumerate(blocks)])
             if at + 1 < len(falling):
-                for j in upper(falling[at + 1]):
+                for j in upper(l, c, falling[at + 1]):
                     x_copy(l, c, falling[at + 1], j).start()
-        for o in range(1, OUTER):
-            z_copy(l, c, o).start()
+        z_start(l, c)
 
     def z_finish(l, c):
         columns = grads[c].shape[2]
-        for o in range(1, OUTER):
-            z_in(l, c, o).wait_recv()
-        moves = [(grads[c].at[l, rows_of(me, kr)], have.at[pl.ds(0, kr), pl.ds(0, columns)])]
-        for o in range(1, OUTER):
-            moves.append((zins[c].at[l, o - 1], got.at[pl.ds((o - 1) * kr, kr), pl.ds(0, columns)]))
-        for i, (src, dst) in enumerate(moves):
-            pltpu.make_async_copy(src, dst, local.at[0, i]).start()
-        for i, (src, dst) in enumerate(moves):
-            pltpu.make_async_copy(src, dst, local.at[0, i]).wait()
-
-        def body(i, carry):
-            r = pl.ds(pl.multiple_of(i * 16, 16), 16)
-            total = have[r, :columns].astype(F32)
-            for o in range(OUTER - 1):
-                at = pl.ds(pl.multiple_of(o * kr + i * 16, 16), 16)
-                total = total + got[at, :columns].astype(F32)
-            final[r, :columns] = total
-            return carry
-
-        lax.fori_loop(0, kr // 16, body, 0)
-        put = pltpu.make_async_copy(final.at[:, pl.ds(0, columns)], results[c].at[l], local.at[1, 0])
-        put.start()
-        put.wait()
-
-    def gradient(l, c, right, start, columns):
-        step = min(columns, TILE) if columns % TILE == 0 else 128
+        for low in lows(l, c):
+            base = low * OUTER
+            z_in(l, c, base).wait_recv()
+            z_in(l, c, base + 1).wait_recv()
+            moved(
+                [
+                    (block(l, c, low), held(have, 0, columns)),
+                    (zins[c].at[l, base], held(got, 0, columns)),
+                    (zins[c].at[l, base + 1], held(got, 1, columns)),
+                ]
+            )
+
+            @pl.when(middle)
+            def _():
+                z_in(l, c, base + 2).wait_recv()
+                moved([(zins[c].at[l, base + 2], held(got, 2, columns))])
+
+            @pl.when(jnp.logical_not(middle))
+            def _():
+                got[2 * kr : 3 * kr, :columns] = jnp.zeros((kr, columns), BF)
+
+            def body(i, carry):
+                r = pl.ds(pl.multiple_of(i * 16, 16), 16)
+                total = have[r, :columns].astype(F32)
+                for o in range(OUTER - 1):
+                    at = pl.ds(pl.multiple_of(o * kr + i * 16, 16), 16)
+                    total = total + got[at, :columns].astype(F32)
+                if outer_first(l, c):
+                    have[r, :columns] = total.astype(BF)
+                else:
+                    final[r, :columns] = total
+                return carry
+
+            lax.fori_loop(0, kr // 16, body, 0)
+            if outer_first(l, c):
+                moved([(held(have, 0, columns), block(l, c, low))])
+            else:
+                put_result(l, c)
+        if outer_first(l, c):
+            x_send(l, c)
+
+    def send(l, c):
+        z_start(l, c) if outer_first(l, c) else x_send(l, c)
+
+    actions = (send, x_fold, z_merge, z_finish)
+
+    def at_point(l, name):
+        for own_layer, todo in zip((1, 0), POINTS[name]):
+            if todo:
+
+                @pl.when(l == own_layer)
+                def _():
+                    for action, m, c in todo:
+                        actions[action](m, c)
+
+    def gradient(l, c, right, columns):
+        half = 2 * width
 
         def put(s):
-            at = rows_of(s, width)
+            at = pl.ds(s * half, half)
             return pltpu.make_async_copy(
                 piece.at[at, pl.ds(0, columns)], grads[c].at[l, at], local.at[1, 0]
             )
 
-        def body(s, carry):
-            def tile(j, carry):
-                lanes = pl.ds(pl.multiple_of(j * step, step), step)
-                piece[rows_of(s, width), lanes] = dot(
-                    turned[rows_of(s, width)], right(lanes)
-                ).astype(BF)
-                return carry
-
-            lax.fori_loop(0, columns // step, tile, 0)
+        for s in range(2):
+            at = pl.ds(s * half, half)
+            done = 0
+            while done < columns:
+                size = TILE if columns - done >= TILE else columns - done
+                number = (columns - done) // size if size == TILE else 1
+
+                def tile(j, carry, done=done, size=size):
+                    lanes = pl.ds(pl.multiple_of(done + j * size, 128), size)
+                    piece[at, lanes] = dot(turned[at], right(lanes)).astype(BF)
+                    return carry
+
+                lax.fori_loop(0, number, tile, 0)
+                done += number * size
             put(s).start()
-            return carry
-
-        lax.fori_loop(0, 4, body, 0)
-        for s in range(4):
+        for s in range(2):
             put(s).wait()
-        x_send(l, c)
-
-    fetch(1, *[name for name in names if name not in ("qkv", "out")])
-    collect(i_resid.at[4], o_y, ysend, yrec, 0)
-    for b in range(batches):
-        pltpu.make_async_copy(i_dy.at[b], low.at[1, 0, pl.ds(b * s_dev, s_dev)], local.at[0, b]).start()
-    for b in range(batches):
-        pltpu.make_async_copy(i_dy.at[b], low.at[1, 0, pl.ds(b * s_dev, s_dev)], local.at[0, b]).wait()
+
+    x_send(1, DOWN)
+    early = ("down", "gate", "up", "xmid", "res1", "inv1", "g", "u", "c")
+    late = ("xmix", "res0", "inv0", "q", "kv", "mix")
+    for s in range(4):
+        for b in range(batches):
+            pltpu.make_async_copy(
+                i_low.at[s, b], low.at[0, s, pl.ds(b * s_dev, s_dev)], local.at[0, s * batches + b]
+            ).start()
+    fetch(1, "down", "g", "u", "inv1", "gate", "up", "xmid", "res1")
+    fetch(1, *late)
+    fetch_tables = [
+        pltpu.make_async_copy(i_cos, cosine, local.at[1, 1]),
+        pltpu.make_async_copy(i_sin, sine, local.at[1, 2]),
+    ]
+    for c in fetch_tables:
+        c.start()
+    collect(i_y, o_y, ysend, yrec, 0)
+    for s in range(4):
+        for b in range(batches):
+            pltpu.make_async_copy(
+                i_low.at[s, b], low.at[0, s, pl.ds(b * s_dev, s_dev)], local.at[0, s * batches + b]
+            ).wait()
+    for c in fetch_tables:
+        c.wait()
 
     def widen(r):
-        dcur[r] = low[1, 0, r].astype(F32)
+        dcur[r] = low[0, n, r].astype(F32)
 
     each_tile(rows, 128, widen)
     gsum[...] = jnp.zeros_like(gsum)
@@ -931,16 +1246,20 @@
 
         @pl.when(l == 0)
         def _():
-            fetch(0, *[name for name in names if name not in ("qkv", "out")])
-
-        ag(0)
-        turn(low.at[0])
-        ready(l, "c")
-        gradient(l, DOWN, lambda lanes: cst[:, lanes], 0, ff)
-
-        @pl.when(l == 0)
-        def _():
-            x_fold(1, UP)
+            fetch(0, *early)
+
+            def before():
+                turn(xmix)
+                gradient(1, QKV, lambda lanes: scaled[:, lanes], 2 * cut)
+                at_point(l, "gathered")
+
+            ag(0, before)
+            fetch(0, *late)
+            turn(low.at[0])
+            ready(0, "c")
+            gradient(0, DOWN, lambda lanes: cst[:, lanes], ff)
+            x_send(0, DOWN)
+            at_point(l, "down")
 
         ready(l, "down", "g", "u", "inv1")
         dots[0, n] = jnp.zeros_like(dots[0, n])
@@ -967,30 +1286,28 @@
         lax.fori_loop(0, ff // TILE, hidden, 0)
         fetch(l, "qkv")
         ready(l, "xmid", "gate", "up", "res1")
-        turn(xmid)
-        gradient(l, GATE, lambda lanes: cst[:, lanes], 0, ff)
+
+        def gate_part():
+            turn(xmid)
+            gradient(l, GATE, lambda lanes: cst[:, lanes], ff)
+            at_point(l, "mid_reduce")
+
         reduce_narrow(
             0,
             2 * l + 1,
             lambda b, r: dot_last(cst[r], w_gate[rows_of(b, width)])
             + dot_last(dus[r], w_up[rows_of(b, width)]),
+            gate_part,
         )
         fetch(l, "out")
-        gradient(l, UP, lambda lanes: dus[:, lanes], 0, ff)
-
-        @pl.when(l == 0)
-        def _():
-            x_fold(1, OUT)
-            z_finish(1, GATE)
-
-        @pl.when(l == 1)
-        def _():
-            x_fold(1, DOWN)
-
-        ag(1)
+        at_point(l, "mid_done")
+
+        def up_part():
+            gradient(l, UP, lambda lanes: dus[:, lanes], ff)
+            at_point(l, "mix_gather")
+
+        ag(1, up_part)
         ready(l, "mix", "q", "kv", "out", "inv0")
-        turn(low.at[1])
-        gradient(l, OUT, lambda lanes: mix[:, lanes], 0, cut)
 
         def back_mix(r):
             do = 0.0
@@ -999,25 +1316,12 @@
             dopad[r] = dot(do.astype(BF), select[...]).astype(BF)
 
         each_tile(rows, TILE, back_mix)
-
-        @pl.when(l == 0)
-        def _():
-            z_finish(1, UP)
-            x_fold(1, QKV)
-
+        at_point(l, "mix_back")
         attention_back()
+        at_point(l, "attended")
         for d in range(1, group):
             k_copy(l, d).start()
-
-        @pl.when(l == 1)
-        def _():
-            x_fold(1, GATE)
-
-        @pl.when(l == 0)
-        def _():
-            z_finish(1, OUT)
-            x_fold(0, DOWN)
-
+        at_point(l, "kv_sent")
         split = kv * 128
 
         def own_rows(r):
@@ -1050,7 +1354,7 @@
             dq = dqpad[r]
             dots[1, n, :, r] = row_sums(dq * qpad[r].astype(F32)) + row_sums(dk * kvpad[at].astype(F32))
             inverse = rinv[0, r]
-            c, s = cosine[r, :cut], sine[r, :cut]
+            c, s = cosine[r], sine[r]
             lane = lax.broadcasted_iota(jnp.int32, c.shape, 1)
             for half, value in ((0, dq), (1, dk)):
                 high = value.astype(BF)
@@ -1065,20 +1369,22 @@
         for d in range(1, group):
             k_copy(l, d).wait_send()
         ready(l, "xmix", "qkv", "res0")
-        turn(xmix)
-        gradient(l, QKV, lambda lanes: scaled[:, lanes], 0, 2 * cut)
+
+        at_point(l, "kv_done")
+
+        def out_part():
+            turn(low.at[1])
+            gradient(l, OUT, lambda lanes: mix[:, lanes], cut)
+            at_point(l, "mix_reduce")
+
         reduce_narrow(
-            1, 2 * l, lambda b, r: dot_last(scaled[r], w_down[rows_of(b, width), : 2 * cut])
+            1, 2 * l, lambda b, r: dot_last(scaled[r], w_down[rows_of(b, width), : 2 * cut]), out_part
         )
-
-        @pl.when(l == 1)
-        def _():
-            z_finish(1, DOWN)
-
         return carry
 
     lax.fori_loop(0, 2, layer, 0)
-    collect(dcur, o_dx, txsend, txrecv, 0)
+    each_tile(rows, 128, lambda r: stage.__setitem__((0, r), dcur[r].astype(BF)))
+    collect(stage.at[0], o_dx, txsend, txrecv, 0)
 
     def gain_copy(d, incoming):
         ref = gall.at[flip(me, d) if incoming else me]
@@ -1087,43 +1393,42 @@
     gall[me] = gsum[...]
     for d in range(1, count):
         gain_copy(d, False).start()
-    z_finish(1, QKV)
-    x_fold(0, GATE)
-    z_finish(0, DOWN)
-    x_fold(0, UP)
-    z_finish(0, GATE)
-    x_fold(0, OUT)
-    x_fold(0, QKV)
-    z_finish(0, UP)
-    z_finish(0, OUT)
+    turn(xmix)
+    gradient(0, QKV, lambda lanes: scaled[:, lanes], 2 * cut)
+    for action, m, c in TAIL:
+        actions[action](m, c)
     for d in range(1, count):
         gain_copy(d, True).wait_recv()
     o_gain[...] = jnp.sum(gall[...], axis=0)
-    collect(i_resid.at[4], o_y, ysend, yrec, 1)
-    collect(dcur, o_dx, txsend, txrecv, 1)
-    collect(i_resid.at[4], o_y, ysend, yrec, 2)
-    collect(dcur, o_dx, txsend, txrecv, 2)
+    collect(i_y, o_y, ysend, yrec, 1)
+    collect(stage.at[0], o_dx, txsend, txrecv, 1)
+    collect(i_y, o_y, ysend, yrec, 2)
+    collect(stage.at[0], o_dx, txsend, txrecv, 2)
     for d in range(1, count):
         gain_copy(d, False).wait_send()
 
-    z_finish(0, QKV)
-
-    def drain(l, carry):
+    for l in (1, 0):
         for c in range(PIECES):
             for bit in falling:
-                for j in upper(bit):
+                for j in upper(l, c, bit):
                     x_copy(l, c, bit, j).wait_send()
-            for o in range(1, OUTER):
-                z_copy(l, c, o).wait_send()
-        return carry
-
-    lax.fori_loop(0, 2, drain, 0)
-
-
-def backward_pass(gains, cosine, sine, select, weights, saved, heads, kv):
+            for low_part in lows(l, c):
+                z_copy(l, c, 1, low_part).wait_send()
+                z_copy(l, c, 2, low_part).wait_send()
+
+                @pl.when(middle)
+                def _():
+                    z_copy(l, c, 3, low_part).wait_send()
+
+                @pl.when(jnp.logical_not(middle))
+                def _():
+                    z_far(l, c, low_part).wait_send()
+
+
+def backward_pass(gains, select, weights, saved, heads, kv):
     count = lax.axis_size("wide")
-    xall, resid, rinv, q, kvp, mix, g, u, c, dy = saved
-    batches, s_dev, width = dy.shape
+    c, low = saved[8], saved[9]
+    batches, s_dev, width = low.shape[1:]
     rows, group = batches * s_dev, count // batches
     length = rows * group
     kr = weights[0].shape[1] // count
@@ -1134,11 +1439,11 @@
     full = kr * count
     outs = (
         [sd((2, kr, s), F32) for s in sizes]
-        + [sd((batches, s_dev, width), F32)] * 2
+        + [sd((batches, s_dev, width), BF)] * 2
         + [sd((8, width), F32)]
         + [sd((2, full, s), BF) for s in sizes]
         + [sd((2, OUTER * (inner - 1), kr, s), BF) for s in sizes]
-        + [sd((2, OUTER - 1, kr, s), BF) for s in sizes]
+        + [sd((2, OUTER * (inner if i == QKV else 1), kr, s), BF) for i, s in enumerate(sizes)]
         + [sd((2, max(group - 1, 1), rows, kv * 256), BF)]
     )
     half = max(1, inner // 2) * OUTER * kr
@@ -1146,6 +1451,7 @@
         vm((full, ff), BF), vm((full, ff), BF), vm((full, ff), BF),
         vm((4, rows, width), BF), vm((4, rows, width), BF),
         vm((2, rows, width), F32), vm((2, rows, 1), F32),
+        vm((rows, heads * HEAD_DIM), F32), vm((rows, heads * HEAD_DIM), F32),
         vm((rows, ff), F32), vm((rows, ff), F32), vm((rows, ff), BF), vm((rows, ff), BF),
         vm((2, 4, rows, width), BF), vm((4 * width, rows), BF),
         vm((rows, heads * 128), BF), vm((length, kv * 256), BF), vm((rows, heads * HEAD_DIM), BF),
@@ -1159,8 +1465,8 @@
         dma((17,)), dma((2, 4)), dma((2, 4)), dma((2, 3)), dma((2, 3)), dma((2, 4)), dma((2, 4)),
         dma((2, group)), dma((2, group)),
         dma((2 * PIECES, OUTER * (inner - 1))), dma((2 * PIECES, OUTER * (inner - 1))),
-        dma((2 * PIECES, OUTER)), dma((2 * PIECES, OUTER)),
-        dma((2, count)), dma((batches,)), dma((batches,)), dma((batches,)), dma((batches,)),
+        dma((2 * PIECES, OUTER * inner)), dma((2 * PIECES, OUTER * inner)),
+        dma((2, max(2 * count, 4 * batches))), dma((batches,)), dma((batches,)), dma((batches,)), dma((batches,)),
         dma((count,)), dma((count,)),
     ]
     hbm = pl.BlockSpec(memory_space=pl.ANY)
@@ -1168,31 +1474,25 @@
     return pl.pallas_call(
         functools.partial(backward_kernel, count),
         out_shape=outs,
-        in_specs=[vmem] * 4 + [hbm] * (PIECES + len(saved)),
+        input_output_aliases={1 + PIECES + len(saved): PIECES + 3 + DOWN},
+        in_specs=[vmem] * 2 + [hbm] * (PIECES + len(saved)),
         out_specs=[hbm] * (PIECES + 2) + [vmem] + [hbm] * (3 * PIECES + 1),
         scratch_shapes=scratch,
         compiler_params=pltpu.CompilerParams(
             collective_id=1, has_side_effects=True, vmem_limit_bytes=60 * 1024 * 1024
         ),
         name="backward",
-    )(gains, cosine, sine, select, *weights, *saved)
+    )(gains, select, *weights, *saved)
 
 
 def per_device(tokens, cotangent, *weights):
     layers = [weights[:9], weights[9:]]
     batches, s_dev, width = tokens.shape
-    group = lax.axis_size("wide") // batches
-    rows = batches * s_dev
     halfway = HEAD_DIM // 2
     heads = layers[0][1].shape[1] // HEAD_DIM
     kv = layers[0][2].shape[1] // HEAD_DIM
     frequency = jnp.power(F32(THETA), -(jnp.arange(halfway, dtype=F32) * 2.0 / HEAD_DIM))
-    pos = (lax.axis_index("wide") % group) * rows + jnp.arange(rows, dtype=jnp.int32)
-    angle = pos.astype(F32)[:, None] * frequency[None, :]
-    cos, sin = jnp.cos(angle), jnp.sin(angle)
-    cut = kv * HEAD_DIM
-    cosine = jnp.concatenate([cos] * (2 * (heads + kv)) + [jnp.ones((rows, cut), F32)], axis=1)
-    sine = jnp.concatenate([-sin, sin] * (heads + kv) + [jnp.zeros((rows, cut), F32)], axis=1)
+    frequency = jnp.tile(frequency, 2 * heads)[None, :]
     place = jnp.arange(heads * HEAD_DIM)
     select = (
         (place // HEAD_DIM * 128 + place % HEAD_DIM)[:, None] == jnp.arange(heads * 128)[None, :]
@@ -1206,13 +1506,13 @@
         jnp.stack([w[7] for w in layers]),
         jnp.stack([w[8].T for w in layers]),
     ]
-    outs = forward_pass(tokens, cotangent, gains_in, cosine, sine, select, packs, heads, kv)
+    outs = forward_pass(tokens, cotangent, gains_in, frequency, select, packs, heads, kv)
     whole = outs[:PIECES]
-    o_xall, o_resid, o_rinv, o_q, o_kv, o_mix, o_lse, o_g, o_u, o_c, o_dy = outs[PIECES:]
-    saved = (o_xall, o_resid, o_rinv, o_q, o_kv, o_mix, o_g, o_u, o_c, o_dy)
-    back = backward_pass(gains_in, cosine, sine, select, whole, saved, heads, kv)
+    o_xall, o_resid, o_rinv, o_q, o_kv, o_mix, o_g, o_u, o_c, o_low, o_cos, o_sin, o_y, o_down = outs[PIECES:]
+    saved = (o_xall, o_resid, o_rinv, o_q, o_kv, o_mix, o_g, o_u, o_c, o_low, o_cos, o_sin, o_y, o_down)
+    back = backward_pass(gains_in, select, whole, saved, heads, kv)
     g_qkv, g_out, g_gate, g_up, g_down, output, input_back, dgain = back[:8]
-    results = [output, input_back]
+    results = [output.astype(F32), input_back.astype(F32)]
     for i, w in enumerate(layers):
         cut_q = w[1].shape[1]
         cut_k = cut_q + w[2].shape[1]

time: 930 us -> 731 us (0.79)
  Pallas kernels: 891 us -> 703 us
  local copies, waits for them, and re-layouts: 25.7 us -> 14.4 us
    pallas_call x1, Pallas kernels: 499 us -> 335 us  [backward_pass(): pl.pallas_call(functools.partial(backward_kernel, count), out_shape=outs,...]
    pallas_call x1, Pallas kernels: 392 us -> 368 us  [forward_pass(): pl.pallas_call(functools.partial(forward_kernel, count), out_shape=outs,...]
where the time goes in v4:
time: 731 us; the launch traced here: 729 us
  Pallas kernels  703 us (96%)
  local copies, waits for them, and re-layouts  14.4 us (2%)
  other arithmetic  11 us (2%)
    pallas_call x1, Pallas kernels, forward_pass(): pl.pallas_call(functools.partial(forward_kernel, count), out_shape=outs,...  368 us
    pallas_call x1, Pallas kernels, backward_pass(): pl.pallas_call(functools.partial(backward_kernel, count), out_shape=outs,...  335 us

profile of v4, /device:TPU:0, one launch (start us, length us, event | category | flops | bytes accessed | tf_op | source)
XLA Modules:
  0.0 729.1 jit_solution(7817843979694072381)
XLA Ops:
  0.7 0.8 stack.57
  1.6 0.7 stack.58
  2.3 0.7 stack.59
  2.9 0.7 stack.60
  3.6 0.6 broadcast_in_dim_tile.3.frequency
  4.9 1.7 pad_maximum_fusion.4.p_out
  6.6 0.9 fusion.select
  7.5 1.3 maximum_bitcast_fusion
  8.8 0.9 pad_maximum_fusion.3.p_qkv
  9.7 0.9 pad_maximum_fusion.2.p_down
  10.7 1.3 pad_maximum_fusion
  11.9 368.1 %forward.1 = (bf16[2,1536,768]{2,1,0:T(8,128)(2,1)}, bf16[2,1536,384]{2,1,0:T(8,128)(2,1)}, bf16[2,1536,1024]{2,1,0:T(8,128)(2,1)}, bf16[2,1536,1024]{2,1,0:T(8,...) custom-call(bf16[4,128,384]{2,1,0:T(8,128)(2,1)} %tokens.1, ...), custom_call_target="tpu_custom_call" | custom-call | tf_op jit(solution)/shard_map/forward/pallas_call | solution.py:695
  380.1 334.8 %backward.1 = (f32[2,192,768]{2,1,0:T(8,128)}, f32[2,192,384]{2,1,0:T(8,128)}, f32[2,192,1024]{2,1,0:T(8,128)}, f32[2,192,1024]{2,1,0:T(8,128)}, f32[2,192,1024]...) custom-call(f32[8,384]{1,0:T(8,128)} %concatenate.9.gains, ...), custom_call_target="tpu_custom_call", output_to_operand_aliasing={{12}: (20, {})} | custom-call | tf_op jit(solution)/shard_map/backward/pallas_call | solution.py:1474
  714.8 1.5 slice_reduce_fusion
  716.3 1.9 convert_element_type.12
  718.2 1.9 slice_bitcast_fusion.8
  720.1 2.0 convert_element_type.13
  722.3 0.7 slice.87
  723.0 0.8 fusion.10
  723.8 0.7 slice.84
  724.5 0.8 fusion.11
  725.3 1.2 slice_bitcast_fusion.2
  726.6 1.2 slice_bitcast_fusion.1
  727.8 1.2 slice_bitcast_fusion
  (26 shorter events, 0.8 us)
Async XLA Ops:
  0.7 9.0 %copy-start.8 = (bf16[1024,192]{0,1:T(8,128)(2,1)S(1)}, bf16[1024,192]{0,1:T(8,128)(2,1)}, u32[]{:S(2)}) copy-start(bf16[1024,192]{0,1:T(8,128)(2,1)} %param.39) | copy-start | bytes 1179652
  0.7 10.0 %copy-start.6 = (bf16[192,1024]{1,0:T(8,128)(2,1)S(1)}, bf16[192,1024]{1,0:T(8,128)(2,1)}, u32[]{:S(2)}) copy-start(bf16[192,1024]{1,0:T(8,128)(2,1)} %param.38) | copy-start | bytes 1179652
  0.7 10.0 %copy-start.4 = (bf16[192,1024]{1,0:T(8,128)(2,1)S(1)}, bf16[192,1024]{1,0:T(8,128)(2,1)}, u32[]{:S(2)}) copy-start(bf16[192,1024]{1,0:T(8,128)(2,1)} %param.37) | copy-start | bytes 1179652
  0.7 9.0 %copy-start.9 = (bf16[1024,192]{0,1:T(8,128)(2,1)S(1)}, bf16[1024,192]{0,1:T(8,128)(2,1)}, u32[]{:S(2)}) copy-start(bf16[1024,192]{0,1:T(8,128)(2,1)} %param.30) | copy-start | bytes 1179652
  0.7 10.0 %copy-start.7 = (bf16[192,1024]{1,0:T(8,128)(2,1)S(1)}, bf16[192,1024]{1,0:T(8,128)(2,1)}, u32[]{:S(2)}) copy-start(bf16[192,1024]{1,0:T(8,128)(2,1)} %param.29) | copy-start | bytes 1179652
  0.7 9.9 %copy-start.5 = (bf16[192,1024]{1,0:T(8,128)(2,1)S(1)}, bf16[192,1024]{1,0:T(8,128)(2,1)}, u32[]{:S(2)}) copy-start(bf16[192,1024]{1,0:T(8,128)(2,1)} %param.28) | copy-start | bytes 1179652
  714.8 7.4 %copy-start.3 = (f32[2,192,768]{2,1,0:T(8,128)S(1)}, f32[2,192,768]{2,1,0:T(8,128)}, u32[]{:S(2)}) copy-start(f32[2,192,768]{2,1,0:T(8,128)} %get-tuple-element.69) | copy-start | bytes 3538948
  720.1 5.2 copy-start.2
  722.3 4.3 copy-start.1
  725.3 2.5 copy-start

commit v5 on v4

--- a/solution.py
+++ b/solution.py
@@ -37,8 +37,6 @@
 QKV, OUT, GATE, UP, DOWN = range(5)
 PIECES = 5
 TILE = 256
-AHEAD = 2
-NEAR_AHEAD = 3
 
 
 def flip(index, distance):
@@ -105,6 +103,49 @@
     return pltpu.make_async_remote_copy(
         src_ref=src, dst_ref=dst, send_sem=send, recv_sem=recv, device_id=target, device_id_type=MESH
     )
+
+
+NEAR, FAR, RELAY_NEAR, RELAY, RELAY_LAST, COTANGENT = range(6)
+AT_START = [(NEAR, 0, UP), (NEAR, 1, UP), (NEAR, 0, QKV), (NEAR, 1, QKV), (NEAR, 1, OUT), (FAR, 0, OUT), (FAR, 0, QKV), (RELAY, 0, OUT)]
+AT_TOKENS = [(NEAR, 1, DOWN), (RELAY_NEAR, 0, QKV), (NEAR, 0, GATE), (FAR, 0, GATE), (NEAR, 0, DOWN)]
+AT = {
+    "gather": (
+        [(NEAR, 0, OUT), (NEAR, 1, GATE)],
+        [(FAR, 1, GATE), (RELAY, 1, OUT)],
+    ),
+    "gathered": (
+        [(RELAY, 0, QKV), (RELAY_LAST, 0, QKV), (FAR, 0, DOWN), (FAR, 0, UP)],
+        [],
+    ),
+    "kv_sent": (
+        [(RELAY_LAST, 0, OUT), (RELAY, 0, GATE), (COTANGENT, 0, QKV)],
+        [(RELAY_LAST, 1, OUT), (RELAY, 1, GATE)],
+    ),
+    "attended": (
+        [(RELAY, 0, DOWN), (RELAY_LAST, 0, GATE), (RELAY, 0, UP)],
+        [(FAR, 1, DOWN)],
+    ),
+    "mix_reduce": (
+        [(FAR, 1, QKV)],
+        [(RELAY_LAST, 1, UP)],
+    ),
+    "mid_gather": (
+        [(RELAY_LAST, 0, UP), (RELAY_LAST, 0, DOWN), (FAR, 1, UP)],
+        [(RELAY_LAST, 1, GATE), (RELAY, 1, DOWN)],
+    ),
+    "mid_gathered": (
+        [(RELAY, 1, QKV)],
+        [(RELAY_LAST, 1, DOWN)],
+    ),
+    "hidden": (
+        [(FAR, 1, OUT)],
+        [],
+    ),
+    "down_reduce": (
+        [(RELAY_LAST, 1, QKV), (RELAY, 1, UP)],
+        [],
+    ),
+}
 
 
 def forward_kernel(
@@ -198,8 +239,8 @@
         )
 
     def far_sends(l, c, low, action):
+        action(piece_copy(l, c, low, 2 * inner))
         action(piece_copy(l, c, low, inner))
-        action(piece_copy(l, c, low, 2 * inner))
 
         @pl.when(middle)
         def _():
@@ -220,8 +261,11 @@
     def wait_send(copy):
         copy.wait_send()
 
+    def near_first(l, c):
+        return l == 0 and c == QKV
+
     def all_sends(l, c, action):
-        if c == QKV:
+        if near_first(l, c):
             for low in range(inner):
                 near_sends(l, c, low, action)
                 far_sends(l, c, low, action)
@@ -232,58 +276,67 @@
             for j in range(count):
                 near_sends(l, c, j, action)
 
+    def send_near(l, c):
+        near_sends(l, c, 0, start)
+
     def send_far(l, c):
-        if c == QKV:
-            near_sends(l, c, 0, start)
         far_sends(l, c, 0, start)
         piece_own(l, c).start()
 
-    def send_near(l, c):
-        if c != QKV:
-            near_sends(l, c, 0, start)
-
-    def at_piece(l, c, action):
-        if c < PIECES:
-            action(l, c)
-        elif not isinstance(l, int):
-
-            @pl.when(l == 0)
-            def _():
-                action(1, c - PIECES)
-
-        elif l == 0:
-            action(1, c - PIECES)
-
-    def relay_near(l):
+    def relay_near(l, c):
         for low in wide.near:
-            piece_in(l, QKV, low).wait_recv()
-            near_sends(l, QKV, low, start)
-            far_sends(l, QKV, low, start)
+            piece_in(l, c, low).wait_recv()
+            near_sends(l, c, low, start)
+            far_sends(l, c, low, start)
 
     def relay(l, c):
-        for outer in (1, 2, 3):
-            for low in range(inner) if c == QKV else (0,):
+        for outer in (2, 1):
+            for low in range(inner) if near_first(l, c) else (0,):
                 piece_in(l, c, outer * inner + low).wait_recv()
                 if outer == 2:
                     pass_on(l, c, low, start)
-                if c != QKV:
+                if not near_first(l, c):
                     near_sends(l, c, outer * inner, start)
-        at_piece(l, c + AHEAD, send_far)
-        at_piece(l, c + NEAR_AHEAD, send_near)
+
+    def relay_last(l, c):
+        for low in range(inner) if near_first(l, c) else (0,):
+            piece_in(l, c, 3 * inner + low).wait_recv()
+            if not near_first(l, c):
+                near_sends(l, c, 3 * inner, start)
+
+    def send_cotangent(l, c):
+        spread(cotangent, o_low.at[n], dsend, drecv, True)
+
+    actions = (send_near, send_far, relay_near, relay, relay_last, send_cotangent)
+
+    def do(todo):
+        for action, l, c in todo:
+            actions[action](l, c)
+
+    def at_point(l, name):
+        for own_layer, todo in enumerate(AT[name]):
+            if todo:
+
+                @pl.when(l == own_layer)
+                def _():
+                    do(todo)
 
     def arrive(l, c):
-        if c != QKV:
+        def rest():
             for j in wide.rest:
                 piece_in(l, c, j).wait_recv()
                 near_sends(l, c, j, start)
+
+        if c == QKV:
+            pl.when(l == 1)(rest)
+        else:
+            rest()
         piece_own(l, c).wait()
         fetch = pltpu.make_async_copy(alls[c].at[l], bufs[c], load.at[c])
         fetch.start()
         fetch.wait()
 
-    send_far(0, QKV)
-    for c in range(1, NEAR_AHEAD):
-        send_near(0, c)
+    do(AT_START)
 
     def tables(r):
         lane = lax.broadcasted_iota(jnp.int32, (128, cosine.shape[1]), 1)
@@ -300,15 +353,12 @@
     ]
     for c in saved_tables:
         c.start()
-    relay_near(0)
-    for c in range(1, AHEAD):
-        send_far(0, c)
-    spread(cotangent, o_low.at[n], dsend, drecv, True)
     spread_wait(tokens, tok, tsend, trecv)
     for b in range(batches):
         resid[0, b * s_dev : (b + 1) * s_dev] = tok[b].astype(F32)
     for d in (1, 2, 3):
         gain_in(d).wait_recv()
+    do(AT_TOKENS)
 
     def ag_own(a, dist):
         return remote(
@@ -494,17 +544,15 @@
     def layer(l, carry):
         first, second = 2 * l, 2 * l + 1
         ag_start(first)
+        at_point(l, "gather")
         ag_finish(first)
-
-        @pl.when(l == 0)
-        def _():
-            relay(0, QKV)
 
         @pl.when(l == 1)
         def _():
             low_copy(other, 2, 2).wait_recv()
             low_copy(other, 1, 3).start()
 
+        at_point(l, "gathered")
         arrive(l, QKV)
 
         def project(r):
@@ -525,17 +573,21 @@
         each_tile(rows, TILE, project)
         for d in range(1, group):
             kv_copy(l, d).start()
-        relay(l, OUT)
+        at_point(l, "kv_sent")
         for d in range(1, group):
             kv_in(l, d).wait_recv()
         attention(l)
+        at_point(l, "attended")
         arrive(l, OUT)
         reduce_narrow(
-            first, lambda b, r: dot_last(mix[l, r], w_out[rows_of(b, width)]), lambda: relay(l, GATE)
+            first,
+            lambda b, r: dot_last(mix[l, r], w_out[rows_of(b, width)]),
+            lambda: at_point(l, "mix_reduce"),
         )
         ag_start(second)
+        at_point(l, "mid_gather")
         ag_finish(second)
-        relay(l, UP)
+        at_point(l, "mid_gathered")
         arrive(l, GATE)
         arrive(l, UP)
 
@@ -569,11 +621,7 @@
             low_copy(n, 2, 2).start()
             low_copy(n, 1, 1).start()
 
-        @pl.when(l == 0)
-        def _():
-            relay_near(1)
-
-        relay(l, DOWN)
+        at_point(l, "hidden")
 
         @pl.when(l == 1)
         def _():
@@ -581,12 +629,11 @@
 
         arrive(l, DOWN)
 
-        def ahead():
-            @pl.when(l == 0)
-            def _():
-                relay(1, QKV)
-
-        reduce_narrow(second, lambda b, r: dot_last(cst[r], w_down[rows_of(b, width)]), ahead)
+        reduce_narrow(
+            second,
+            lambda b, r: dot_last(cst[r], w_down[rows_of(b, width)]),
+            lambda: at_point(l, "down_reduce"),
+        )
         return carry
 
     lax.fori_loop(0, 2, layer, 0)
@@ -608,7 +655,7 @@
     for d in (1, 2, 3):
         gain_copy(d).wait_send()
 
-    def drain(l, carry):
+    for l in (0, 1):
         for c in range(PIECES):
             all_sends(l, c, wait_send)
         for d in range(1, group):
@@ -617,9 +664,6 @@
             ag_own(a, 1).wait_send()
             ag_own(a, 2).wait_send()
             ag_forward(a).wait_send()
-        return carry
-
-    lax.fori_loop(0, 2, drain, 0)
 
 
 def forward_pass(tokens, cotangent, gains, frequency, select, packs, heads, kv):

time: 731 us -> 677 us (0.926)
  Pallas kernels: 703 us -> 649 us
    pallas_call x1, Pallas kernels: 368 us -> 312 us  [forward_pass(): pl.pallas_call(functools.partial(forward_kernel, count), out_shape=outs,...]
where the time goes in v5:
time: 677 us; the launch traced here: 675 us
  Pallas kernels  649 us (96%)
  local copies, waits for them, and re-layouts  14.4 us (2%)
  other arithmetic  11 us (2%)
    pallas_call x1, Pallas kernels, backward_pass(): pl.pallas_call(functools.partial(backward_kernel, count), out_shape=outs,...  336 us
    pallas_call x1, Pallas kernels, forward_pass(): pl.pallas_call(functools.partial(forward_kernel, count), out_shape=outs,...  312 us

profile of v5, /device:TPU:0, one launch (start us, length us, event | category | flops | bytes accessed | tf_op | source)
XLA Modules:
  0.0 674.8 jit_solution(14215560297199590173)
XLA Ops:
  0.7 0.8 stack.57
  1.6 0.7 stack.58
  2.3 0.7 stack.59
  2.9 0.7 stack.60
  3.6 0.6 broadcast_in_dim_tile.3.frequency
  4.9 1.7 pad_maximum_fusion.4.p_out
  6.6 0.9 fusion.select
  7.5 1.3 maximum_bitcast_fusion
  8.8 0.9 pad_maximum_fusion.3.p_qkv
  9.7 0.9 pad_maximum_fusion.2.p_down
  10.7 1.3 pad_maximum_fusion
  11.9 312.4 %forward.1 = (bf16[2,1536,768]{2,1,0:T(8,128)(2,1)}, bf16[2,1536,384]{2,1,0:T(8,128)(2,1)}, bf16[2,1536,1024]{2,1,0:T(8,128)(2,1)}, bf16[2,1536,1024]{2,1,0:T(8,...) custom-call(bf16[4,128,384]{2,1,0:T(8,128)(2,1)} %tokens.1, ...), custom_call_target="tpu_custom_call" | custom-call | tf_op jit(solution)/shard_map/forward/pallas_call | solution.py:739
  324.3 336.2 %backward.1 = (f32[2,192,768]{2,1,0:T(8,128)}, f32[2,192,384]{2,1,0:T(8,128)}, f32[2,192,1024]{2,1,0:T(8,128)}, f32[2,192,1024]{2,1,0:T(8,128)}, f32[2,192,1024]...) custom-call(f32[8,384]{1,0:T(8,128)} %concatenate.9.gains, ...), custom_call_target="tpu_custom_call", output_to_operand_aliasing={{12}: (20, {})} | custom-call | tf_op jit(solution)/shard_map/backward/pallas_call | solution.py:1518
  660.6 1.5 slice_reduce_fusion
  662.0 1.9 convert_element_type.12
  664.0 1.9 slice_bitcast_fusion.8
  665.9 2.0 convert_element_type.13
  668.0 0.7 slice.87
  668.7 0.8 fusion.10
  669.5 0.7 slice.84
  670.3 0.8 fusion.11
  671.1 1.2 slice_bitcast_fusion.2
  672.3 1.2 slice_bitcast_fusion.1
  673.5 1.2 slice_bitcast_fusion
  (26 shorter events, 0.8 us)
Async XLA Ops:
  0.7 9.0 %copy-start.8 = (bf16[1024,192]{0,1:T(8,128)(2,1)S(1)}, bf16[1024,192]{0,1:T(8,128)(2,1)}, u32[]{:S(2)}) copy-start(bf16[1024,192]{0,1:T(8,128)(2,1)} %param.39) | copy-start | bytes 1179652
  0.7 10.0 %copy-start.6 = (bf16[192,1024]{1,0:T(8,128)(2,1)S(1)}, bf16[192,1024]{1,0:T(8,128)(2,1)}, u32[]{:S(2)}) copy-start(bf16[192,1024]{1,0:T(8,128)(2,1)} %param.38) | copy-start | bytes 1179652
  0.7 10.0 %copy-start.4 = (bf16[192,1024]{1,0:T(8,128)(2,1)S(1)}, bf16[192,1024]{1,0:T(8,128)(2,1)}, u32[]{:S(2)}) copy-start(bf16[192,1024]{1,0:T(8,128)(2,1)} %param.37) | copy-start | bytes 1179652
  0.7 9.0 %copy-start.9 = (bf16[1024,192]{0,1:T(8,128)(2,1)S(1)}, bf16[1024,192]{0,1:T(8,128)(2,1)}, u32[]{:S(2)}) copy-start(bf16[1024,192]{0,1:T(8,128)(2,1)} %param.30) | copy-start | bytes 1179652
  0.7 10.0 %copy-start.7 = (bf16[192,1024]{1,0:T(8,128)(2,1)S(1)}, bf16[192,1024]{1,0:T(8,128)(2,1)}, u32[]{:S(2)}) copy-start(bf16[192,1024]{1,0:T(8,128)(2,1)} %param.29) | copy-start | bytes 1179652
  0.7 9.9 %copy-start.5 = (bf16[192,1024]{1,0:T(8,128)(2,1)S(1)}, bf16[192,1024]{1,0:T(8,128)(2,1)}, u32[]{:S(2)}) copy-start(bf16[192,1024]{1,0:T(8,128)(2,1)} %param.28) | copy-start | bytes 1179652
  660.5 7.4 %copy-start.3 = (f32[2,192,768]{2,1,0:T(8,128)S(1)}, f32[2,192,768]{2,1,0:T(8,128)}, u32[]{:S(2)}) copy-start(f32[2,192,768]{2,1,0:T(8,128)} %get-tuple-element.69) | copy-start | bytes 3538948
  665.9 5.2 copy-start.2
  668.0 4.3 copy-start.1
  671.1 2.5 copy-start

commit v6 on v5

--- a/solution.py
+++ b/solution.py
@@ -2,6 +2,7 @@
 
 import jax
 import jax.numpy as jnp
+import numpy as np
 from jax import lax
 from jax.experimental import pallas as pl
 from jax.experimental.pallas import tpu as pltpu
@@ -153,7 +154,7 @@
     tokens, cotangent, gains, frequency, select,
     p_qkv, p_out, p_gate, p_up, p_down,
     a_qkv, a_out, a_gate, a_up, a_down,
-    o_xall, o_resid, o_rinv, o_q, o_kv, o_mix, o_g, o_u, o_c, o_low, o_cos, o_sin, o_y, o_down,
+    o_xall, o_resid, o_rinv, o_q, o_kv, o_mix, o_g, o_u, o_c, o_low, o_cos, o_sin, o_down,
     w_qkv, w_out, w_gate, w_up, w_down,
     tok, gall, xall, resid, rinv, qpad, kvall, kvpad, mixpad, mix, cosine, sine, gst, ust, cst,
     own, stage, crecv, yrecv,
@@ -321,7 +322,7 @@
                 def _():
                     do(todo)
 
-    def arrive(l, c):
+    def arrive(l, c, used=True):
         def rest():
             for j in wide.rest:
                 piece_in(l, c, j).wait_recv()
@@ -332,9 +333,13 @@
         else:
             rest()
         piece_own(l, c).wait()
-        fetch = pltpu.make_async_copy(alls[c].at[l], bufs[c], load.at[c])
-        fetch.start()
-        fetch.wait()
+
+        def get():
+            fetch = pltpu.make_async_copy(alls[c].at[l], bufs[c], load.at[c])
+            fetch.start()
+            fetch.wait()
+
+        get() if used is True else pl.when(used)(get)
 
     do(AT_START)
 
@@ -627,24 +632,24 @@
         def _():
             down_gradient()
 
-        arrive(l, DOWN)
-
-        reduce_narrow(
-            second,
-            lambda b, r: dot_last(cst[r], w_down[rows_of(b, width)]),
-            lambda: at_point(l, "down_reduce"),
-        )
+        arrive(l, DOWN, l == 0)
+
+
+        @pl.when(l == 0)
+        def _():
+            reduce_narrow(
+                1,
+                lambda b, r: dot_last(cst[r], w_down[rows_of(b, width)]),
+                lambda: at_point(l, "down_reduce"),
+            )
+
         return carry
 
     lax.fori_loop(0, 2, layer, 0)
-    each_tile(rows, 128, lambda r: stage.__setitem__((0, r), resid[4, r].astype(BF)))
-    last = saved(stage.at[0], o_y, 12)
-    last.start()
     for c in layer_saves(0)[:9]:
         c().wait()
     for c in layer_saves(1):
         c().wait()
-    last.wait()
     for c in saved_tables:
         c.wait()
     low_copy(n, 2, 2).wait_send()
@@ -688,7 +693,6 @@
         sd((4, batches, s_dev, width), BF),
         sd((rows, heads * HEAD_DIM), F32),
         sd((rows, heads * HEAD_DIM), F32),
-        sd((rows, width), BF),
         sd(whole[DOWN].shape, BF),
     ]
     dma = pltpu.SemaphoreType.DMA
@@ -797,11 +801,11 @@
     count,
     gains, select,
     a_qkv, a_out, a_gate, a_up, a_down,
-    i_xall, i_resid, i_rinv, i_q, i_kv, i_mix, i_g, i_u, i_c, i_low, i_cos, i_sin, i_y, i_down,
+    i_xall, i_resid, i_rinv, i_q, i_kv, i_mix, i_g, i_u, i_c, i_low, i_cos, i_sin, i_down,
     g_qkv, g_out, g_gate, g_up, g_down, o_y, o_dx, o_gain,
     d_qkv, d_out, d_gate, d_up, d_down,
     x_qkv, x_out, x_gate, x_up, x_down,
-    z_qkv, z_out, z_gate, z_up, z_down, o_kin,
+    z_qkv, z_out, z_gate, z_up, z_down, o_kin, o_ysrc,
     w_gate, w_up, w_down, xmid, xmix, resid, rinv, cosine, sine, gst, ust, cst, dus, low, turned, qpad, kvpad, mix,
     dcur, own, stage, crecv, yrecv, dopad, dqpad, dkv, ksend_buf, scaled, piece, have, got, final,
     dots, gsum, gall,
@@ -935,33 +939,56 @@
     def rs_other(k):
         return remote(stage.at[2], yrecv.at[k], rsend.at[k, 2], rrecv.at[k, 2], (me, other))
 
+    def reduce_start(k, product):
+        for j, b in ((1, cross), (0, core)):
+
+            def body(r, j=j, b=b):
+                stage[j, r] = product(b, r).astype(BF)
+
+            each_tile(rows, TILE, body)
+            rs_core(k, j).start()
+
+        def body_other(r):
+            own[r] = product(other, r)
+
+        each_tile(rows, TILE, body_other)
+        rs_core(k, 1).wait_recv()
+
+        def add_other(r):
+            stage[2, r] = (own[r] + crecv[k, 1, r].astype(F32)).astype(BF)
+
+        each_tile(rows, 128, add_other)
+        rs_other(k).start()
+
+        def body_own(r):
+            own[r] = product(n, r)
+
+        each_tile(rows, TILE, body_own)
+
+    def reduce_sent(k):
+        rs_core(k, 1).wait_send()
+        rs_core(k, 0).wait_send()
+        rs_other(k).wait_send()
+
+    def output_finish():
+        rs_core(2, 0).wait_recv()
+        rs_other(2).wait_recv()
+        reduce_sent(2)
+
+        def add_own(r):
+            total = resid[1, r] + own[r] + crecv[2, 0, r].astype(F32) + yrecv[2, r].astype(F32)
+            stage[0, r] = total.astype(BF)
+
+        each_tile(rows, 128, add_own)
+        put = pltpu.make_async_copy(stage.at[0], o_ysrc, local.at[1, 0])
+        put.start()
+        put.wait()
+        collect(o_ysrc, o_y, ysend, yrec, 0)
+
     def reduce_narrow(k, a, product, filler):
         for d in (1, 2, 3):
             dots_copy(k, d, False).start()
-        for j, b in ((1, cross), (0, core)):
-
-            def body(r, j=j, b=b):
-                stage[j, r] = product(b, r).astype(BF)
-
-            each_tile(rows, TILE, body)
-            rs_core(k, j).start()
-
-        def body_other(r):
-            own[r] = product(other, r)
-
-        each_tile(rows, TILE, body_other)
-        rs_core(k, 1).wait_recv()
-
-        def add_other(r):
-            stage[2, r] = (own[r] + crecv[k, 1, r].astype(F32)).astype(BF)
-
-        each_tile(rows, 128, add_other)
-        rs_other(k).start()
-
-        def body_own(r):
-            own[r] = product(n, r)
-
-        each_tile(rows, TILE, body_own)
+        reduce_start(k, product)
         filler()
         rs_core(k, 0).wait_recv()
         for d in (1, 2, 3):
@@ -980,9 +1007,7 @@
             gsum[pl.ds(a, 1), :] += jnp.sum(total * x, axis=0, keepdims=True)
 
         each_tile(rows, 128, add_own)
-        rs_core(k, 1).wait_send()
-        rs_core(k, 0).wait_send()
-        rs_other(k).wait_send()
+        reduce_sent(k)
         for d in (1, 2, 3):
             dots_copy(k, d, False).wait_send()
 
@@ -1069,17 +1094,19 @@
     def held(buffer, i, columns, size=1):
         return buffer.at[pl.ds(i * kr, size * kr), pl.ds(0, columns)]
 
-    def add_held(count_of, columns, wide_out):
+    def add_held(i, columns, wide_out):
         tile = 64 if kr % 64 == 0 else 16
 
-        def body(r):
+        def body(k, carry):
+            r = pl.ds(pl.multiple_of(i * kr + k * tile, 16), tile)
             total = have[r, :columns].astype(F32) + got[r, :columns].astype(F32)
             if wide_out:
                 final[r, :columns] = total
             else:
                 have[r, :columns] = total.astype(BF)
-
-        each_tile(count_of * kr, tile, body)
+            return carry
+
+        lax.fori_loop(0, kr // tile, body, 0)
 
     def z_merge(l, c):
         columns = grads[c].shape[2]
@@ -1091,7 +1118,7 @@
                 mine_at = held(have, 0, columns)
                 far = block(l, c, 2 * inner + low)
                 moved([(far, mine_at), (zins[c].at[l, low * OUTER + 3], held(got, 0, columns))])
-                add_held(1, columns, False)
+                add_held(0, columns, False)
                 moved([(mine_at, far)])
                 z_copy(l, c, 2, low).start()
 
@@ -1112,12 +1139,29 @@
             for i, j in enumerate(blocks):
                 pairs.append((block(l, c, j), held(have, i, columns)))
                 pairs.append((xins[c].at[l, fold_slot(l, c, bit, j)], held(got, i, columns)))
-            moved(pairs)
-            add_held(len(blocks), columns, last)
+            copies = [
+                functools.partial(pltpu.make_async_copy, src, dst, local.at[0, k])
+                for k, (src, dst) in enumerate(pairs)
+            ]
+            for copy in copies:
+                copy().start()
+            backs = [
+                functools.partial(
+                    pltpu.make_async_copy, held(have, i, columns), block(l, c, j), local.at[1, i]
+                )
+                for i, j in enumerate(blocks)
+            ]
+            for i, j in enumerate(blocks):
+                copies[2 * i]().wait()
+                copies[2 * i + 1]().wait()
+                add_held(i, columns, last)
+                if not last:
+                    backs[i]().start()
             if last:
                 put_result(l, c)
                 return
-            moved([(held(have, i, columns), block(l, c, j)) for i, j in enumerate(blocks)])
+            for back in backs:
+                back().wait()
             if at + 1 < len(falling):
                 for j in upper(l, c, falling[at + 1]):
                     x_copy(l, c, falling[at + 1], j).start()
@@ -1129,6 +1173,15 @@
             base = low * OUTER
             z_in(l, c, base).wait_recv()
             z_in(l, c, base + 1).wait_recv()
+            third = functools.partial(
+                pltpu.make_async_copy, zins[c].at[l, base + 2], held(got, 2, columns), local.at[0, 3]
+            )
+
+            @pl.when(middle)
+            def _():
+                z_in(l, c, base + 2).wait_recv()
+                third().start()
+
             moved(
                 [
                     (block(l, c, low), held(have, 0, columns)),
@@ -1139,8 +1192,7 @@
 
             @pl.when(middle)
             def _():
-                z_in(l, c, base + 2).wait_recv()
-                moved([(zins[c].at[l, base + 2], held(got, 2, columns))])
+                third().wait()
 
             @pl.when(jnp.logical_not(middle))
             def _():
@@ -1215,7 +1267,7 @@
             pltpu.make_async_copy(
                 i_low.at[s, b], low.at[0, s, pl.ds(b * s_dev, s_dev)], local.at[0, s * batches + b]
             ).start()
-    fetch(1, "down", "g", "u", "inv1", "gate", "up", "xmid", "res1")
+    fetch(1, "c", "down", "res1", "g", "u", "inv1", "gate", "up", "xmid")
     fetch(1, *late)
     fetch_tables = [
         pltpu.make_async_copy(i_cos, cosine, local.at[1, 1]),
@@ -1223,7 +1275,6 @@
     ]
     for c in fetch_tables:
         c.start()
-    collect(i_y, o_y, ysend, yrec, 0)
     for s in range(4):
         for b in range(batches):
             pltpu.make_async_copy(
@@ -1305,7 +1356,14 @@
             x_send(0, DOWN)
             at_point(l, "down")
 
-        ready(l, "down", "g", "u", "inv1")
+        ready(l, "down")
+
+        @pl.when(l == 1)
+        def _():
+            ready(1, "c")
+            reduce_start(2, lambda b, r: dot_last(cst[r], w_down[rows_of(b, width)]))
+
+        ready(l, "g", "u", "inv1")
         dots[0, n] = jnp.zeros_like(dots[0, n])
 
         def hidden(j, carry):
@@ -1330,6 +1388,7 @@
         lax.fori_loop(0, ff // TILE, hidden, 0)
         fetch(l, "qkv")
         ready(l, "xmid", "gate", "up", "res1")
+        pl.when(l == 1)(output_finish)
 
         def gate_part():
             turn(xmid)
@@ -1444,9 +1503,9 @@
     for d in range(1, count):
         gain_copy(d, True).wait_recv()
     o_gain[...] = jnp.sum(gall[...], axis=0)
-    collect(i_y, o_y, ysend, yrec, 1)
+    collect(o_ysrc, o_y, ysend, yrec, 1)
     collect(stage.at[0], o_dx, txsend, txrecv, 1)
-    collect(i_y, o_y, ysend, yrec, 2)
+    collect(o_ysrc, o_y, ysend, yrec, 2)
     collect(stage.at[0], o_dx, txsend, txrecv, 2)
     for d in range(1, count):
         gain_copy(d, False).wait_send()
@@ -1488,7 +1547,7 @@
         + [sd((2, full, s), BF) for s in sizes]
         + [sd((2, OUTER * (inner - 1), kr, s), BF) for s in sizes]
         + [sd((2, OUTER * (inner if i == QKV else 1), kr, s), BF) for i, s in enumerate(sizes)]
-        + [sd((2, max(group - 1, 1), rows, kv * 256), BF)]
+        + [sd((2, max(group - 1, 1), rows, kv * 256), BF), sd((rows, width), BF)]
     )
     half = max(1, inner // 2) * OUTER * kr
     scratch = [
@@ -1500,13 +1559,13 @@
         vm((2, 4, rows, width), BF), vm((4 * width, rows), BF),
         vm((rows, heads * 128), BF), vm((length, kv * 256), BF), vm((rows, heads * HEAD_DIM), BF),
         vm((rows, width), F32), vm((rows, width), F32), vm((3, rows, width), BF),
-        vm((2, 2, rows, width), BF), vm((2, rows, width), BF),
+        vm((3, 2, rows, width), BF), vm((3, rows, width), BF),
         vm((rows, heads * 128), BF), vm((rows, heads * 128), F32), vm((length, 256), F32),
         vm((length, kv * 256), BF),
         vm((rows, 2 * heads * HEAD_DIM), BF),
         vm((full, ff), BF), vm((half, ff), BF), vm((max(half, (OUTER - 1) * kr), ff), BF), vm((kr, ff), F32),
         vm((2, 4, 8, rows), F32), vm((8, width), F32), vm((count, 8, width), F32),
-        dma((17,)), dma((2, 4)), dma((2, 4)), dma((2, 3)), dma((2, 3)), dma((2, 4)), dma((2, 4)),
+        dma((17,)), dma((2, 4)), dma((2, 4)), dma((3, 3)), dma((3, 3)), dma((2, 4)), dma((2, 4)),
         dma((2, group)), dma((2, group)),
         dma((2 * PIECES, OUTER * (inner - 1))), dma((2 * PIECES, OUTER * (inner - 1))),
         dma((2 * PIECES, OUTER * inner)), dma((2 * PIECES, OUTER * inner)),
@@ -1520,7 +1579,7 @@
         out_shape=outs,
         input_output_aliases={1 + PIECES + len(saved): PIECES + 3 + DOWN},
         in_specs=[vmem] * 2 + [hbm] * (PIECES + len(saved)),
-        out_specs=[hbm] * (PIECES + 2) + [vmem] + [hbm] * (3 * PIECES + 1),
+        out_specs=[hbm] * (PIECES + 2) + [vmem] + [hbm] * (3 * PIECES + 2),
         scratch_shapes=scratch,
         compiler_params=pltpu.CompilerParams(
             collective_id=1, has_side_effects=True, vmem_limit_bytes=60 * 1024 * 1024
@@ -1535,12 +1594,11 @@
     halfway = HEAD_DIM // 2
     heads = layers[0][1].shape[1] // HEAD_DIM
     kv = layers[0][2].shape[1] // HEAD_DIM
-    frequency = jnp.power(F32(THETA), -(jnp.arange(halfway, dtype=F32) * 2.0 / HEAD_DIM))
-    frequency = jnp.tile(frequency, 2 * heads)[None, :]
-    place = jnp.arange(heads * HEAD_DIM)
-    select = (
-        (place // HEAD_DIM * 128 + place % HEAD_DIM)[:, None] == jnp.arange(heads * 128)[None, :]
-    ).astype(BF)
+    exponent = np.arange(halfway, dtype=np.float32) * np.float32(2.0 / HEAD_DIM)
+    frequency = np.tile(np.power(np.float32(THETA), -exponent), 2 * heads)[None, :]
+    place = np.arange(heads * HEAD_DIM)
+    target = place // HEAD_DIM * 128 + place % HEAD_DIM
+    select = (target[:, None] == np.arange(heads * 128)[None, :]).astype(jnp.bfloat16)
     gains = jnp.stack([layers[0][0], layers[0][5], layers[1][0], layers[1][5]])
     gains_in = jnp.concatenate([gains, jnp.ones_like(gains)], axis=0)
     packs = [
@@ -1552,8 +1610,8 @@
     ]
     outs = forward_pass(tokens, cotangent, gains_in, frequency, select, packs, heads, kv)
     whole = outs[:PIECES]
-    o_xall, o_resid, o_rinv, o_q, o_kv, o_mix, o_g, o_u, o_c, o_low, o_cos, o_sin, o_y, o_down = outs[PIECES:]
-    saved = (o_xall, o_resid, o_rinv, o_q, o_kv, o_mix, o_g, o_u, o_c, o_low, o_cos, o_sin, o_y, o_down)
+    o_xall, o_resid, o_rinv, o_q, o_kv, o_mix, o_g, o_u, o_c, o_low, o_cos, o_sin, o_down = outs[PIECES:]
+    saved = (o_xall, o_resid, o_rinv, o_q, o_kv, o_mix, o_g, o_u, o_c, o_low, o_cos, o_sin, o_down)
     back = backward_pass(gains_in, select, whole, saved, heads, kv)
     g_qkv, g_out, g_gate, g_up, g_down, output, input_back, dgain = back[:8]
     results = [output.astype(F32), input_back.astype(F32)]

time: 677 us -> 658 us (0.972)
  Pallas kernels: 649 us -> 632 us
    pallas_call x1, Pallas kernels: 312 us -> 297 us  [forward_pass(): pl.pallas_call(functools.partial(forward_kernel, count), out_shape=outs,...]
where the time goes in v6:
time: 658 us; the launch traced here: 657 us
  Pallas kernels  632 us (96%)
  local copies, waits for them, and re-layouts  13.8 us (2%)
  other arithmetic  10.1 us (2%)
    pallas_call x1, Pallas kernels, backward_pass(): pl.pallas_call(functools.partial(backward_kernel, count), out_shape=outs,...  335 us
    pallas_call x1, Pallas kernels, forward_pass(): pl.pallas_call(functools.partial(forward_kernel, count), out_shape=outs,...  297 us

profile of v6, /device:TPU:0, one launch (start us, length us, event | category | flops | bytes accessed | tf_op | source)
XLA Modules:
  0.0 656.7 jit_solution(9773238891207217142)
XLA Ops:
  0.7 0.8 stack.57
  1.6 0.7 stack.58
  2.2 0.7 stack.59
  2.9 0.7 stack.60
  3.6 0.6 concatenate.9.gains
  4.2 1.7 pad_maximum_fusion.4.p_out
  6.0 1.3 maximum_bitcast_fusion
  7.3 0.9 pad_maximum_fusion.3.p_qkv
  8.1 0.9 pad_maximum_fusion.2.p_down
  9.1 1.3 pad_maximum_fusion
  10.4 296.9 %forward.1 = (bf16[2,1536,768]{2,1,0:T(8,128)(2,1)}, bf16[2,1536,384]{2,1,0:T(8,128)(2,1)}, bf16[2,1536,1024]{2,1,0:T(8,128)(2,1)}, bf16[2,1536,1024]{2,1,0:T(8,...) custom-call(bf16[4,128,384]{2,1,0:T(8,128)(2,1)} %tokens.1, ...), custom_call_target="tpu_custom_call" | custom-call | tf_op jit(solution)/shard_map/forward/pallas_call | solution.py:743
  307.3 335.2 %backward.1 = (f32[2,192,768]{2,1,0:T(8,128)}, f32[2,192,384]{2,1,0:T(8,128)}, f32[2,192,1024]{2,1,0:T(8,128)}, f32[2,192,1024]{2,1,0:T(8,128)}, f32[2,192,1024]...) custom-call(f32[8,384]{1,0:T(8,128)} %concatenate.9.gains, ...), custom_call_target="tpu_custom_call", output_to_operand_aliasing={{12}: (19, {})} | custom-call | tf_op jit(solution)/shard_map/backward/pallas_call | solution.py:1577
  642.4 1.5 slice_reduce_fusion
  643.9 1.9 convert_element_type.6
  645.8 1.9 slice_bitcast_fusion.8
  647.7 2.0 convert_element_type.7
  649.8 0.1 slice_bitcast_fusion.6
  649.9 0.7 slice.87
  650.6 0.8 fusion
  651.4 0.7 slice.84
  652.1 0.8 fusion.1
  652.9 1.2 slice_bitcast_fusion.2
  654.2 1.2 slice_bitcast_fusion.1
  655.4 1.2 slice_bitcast_fusion
  (21 shorter events, 0.0 us)
Async XLA Ops:
  0.7 7.5 %copy-start.8 = (bf16[1024,192]{0,1:T(8,128)(2,1)S(1)}, bf16[1024,192]{0,1:T(8,128)(2,1)}, u32[]{:S(2)}) copy-start(bf16[1024,192]{0,1:T(8,128)(2,1)} %param.41) | copy-start | bytes 1179652
  0.7 8.4 %copy-start.6 = (bf16[192,1024]{1,0:T(8,128)(2,1)S(1)}, bf16[192,1024]{1,0:T(8,128)(2,1)}, u32[]{:S(2)}) copy-start(bf16[192,1024]{1,0:T(8,128)(2,1)} %param.40) | copy-start | bytes 1179652
  0.7 8.4 %copy-start.4 = (bf16[192,1024]{1,0:T(8,128)(2,1)S(1)}, bf16[192,1024]{1,0:T(8,128)(2,1)}, u32[]{:S(2)}) copy-start(bf16[192,1024]{1,0:T(8,128)(2,1)} %param.39) | copy-start | bytes 1179652
  0.7 7.4 %copy-start.9 = (bf16[1024,192]{0,1:T(8,128)(2,1)S(1)}, bf16[1024,192]{0,1:T(8,128)(2,1)}, u32[]{:S(2)}) copy-start(bf16[1024,192]{0,1:T(8,128)(2,1)} %param.32) | copy-start | bytes 1179652
  0.7 8.4 %copy-start.7 = (bf16[192,1024]{1,0:T(8,128)(2,1)S(1)}, bf16[192,1024]{1,0:T(8,128)(2,1)}, u32[]{:S(2)}) copy-start(bf16[192,1024]{1,0:T(8,128)(2,1)} %param.31) | copy-start | bytes 1179652
  0.7 8.4 %copy-start.5 = (bf16[192,1024]{1,0:T(8,128)(2,1)S(1)}, bf16[192,1024]{1,0:T(8,128)(2,1)}, u32[]{:S(2)}) copy-start(bf16[192,1024]{1,0:T(8,128)(2,1)} %param.30) | copy-start | bytes 1179652
  642.4 7.4 %copy-start.3 = (f32[2,192,768]{2,1,0:T(8,128)S(1)}, f32[2,192,768]{2,1,0:T(8,128)}, u32[]{:S(2)}) copy-start(f32[2,192,768]{2,1,0:T(8,128)} %get-tuple-element.67) | copy-start | bytes 3538948
  647.7 5.2 copy-start.2
  649.9 4.3 copy-start.1
  652.9 2.5 copy-start

commit v7 on v6

--- a/solution.py
+++ b/solution.py
@@ -66,6 +66,11 @@
         return [b for b in self.bits if low == 0 or b > top_bit(low)]
 
 
+def paired(index, inner):
+    low, high = index % 2, (index // inner) % 2
+    return index - low + high - high * inner + low * inner
+
+
 def is_middle(me, inner):
     return ((me // inner + 1) // 2) % 2 == 1
 
@@ -107,43 +112,44 @@
 
 
 NEAR, FAR, RELAY_NEAR, RELAY, RELAY_LAST, COTANGENT = range(6)
-AT_START = [(NEAR, 0, UP), (NEAR, 1, UP), (NEAR, 0, QKV), (NEAR, 1, QKV), (NEAR, 1, OUT), (FAR, 0, OUT), (FAR, 0, QKV), (RELAY, 0, OUT)]
-AT_TOKENS = [(NEAR, 1, DOWN), (RELAY_NEAR, 0, QKV), (NEAR, 0, GATE), (FAR, 0, GATE), (NEAR, 0, DOWN)]
+NEAR_FIRST = ((0, QKV),)
+AT_START = [(FAR, 0, OUT), (NEAR, 0, OUT), (NEAR, 0, QKV), (NEAR, 1, UP), (FAR, 0, QKV), (RELAY, 0, OUT), (RELAY_NEAR, 0, QKV)]
+AT_TOKENS = [(NEAR, 0, UP), (NEAR, 0, DOWN), (NEAR, 1, QKV)]
 AT = {
     "gather": (
-        [(NEAR, 0, OUT), (NEAR, 1, GATE)],
-        [(FAR, 1, GATE), (RELAY, 1, OUT)],
+        [(FAR, 0, GATE), (NEAR, 1, DOWN), (RELAY, 0, QKV)],
+        [(RELAY_LAST, 1, OUT), (RELAY, 1, UP)],
     ),
     "gathered": (
-        [(RELAY, 0, QKV), (RELAY_LAST, 0, QKV), (FAR, 0, DOWN), (FAR, 0, UP)],
+        [(FAR, 0, DOWN), (NEAR, 1, GATE), (NEAR, 1, OUT), (NEAR, 0, GATE), (RELAY_LAST, 0, QKV)],
         [],
     ),
     "kv_sent": (
-        [(RELAY_LAST, 0, OUT), (RELAY, 0, GATE), (COTANGENT, 0, QKV)],
-        [(RELAY_LAST, 1, OUT), (RELAY, 1, GATE)],
+        [(RELAY, 0, GATE), (RELAY_LAST, 0, OUT), (FAR, 0, UP), (RELAY, 0, DOWN)],
+        [(RELAY_LAST, 1, UP), (RELAY, 1, GATE), (FAR, 1, DOWN)],
     ),
     "attended": (
-        [(RELAY, 0, DOWN), (RELAY_LAST, 0, GATE), (RELAY, 0, UP)],
-        [(FAR, 1, DOWN)],
+        [(RELAY_LAST, 0, GATE), (FAR, 1, OUT)],
+        [],
     ),
     "mix_reduce": (
-        [(FAR, 1, QKV)],
-        [(RELAY_LAST, 1, UP)],
+        [(RELAY, 0, UP), (COTANGENT, 0, QKV)],
+        [(RELAY_LAST, 1, GATE)],
     ),
     "mid_gather": (
-        [(RELAY_LAST, 0, UP), (RELAY_LAST, 0, DOWN), (FAR, 1, UP)],
-        [(RELAY_LAST, 1, GATE), (RELAY, 1, DOWN)],
+        [(FAR, 1, QKV)],
+        [(RELAY, 1, DOWN)],
     ),
     "mid_gathered": (
-        [(RELAY, 1, QKV)],
+        [(FAR, 1, UP), (RELAY_LAST, 0, UP), (RELAY_LAST, 0, DOWN), (RELAY, 1, OUT)],
         [(RELAY_LAST, 1, DOWN)],
     ),
     "hidden": (
-        [(FAR, 1, OUT)],
+        [(RELAY, 1, QKV)],
         [],
     ),
     "down_reduce": (
-        [(RELAY_LAST, 1, QKV), (RELAY, 1, UP)],
+        [(RELAY_LAST, 1, QKV), (FAR, 1, GATE)],
         [],
     ),
 }
@@ -177,10 +183,12 @@
     enter(count, me, n)
 
     rank, place = me % batches, me // batches
+    inner = wide.inner
+    mine = paired(me, inner) % group
 
     def spread(source, target, send, recv, start):
         for b in range(batches):
-            to = b * group + place
+            to = paired(b * group + place, inner)
 
             @pl.when(to != me)
             def _():
@@ -195,7 +203,7 @@
 
     def spread_wait(source, target, send, recv):
         for r in range(batches):
-            origin = (me % group) * batches + r
+            origin = mine * batches + r
 
             @pl.when(origin != me)
             def _():
@@ -216,7 +224,6 @@
     for d in (1, 2, 3):
         gain_copy(d).start()
 
-    inner = wide.inner
     middle = is_middle(me, inner)
 
     def piece_copy(l, c, i, dist, slot=None):
@@ -263,7 +270,7 @@
         copy.wait_send()
 
     def near_first(l, c):
-        return l == 0 and c == QKV
+        return (l, c) in NEAR_FIRST
 
     def all_sends(l, c, action):
         if near_first(l, c):
@@ -328,9 +335,10 @@
                 piece_in(l, c, j).wait_recv()
                 near_sends(l, c, j, start)
 
-        if c == QKV:
-            pl.when(l == 1)(rest)
-        else:
+        far_first = [m for m in (0, 1) if not near_first(m, c)]
+        if len(far_first) == 1:
+            pl.when(l == far_first[0])(rest)
+        elif far_first:
             rest()
         piece_own(l, c).wait()
 
@@ -345,7 +353,7 @@
 
     def tables(r):
         lane = lax.broadcasted_iota(jnp.int32, (128, cosine.shape[1]), 1)
-        pos = (me % group) * rows + r.start + lax.broadcasted_iota(jnp.int32, lane.shape, 0)
+        pos = mine * rows + r.start + lax.broadcasted_iota(jnp.int32, lane.shape, 0)
         angle = pos.astype(F32) * frequency[...]
         cosine[r] = jnp.cos(angle)
         turn = jnp.sin(angle)
@@ -454,15 +462,14 @@
         rs_core(a, 0).wait_send()
         rs_other(a).wait_send()
 
-    mine = me % group
 
     def kv_copy(l, d):
         part = kvall.at[l, rows_of(mine, rows)]
-        return remote(part, part, ksend.at[l, d], krecv.at[l, d], (flip(me, d), n))
+        return remote(part, part, ksend.at[l, d], krecv.at[l, d], (flip(me, paired(d, inner)), n))
 
     def kv_in(l, d):
         part = kvall.at[l, rows_of(flip(mine, d), rows)]
-        return remote(part, part, ksend.at[l, d], krecv.at[l, d], (flip(me, d), n))
+        return remote(part, part, ksend.at[l, d], krecv.at[l, d], (flip(me, paired(d, inner)), n))
 
     tile_q = TILE if length <= 2048 else 128
 
@@ -758,43 +765,44 @@
 
 
 SEND, FOLD, MERGE, FINISH = range(4)
+OUTER_FIRST = ((1, OUT),)
 POINTS = {
-    "gathered": ([], [(SEND, 1, QKV), (FOLD, 1, UP)]),
+    "gathered": ([], [(SEND, 1, QKV), (MERGE, 1, OUT), (FOLD, 1, UP)]),
     "down": ([], []),
     "mid_reduce": (
         [(SEND, 1, GATE)],
-        [(MERGE, 1, QKV), (SEND, 0, GATE)],
+        [(FOLD, 1, QKV), (SEND, 0, GATE)],
     ),
     "mid_done": (
         [],
         [],
     ),
     "mix_gather": (
-        [(FOLD, 1, DOWN)],
-        [(FOLD, 0, DOWN)],
+        [(FOLD, 1, DOWN), (SEND, 1, UP)],
+        [(MERGE, 1, UP), (MERGE, 1, QKV)],
     ),
     "mix_back": (
         [],
-        [],
+        [(FOLD, 0, DOWN), (SEND, 0, UP)],
     ),
     "attended": (
         [],
-        [(FOLD, 1, OUT)],
+        [],
     ),
     "kv_sent": (
-        [(SEND, 1, UP), (MERGE, 1, DOWN), (FOLD, 1, GATE)],
-        [(MERGE, 1, UP), (FINISH, 1, GATE), (SEND, 0, UP), (FOLD, 0, GATE), (MERGE, 1, OUT)],
+        [(FOLD, 1, GATE)],
+        [(FINISH, 1, GATE), (MERGE, 0, DOWN), (FINISH, 1, UP)],
     ),
     "kv_done": (
         [],
-        [(MERGE, 0, DOWN)],
+        [(FOLD, 0, GATE)],
     ),
     "mix_reduce": (
-        [(MERGE, 1, GATE), (SEND, 1, OUT)],
-        [(SEND, 0, OUT), (FINISH, 1, OUT), (MERGE, 0, GATE)],
+        [(SEND, 1, OUT), (MERGE, 1, DOWN), (MERGE, 1, GATE)],
+        [(FINISH, 1, DOWN)],
     ),
 }
-TAIL = [(FOLD, 0, UP), (SEND, 0, QKV), (FINISH, 1, DOWN), (FINISH, 0, DOWN), (FOLD, 0, OUT), (MERGE, 0, UP), (FINISH, 1, QKV), (MERGE, 0, OUT), (FOLD, 0, QKV), (FINISH, 0, OUT), (FINISH, 1, UP), (FOLD, 1, QKV), (FINISH, 0, UP), (MERGE, 0, QKV), (FINISH, 0, GATE), (FINISH, 0, QKV)]
+TAIL = [(SEND, 0, QKV), (SEND, 0, OUT), (FINISH, 1, QKV), (MERGE, 0, GATE), (FOLD, 0, UP), (FOLD, 0, QKV), (FOLD, 0, OUT), (MERGE, 0, UP), (FINISH, 1, OUT), (MERGE, 0, QKV), (FINISH, 0, DOWN), (FOLD, 1, OUT), (FINISH, 0, GATE), (MERGE, 0, OUT), (FINISH, 0, UP), (FINISH, 0, QKV), (FINISH, 0, OUT)]
 
 
 def backward_kernel(
@@ -831,7 +839,8 @@
     cut = heads * HEAD_DIM
     kv_cut = kv * HEAD_DIM
     core, other, cross = flip(n, 1), flip(n, 2), flip(n, 3)
-    mine = me % group
+    mine = paired(me, inner) % group
+    batch = paired(me, inner) // group
     enter(count, me, n)
 
     def loads(l):
@@ -869,7 +878,7 @@
             @pl.when(to != me)
             def _():
                 if phase == 0:
-                    remote(part, target.at[me // group], send.at[r], recv.at[me // group], (to, n)).start()
+                    remote(part, target.at[batch], send.at[r], recv.at[batch], (to, n)).start()
                 elif phase == 2:
                     remote(part, target.at[0], send.at[r], recv.at[0], (to, n)).wait_send()
 
@@ -877,11 +886,11 @@
 
                 @pl.when(to == me)
                 def _():
-                    pltpu.make_async_copy(part, target.at[me // group], recv.at[me // group]).start()
+                    pltpu.make_async_copy(part, target.at[batch], recv.at[batch]).start()
 
         if phase == 1:
             for b in range(batches):
-                origin = b * group + me // batches
+                origin = paired(b * group + me // batches, inner)
                 part = source.at[pl.ds(0, s_dev)]
 
                 @pl.when(origin != me)
@@ -1015,7 +1024,7 @@
     falling = list(reversed(wide.bits))
 
     def outer_first(l, c):
-        return l == 1 and c == QKV
+        return (l, c) in OUTER_FIRST
 
     def lows(l, c):
         return list(range(inner)) if outer_first(l, c) else [0]
@@ -1327,13 +1336,13 @@
     def k_copy(l, d):
         return remote(
             ksend_buf.at[rows_of(flip(mine, d), rows)], o_kin.at[l, d - 1],
-            ksend.at[l, d], krecv.at[l, d], (flip(me, d), n),
+            ksend.at[l, d], krecv.at[l, d], (flip(me, paired(d, inner)), n),
         )
 
     def k_in(l, d):
         return remote(
             o_kin.at[l, d - 1], o_kin.at[l, d - 1], ksend.at[l, d], krecv.at[l, d],
-            (flip(me, d), n),
+            (flip(me, paired(d, inner)), n),
         )
 
     def layer(step, carry):
@@ -1546,7 +1555,7 @@
         + [sd((8, width), F32)]
         + [sd((2, full, s), BF) for s in sizes]
         + [sd((2, OUTER * (inner - 1), kr, s), BF) for s in sizes]
-        + [sd((2, OUTER * (inner if i == QKV else 1), kr, s), BF) for i, s in enumerate(sizes)]
+        + [sd((2, OUTER * inner, kr, s), BF) for s in sizes]
         + [sd((2, max(group - 1, 1), rows, kv * 256), BF), sd((rows, width), BF)]
     )
     half = max(1, inner // 2) * OUTER * kr

time: 658 us -> 645 us (0.980)
  Pallas kernels: 632 us -> 619 us
    pallas_call x1, Pallas kernels: 297 us -> 288 us  [forward_pass(): pl.pallas_call(functools.partial(forward_kernel, count), out_shape=outs,...]
where the time goes in v7:
time: 645 us; the launch traced here: 643 us
  Pallas kernels  619 us (96%)
  local copies, waits for them, and re-layouts  13.8 us (2%)
  other arithmetic  10.1 us (2%)
    pallas_call x1, Pallas kernels, backward_pass(): pl.pallas_call(functools.partial(backward_kernel, count), out_shape=outs,...  331 us
    pallas_call x1, Pallas kernels, forward_pass(): pl.pallas_call(functools.partial(forward_kernel, count), out_shape=outs,...  288 us

profile of v7, /device:TPU:0, one launch (start us, length us, event | category | flops | bytes accessed | tf_op | source)
XLA Modules:
  0.0 643.5 jit_solution(15534933605203587114)
XLA Ops:
  0.7 0.8 stack.57
  1.6 0.7 stack.58
  2.2 0.7 stack.59
  2.9 0.7 stack.60
  3.6 0.6 concatenate.9.gains
  4.2 1.7 pad_maximum_fusion.4.p_out
  6.0 1.3 maximum_bitcast_fusion
  7.3 0.9 pad_maximum_fusion.3.p_qkv
  8.1 0.9 pad_maximum_fusion.2.p_down
  9.1 1.3 pad_maximum_fusion
  10.4 288.1 %forward.1 = (bf16[2,1536,768]{2,1,0:T(8,128)(2,1)}, bf16[2,1536,384]{2,1,0:T(8,128)(2,1)}, bf16[2,1536,1024]{2,1,0:T(8,128)(2,1)}, bf16[2,1536,1024]{2,1,0:T(8,...) custom-call(bf16[4,128,384]{2,1,0:T(8,128)(2,1)} %tokens.1, ...), custom_call_target="tpu_custom_call" | custom-call | tf_op jit(solution)/shard_map/forward/pallas_call | solution.py:750
  298.5 330.7 %backward.1 = (f32[2,192,768]{2,1,0:T(8,128)}, f32[2,192,384]{2,1,0:T(8,128)}, f32[2,192,1024]{2,1,0:T(8,128)}, f32[2,192,1024]{2,1,0:T(8,128)}, f32[2,192,1024]...) custom-call(f32[8,384]{1,0:T(8,128)} %concatenate.9.gains, ...), custom_call_target="tpu_custom_call", output_to_operand_aliasing={{12}: (19, {})} | custom-call | tf_op jit(solution)/shard_map/backward/pallas_call | solution.py:1586
  629.2 1.5 slice_reduce_fusion
  630.7 1.9 convert_element_type.6
  632.6 1.9 slice_bitcast_fusion.8
  634.5 2.0 convert_element_type.7
  636.6 0.1 slice_bitcast_fusion.6
  636.7 0.7 slice.87
  637.4 0.8 fusion
  638.2 0.7 slice.84
  638.9 0.8 fusion.1
  639.7 1.2 slice_bitcast_fusion.2
  641.0 1.2 slice_bitcast_fusion.1
  642.2 1.2 slice_bitcast_fusion
  (21 shorter events, 0.0 us)
Async XLA Ops:
  0.7 7.5 %copy-start.8 = (bf16[1024,192]{0,1:T(8,128)(2,1)S(1)}, bf16[1024,192]{0,1:T(8,128)(2,1)}, u32[]{:S(2)}) copy-start(bf16[1024,192]{0,1:T(8,128)(2,1)} %param.41) | copy-start | bytes 1179652
  0.7 8.4 %copy-start.6 = (bf16[192,1024]{1,0:T(8,128)(2,1)S(1)}, bf16[192,1024]{1,0:T(8,128)(2,1)}, u32[]{:S(2)}) copy-start(bf16[192,1024]{1,0:T(8,128)(2,1)} %param.40) | copy-start | bytes 1179652
  0.7 8.4 %copy-start.4 = (bf16[192,1024]{1,0:T(8,128)(2,1)S(1)}, bf16[192,1024]{1,0:T(8,128)(2,1)}, u32[]{:S(2)}) copy-start(bf16[192,1024]{1,0:T(8,128)(2,1)} %param.39) | copy-start | bytes 1179652
  0.7 7.4 %copy-start.9 = (bf16[1024,192]{0,1:T(8,128)(2,1)S(1)}, bf16[1024,192]{0,1:T(8,128)(2,1)}, u32[]{:S(2)}) copy-start(bf16[1024,192]{0,1:T(8,128)(2,1)} %param.32) | copy-start | bytes 1179652
  0.7 8.4 %copy-start.7 = (bf16[192,1024]{1,0:T(8,128)(2,1)S(1)}, bf16[192,1024]{1,0:T(8,128)(2,1)}, u32[]{:S(2)}) copy-start(bf16[192,1024]{1,0:T(8,128)(2,1)} %param.31) | copy-start | bytes 1179652
  0.7 8.4 %copy-start.5 = (bf16[192,1024]{1,0:T(8,128)(2,1)S(1)}, bf16[192,1024]{1,0:T(8,128)(2,1)}, u32[]{:S(2)}) copy-start(bf16[192,1024]{1,0:T(8,128)(2,1)} %param.30) | copy-start | bytes 1179652
  629.2 7.4 %copy-start.3 = (f32[2,192,768]{2,1,0:T(8,128)S(1)}, f32[2,192,768]{2,1,0:T(8,128)}, u32[]{:S(2)}) copy-start(f32[2,192,768]{2,1,0:T(8,128)} %get-tuple-element.67) | copy-start | bytes 3538948
  634.5 5.2 copy-start.2
  636.7 4.3 copy-start.1
  639.7 2.5 copy-start

commit v8 on v7

--- a/solution.py
+++ b/solution.py
@@ -158,7 +158,7 @@
 def forward_kernel(
     count,
     tokens, cotangent, gains, frequency, select,
-    p_qkv, p_out, p_gate, p_up, p_down,
+    p_qkv, q_qkv, p_out, q_out, p_gate, q_gate, p_up, q_up, p_down, q_down,
     a_qkv, a_out, a_gate, a_up, a_down,
     o_xall, o_resid, o_rinv, o_q, o_kv, o_mix, o_g, o_u, o_c, o_low, o_cos, o_sin, o_down,
     w_qkv, w_out, w_gate, w_up, w_down,
@@ -172,10 +172,10 @@
     batches, s_dev, width = tokens.shape
     rows = batches * s_dev
     group = count // batches
-    packs = (p_qkv, p_out, p_gate, p_up, p_down)
+    packs = ((p_qkv, q_qkv), (p_out, q_out), (p_gate, q_gate), (p_up, q_up), (p_down, q_down))
     alls = (a_qkv, a_out, a_gate, a_up, a_down)
     bufs = (w_qkv, w_out, w_gate, w_up, w_down)
-    kr = p_qkv.shape[1]
+    kr = p_qkv.shape[0]
     heads = qpad.shape[2] // 128
     kv = kvpad.shape[2] // 256
     length = kvpad.shape[1]
@@ -228,7 +228,7 @@
 
     def piece_copy(l, c, i, dist, slot=None):
         block = rows_of(flip(me, i), kr)
-        src = packs[c].at[l] if i == 0 else alls[c].at[l, block]
+        src = packs[c][l] if i == 0 else alls[c].at[l, block]
         t, j = l * PIECES + c, i ^ dist
         slot = j if slot is None else slot
         return remote(
@@ -243,7 +243,7 @@
 
     def piece_own(l, c):
         return pltpu.make_async_copy(
-            packs[c].at[l], alls[c].at[l, rows_of(me, kr)], bown.at[l * PIECES + c]
+            packs[c][l], alls[c].at[l, rows_of(me, kr)], bown.at[l * PIECES + c]
         )
 
     def far_sends(l, c, low, action):
@@ -340,7 +340,8 @@
             pl.when(l == far_first[0])(rest)
         elif far_first:
             rest()
-        piece_own(l, c).wait()
+        placed = alls[c].at[l, rows_of(me, kr)]
+        pltpu.make_async_copy(placed, placed, bown.at[l * PIECES + c]).wait()
 
         def get():
             fetch = pltpu.make_async_copy(alls[c].at[l], bufs[c], load.at[c])
@@ -683,10 +684,11 @@
     batches, s_dev, width = tokens.shape
     rows, group = batches * s_dev, count // batches
     length = rows * group
-    kr = packs[0].shape[1]
-    ff = packs[GATE].shape[2]
+    kr = packs[0][0].shape[0]
+    ff = packs[GATE][0].shape[1]
+    sizes = [p[0].shape[1] for p in packs]
     sd = jax.ShapeDtypeStruct
-    whole = [sd((2, kr * count, p.shape[2]), BF) for p in packs]
+    whole = [sd((2, kr * count, size), BF) for size in sizes]
     outs = whole + [
         sd((4, 4, rows, width), BF),
         sd((4, rows, width), F32),
@@ -703,7 +705,7 @@
         sd(whole[DOWN].shape, BF),
     ]
     dma = pltpu.SemaphoreType.DMA
-    scratch = [pltpu.VMEM((kr * count, p.shape[2]), BF) for p in packs] + [
+    scratch = [pltpu.VMEM((kr * count, size), BF) for size in sizes] + [
         pltpu.VMEM((batches, s_dev, width), BF),
         pltpu.VMEM((4, 8, width), F32),
         pltpu.VMEM((4, 4, rows, width), BF),
@@ -750,14 +752,14 @@
     return pl.pallas_call(
         functools.partial(forward_kernel, count),
         out_shape=outs,
-        in_specs=[hbm, hbm] + [vmem] * 3 + [hbm] * PIECES,
+        in_specs=[hbm, hbm] + [vmem] * 3 + [hbm] * (2 * PIECES),
         out_specs=[hbm] * len(outs),
         scratch_shapes=scratch,
         compiler_params=pltpu.CompilerParams(
             collective_id=0, has_side_effects=True, vmem_limit_bytes=60 * 1024 * 1024
         ),
         name="forward",
-    )(tokens, cotangent, gains, frequency, select, *packs)
+    )(tokens, cotangent, gains, frequency, select, *[p for pair in packs for p in pair])
 
 
 def dot_rows(left, right):
@@ -1608,14 +1610,14 @@
     place = np.arange(heads * HEAD_DIM)
     target = place // HEAD_DIM * 128 + place % HEAD_DIM
     select = (target[:, None] == np.arange(heads * 128)[None, :]).astype(jnp.bfloat16)
-    gains = jnp.stack([layers[0][0], layers[0][5], layers[1][0], layers[1][5]])
-    gains_in = jnp.concatenate([gains, jnp.ones_like(gains)], axis=0)
+    parts = [layers[0][0], layers[0][5], layers[1][0], layers[1][5], jnp.ones((4 * width,), F32)]
+    gains_in = jnp.concatenate(parts).reshape(8, width)
     packs = [
-        jnp.stack([jnp.concatenate([w[1], w[2], w[3]], axis=1) for w in layers]),
-        jnp.stack([w[4].T for w in layers]),
-        jnp.stack([w[6] for w in layers]),
-        jnp.stack([w[7] for w in layers]),
-        jnp.stack([w[8].T for w in layers]),
+        [jnp.concatenate([w[1], w[2], w[3]], axis=1) for w in layers],
+        [w[4].T for w in layers],
+        [w[6] for w in layers],
+        [w[7] for w in layers],
+        [w[8].T for w in layers],
     ]
     outs = forward_pass(tokens, cotangent, gains_in, frequency, select, packs, heads, kv)
     whole = outs[:PIECES]

time: 645 us -> 641 us (level)
  no operation moved by 1% of the time
where the time goes in v8:
time: 641 us; the launch traced here: 639 us
  Pallas kernels  619 us (97%)
  local copies, waits for them, and re-layouts  13.6 us (2%)
    pallas_call x1, Pallas kernels, backward_pass(): pl.pallas_call(functools.partial(backward_kernel, count), out_shape=outs,...  331 us
    pallas_call x1, Pallas kernels, forward_pass(): pl.pallas_call(functools.partial(forward_kernel, count), out_shape=outs,...  288 us

profile of v8, /device:TPU:0, one launch (start us, length us, event | category | flops | bytes accessed | tf_op | source)
XLA Modules:
  0.0 639.1 jit_solution(2637533653589499249)
XLA Ops:
  0.7 0.7 constant_dynamic-update-slice_fusion.4
  1.4 0.7 constant_dynamic-update-slice_fusion.3
  2.0 0.7 constant_dynamic-update-slice_fusion.2
  2.7 0.7 constant_dynamic-update-slice_fusion.1
  3.4 0.6 reshape.43.gains
  4.0 2.1 pad_maximum_fusion
  6.1 288.1 %forward.1 = (bf16[2,1536,768]{2,1,0:T(8,128)(2,1)}, bf16[2,1536,384]{2,1,0:T(8,128)(2,1)}, bf16[2,1536,1024]{2,1,0:T(8,128)(2,1)}, bf16[2,1536,1024]{2,1,0:T(8,...) custom-call(bf16[4,128,384]{2,1,0:T(8,128)(2,1)} %tokens.1, ...), custom_call_target="tpu_custom_call" | custom-call | tf_op jit(solution)/shard_map/forward/pallas_call | solution.py:752
  294.3 330.6 %backward.1 = (f32[2,192,768]{2,1,0:T(8,128)}, f32[2,192,384]{2,1,0:T(8,128)}, f32[2,192,1024]{2,1,0:T(8,128)}, f32[2,192,1024]{2,1,0:T(8,128)}, f32[2,192,1024]...) custom-call(f32[8,384]{1,0:T(8,128)} %reshape.43.gains, ...), custom_call_target="tpu_custom_call", output_to_operand_aliasing={{12}: (19, {})} | custom-call | tf_op jit(solution)/shard_map/backward/pallas_call | solution.py:1588
  624.9 0.0 copy-start.3
  624.9 1.5 slice_reduce_fusion
  626.3 1.9 convert_element_type.6
  628.3 1.9 slice_bitcast_fusion.8
  630.2 2.0 convert_element_type.7
  632.2 0.0 copy-done.3
  632.2 0.1 slice_bitcast_fusion.6
  632.3 0.0 copy-start.1
  632.3 0.7 slice.87
  633.1 0.8 fusion
  633.9 0.7 slice.84
  634.6 0.8 fusion.1
  635.4 0.0 copy-done.2
  635.4 1.2 slice_bitcast_fusion.2
  636.6 1.2 slice_bitcast_fusion.1
  637.9 1.2 slice_bitcast_fusion
  (6 shorter events, 0.0 us)
Async XLA Ops:
  624.9 7.4 %copy-start.3 = (f32[2,192,768]{2,1,0:T(8,128)S(1)}, f32[2,192,768]{2,1,0:T(8,128)}, u32[]{:S(2)}) copy-start(f32[2,192,768]{2,1,0:T(8,128)} %get-tuple-element.67) | copy-start | bytes 3538948
  630.2 5.2 copy-start.2
  632.3 4.3 copy-start.1
  635.4 2.5 copy-start
